TPU v7x, 256 devices: a whole 4x4x8 slice. The times are simulated.
256 devices in a mesh: sub: 4 (over x), row: 16 (over z, core), col: 4 (over y).
Axes of the slice: x: 4, y: 4, z: 8, core: 2. Of those that a mesh axis runs over, the one named last changes fastest.
Arguments:
- leaf_rhs: bfloat16 [4, 64, 4, 64, 256], P('sub', 'row', 'col'), may hold values from -6 to 6
- leaf_inverse: bfloat16 [4, 64, 4, 256, 256], P('sub', 'row', 'col'), may hold values from -0.5 to 0.5
- coupling: bfloat16 [4, 16, 64, 4, 256, 256], P('sub', 'row', None, 'col'), may hold values from -0.01171875 to 0.01171875
- pattern: int32 [4, 16, 64, 4], P('sub', 'row', None, 'col'), may hold values 0 or 1
- top_rhs: bfloat16 [16, 64, 256], replicated, may hold values from -6 to 6
- top_inverse: bfloat16 [16, 256, 256], replicated, may hold values from -0.5 to 0.5
- top_factor: bfloat16 [16, 16, 256, 256], P('row', 'col'), may hold values from -0.09375 to 0.09375
Outputs:
- leaf_solution: bfloat16 [4, 64, 4, 64, 256], P('sub', 'row', 'col')
- top_solution: bfloat16 [16, 64, 256], P('row')
All inputs are finite; a program needn't handle non-finite values. No bound on the sum of `pattern` on one device may be relied on, other than what follows from the above.
Results may differ from a plain program's by a relative error of at most 0.025.
Values may be sent and summed in bfloat16 or wider, within the bound.
No kernel may reach another device: no remote copies, remote signals or barrier semaphores. Data moves between devices by JAX's collectives and lax.ppermute only.
A program may use at most 128 MiB of HBM per device.

v0:
```python
import jax
import jax.numpy as jnp
from jax import lax
from jax.sharding import PartitionSpec as P


def spread(block, axis, source):
    block = jnp.where(lax.axis_index(axis) == source, block, jnp.zeros_like(block))
    return lax.psum(block, axis)


def local(leaf_rhs, leaf_inverse, coupling, pattern, top_rhs, top_inverse, top_factor):
    own_rhs = leaf_rhs[0, :, 0]
    own_inverse = jnp.tril(leaf_inverse[0, :, 0])
    coupled = coupling[0, :, :, 0]
    weights = pattern[0, :, :, 0].astype(jnp.bfloat16)
    blocks_row = coupled.shape[0]
    rhs_count = own_rhs.shape[1]
    block_size = own_rhs.shape[2]
    total_top = top_rhs.shape[0]
    leaf_forward = jnp.einsum(
        "inb,idb->ind", own_rhs, own_inverse, preferred_element_type=jnp.float32
    ).astype(jnp.bfloat16)
    block_slice = coupled
    weight_slice = weights
    scaled = (
        lax.all_gather(leaf_forward, "row", axis=0, tiled=True)[None]
        * weight_slice[:, :, None, None]
    )
    partial_value = jnp.einsum(
        "ainb,aieb->ane", scaled, block_slice, preferred_element_type=jnp.float32
    )
    updates = lax.psum(partial_value.astype(jnp.bfloat16), ("sub", "col")).astype(jnp.float32)
    row_start = lax.axis_index("row") * blocks_row
    full_row = lax.all_gather(top_factor, "col", axis=1, tiled=True)
    row_ids = row_start + jnp.arange(blocks_row)

    def forward_step(block_id, carried):
        pending, solved = carried
        local_row = jnp.clip(block_id - row_start, 0, blocks_row - 1)
        owner_row = block_id // blocks_row
        residue = (
            top_rhs[block_id].astype(jnp.float32) - updates[local_row] - pending[local_row]
        ).astype(jnp.bfloat16)
        solved_piece = jnp.dot(
            residue, jnp.tril(top_inverse[block_id]).T, preferred_element_type=jnp.float32
        ).astype(jnp.bfloat16)
        solved_piece = spread(solved_piece, "row", owner_row)
        column = lax.dynamic_index_in_dim(full_row, block_id, 1, keepdims=False)
        below = (row_ids > block_id).astype(jnp.float32)
        pending = pending + below[:, None, None] * jnp.einsum(
            "nb,aeb->ane", solved_piece, column, preferred_element_type=jnp.float32
        )
        solved = lax.dynamic_update_index_in_dim(solved, solved_piece, block_id, 0)
        return (pending, solved)

    start_state = (
        jnp.zeros((blocks_row, rhs_count, block_size), jnp.float32),
        jnp.zeros((total_top, rhs_count, block_size), jnp.bfloat16),
    )
    forward_all = lax.fori_loop(0, total_top, forward_step, start_state)[1]

    def backward_step(iteration, solved):
        block_id = total_top - 1 - iteration
        own_rows = lax.dynamic_slice_in_dim(solved, row_start, blocks_row, 0)
        above = (row_ids > block_id).astype(jnp.bfloat16)
        column = lax.dynamic_index_in_dim(full_row, block_id, 1, keepdims=False)
        term = jnp.einsum(
            "ane,aeb->nb",
            own_rows * above[:, None, None],
            column,
            preferred_element_type=jnp.float32,
        )
        summed = lax.psum(term.astype(jnp.bfloat16), "row").astype(jnp.float32)
        residue = (forward_all[block_id].astype(jnp.float32) - summed).astype(jnp.bfloat16)
        solved_piece = jnp.dot(
            residue, jnp.tril(top_inverse[block_id]), preferred_element_type=jnp.float32
        ).astype(jnp.bfloat16)
        return lax.dynamic_update_index_in_dim(solved, solved_piece, block_id, 0)

    solution = lax.fori_loop(
        0, total_top, backward_step, jnp.zeros((total_top, rhs_count, block_size), jnp.bfloat16)
    )
    own_top = lax.dynamic_slice_in_dim(solution, row_start, blocks_row, 0)
    block_slice = coupled
    weight_slice = weights
    scaled = own_top[:, None] * weight_slice[:, :, None, None]
    back_sums = lax.psum_scatter(
        jnp.einsum(
            "aine,aieb->inb", scaled, block_slice, preferred_element_type=jnp.float32
        ).astype(jnp.bfloat16),
        "row",
        scatter_dimension=0,
        tiled=True,
    ).astype(jnp.float32)
    leaf_residue = (leaf_forward.astype(jnp.float32) - back_sums).astype(jnp.bfloat16)
    leaf_result = jnp.einsum(
        "inb,ibd->ind", leaf_residue, own_inverse, preferred_element_type=jnp.float32
    ).astype(jnp.bfloat16)
    return (leaf_result[None, :, None], own_top)


def solution(mesh):
    placed = (
        P("sub", "row", "col", None, None),
        P("sub", "row", "col", None, None),
        P("sub", "row", None, "col", None, None),
        P("sub", "row", None, "col"),
        P(),
        P(),
        P("row", "col", None, None),
    )
    return jax.shard_map(
        local,
        mesh=mesh,
        in_specs=placed,
        out_specs=(P("sub", "row", "col", None, None), P("row", None, None)),
        check_vma=False,
    )
```

profile of v0, /device:TPU:1, one launch (start us, length us, event | category | flops | bytes accessed | tf_op | source)
XLA Modules:
  0.0 1734.4 jit_solution(8568360056786855845)
XLA Ops:
  61.1 60.7 %psum.35 = bf16[1,64,256]{2,1,0:T(8,128)(2,1)S(1)} all-reduce(bf16[1,64,256]{2,1,0:T(8,128)(2,1)S(1)} %fusion.62), channel_id=1, replica_groups=mesh['sub'=4,'row'=16,'col'=4] {'sub','col'}, use_global_device_ids=true, to_apply=%region_0.1 | all-reduce | flops 16384 | bytes 65536 | tf_op jit(solution)/shard_map/psum | solution.py:33
  121.8 778.5 %while.34 = (s32[]{:T(128)}, f32[1,64,256]{2,1,0:T(8,128)S(1)}, bf16[16,64,256]{2,1,0:T(8,128)(2,1)S(1)}, s32[1]{0:T(128)}, bf16[1,16,256,256]{3,2,1,0:T(8,128)(...) while((s32[]{:T(128)}, f32[1,64,256]{2,1,0:T(8,128)S(1)}, ...), condition=%wide.region_3.4_spmd.clone, body=%wide.region_1.3_spmd.clone.sunk | while | flops 17088520 | bytes 755900 | solution.py:61
  123.0 56.3 %psum.40 = bf16[64,256]{1,0:T(8,128)(2,1)S(1)} all-reduce(bf16[64,256]{1,0:T(8,128)(2,1)S(1)} %fusion.97), channel_id=1, replica_groups=mesh['sub'=4,'row'=16,'col'=4] {'row'}, use_global_device_ids=true, to_apply=%region_2.2 | all-reduce | flops 16384 | bytes 65536 | tf_op jit(solution)/shard_map/while/body/eval_jaxpr/psum | solution.py:9
  181.5 45.7 %psum.40 = bf16[64,256]{1,0:T(8,128)(2,1)S(1)} all-reduce(bf16[64,256]{1,0:T(8,128)(2,1)S(1)} %fusion.97), channel_id=1, replica_groups=mesh['sub'=4,'row'=16,'col'=4] {'row'}, use_global_device_ids=true, to_apply=%region_2.2 | all-reduce | flops 16384 | bytes 65536 | tf_op jit(solution)/shard_map/while/body/eval_jaxpr/psum | solution.py:9
  229.5 45.7 %psum.40 = bf16[64,256]{1,0:T(8,128)(2,1)S(1)} all-reduce(bf16[64,256]{1,0:T(8,128)(2,1)S(1)} %fusion.97), channel_id=1, replica_groups=mesh['sub'=4,'row'=16,'col'=4] {'row'}, use_global_device_ids=true, to_apply=%region_2.2 | all-reduce | flops 16384 | bytes 65536 | tf_op jit(solution)/shard_map/while/body/eval_jaxpr/psum | solution.py:9
  325.5 45.7 %psum.40 = bf16[64,256]{1,0:T(8,128)(2,1)S(1)} all-reduce(bf16[64,256]{1,0:T(8,128)(2,1)S(1)} %fusion.97), channel_id=1, replica_groups=mesh['sub'=4,'row'=16,'col'=4] {'row'}, use_global_device_ids=true, to_apply=%region_2.2 | all-reduce | flops 16384 | bytes 65536 | tf_op jit(solution)/shard_map/while/body/eval_jaxpr/psum | solution.py:9
  900.4 765.6 %while.33 = (s32[]{:T(128)}, bf16[16,64,256]{2,1,0:T(8,128)(2,1)S(1)}, bf16[16,64,256]{2,1,0:T(8,128)(2,1)S(1)}, s32[]{:T(128)}, s32[1]{0:T(128)}, /*index=5*/bf...) while((s32[]{:T(128)}, ...), condition=%wide.region_6.7_spmd, body=%wide.region_4.6_spmd.sunk | while | flops 17039368 | bytes 494251 | solution.py:81
  901.5 45.7 %psum.39 = bf16[64,256]{1,0:T(8,128)(2,1)S(1)} all-reduce(bf16[64,256]{1,0:T(8,128)(2,1)S(1)} %convolution_convert_fusion.6), channel_id=1, replica_groups=mesh['sub'=4,'row'=16,'col'=4] {'row'}, use_global_device_ids=true, to_apply=%region_5.5 | all-reduce | flops 16384 | bytes 65536 | tf_op jit(solution)/shard_map/while/body/eval_jaxpr/psum | solution.py:74
  949.3 45.7 %psum.39 = bf16[64,256]{1,0:T(8,128)(2,1)S(1)} all-reduce(bf16[64,256]{1,0:T(8,128)(2,1)S(1)} %convolution_convert_fusion.6), channel_id=1, replica_groups=mesh['sub'=4,'row'=16,'col'=4] {'row'}, use_global_device_ids=true, to_apply=%region_5.5 | all-reduce | flops 16384 | bytes 65536 | tf_op jit(solution)/shard_map/while/body/eval_jaxpr/psum | solution.py:74
  997.2 45.7 %psum.39 = bf16[64,256]{1,0:T(8,128)(2,1)S(1)} all-reduce(bf16[64,256]{1,0:T(8,128)(2,1)S(1)} %convolution_convert_fusion.6), channel_id=1, replica_groups=mesh['sub'=4,'row'=16,'col'=4] {'row'}, use_global_device_ids=true, to_apply=%region_5.5 | all-reduce | flops 16384 | bytes 65536 | tf_op jit(solution)/shard_map/while/body/eval_jaxpr/psum | solution.py:74
  1045.0 45.7 %psum.39 = bf16[64,256]{1,0:T(8,128)(2,1)S(1)} all-reduce(bf16[64,256]{1,0:T(8,128)(2,1)S(1)} %convolution_convert_fusion.6), channel_id=1, replica_groups=mesh['sub'=4,'row'=16,'col'=4] {'row'}, use_global_device_ids=true, to_apply=%region_5.5 | all-reduce | flops 16384 | bytes 65536 | tf_op jit(solution)/shard_map/while/body/eval_jaxpr/psum | solution.py:74
  1092.9 45.7 %psum.39 = bf16[64,256]{1,0:T(8,128)(2,1)S(1)} all-reduce(bf16[64,256]{1,0:T(8,128)(2,1)S(1)} %convolution_convert_fusion.6), channel_id=1, replica_groups=mesh['sub'=4,'row'=16,'col'=4] {'row'}, use_global_device_ids=true, to_apply=%region_5.5 | all-reduce | flops 16384 | bytes 65536 | tf_op jit(solution)/shard_map/while/body/eval_jaxpr/psum | solution.py:74
  1140.7 45.7 %psum.39 = bf16[64,256]{1,0:T(8,128)(2,1)S(1)} all-reduce(bf16[64,256]{1,0:T(8,128)(2,1)S(1)} %convolution_convert_fusion.6), channel_id=1, replica_groups=mesh['sub'=4,'row'=16,'col'=4] {'row'}, use_global_device_ids=true, to_apply=%region_5.5 | all-reduce | flops 16384 | bytes 65536 | tf_op jit(solution)/shard_map/while/body/eval_jaxpr/psum | solution.py:74
  1188.6 45.7 %psum.39 = bf16[64,256]{1,0:T(8,128)(2,1)S(1)} all-reduce(bf16[64,256]{1,0:T(8,128)(2,1)S(1)} %convolution_convert_fusion.6), channel_id=1, replica_groups=mesh['sub'=4,'row'=16,'col'=4] {'row'}, use_global_device_ids=true, to_apply=%region_5.5 | all-reduce | flops 16384 | bytes 65536 | tf_op jit(solution)/shard_map/while/body/eval_jaxpr/psum | solution.py:74
  1236.4 45.7 %psum.39 = bf16[64,256]{1,0:T(8,128)(2,1)S(1)} all-reduce(bf16[64,256]{1,0:T(8,128)(2,1)S(1)} %convolution_convert_fusion.6), channel_id=1, replica_groups=mesh['sub'=4,'row'=16,'col'=4] {'row'}, use_global_device_ids=true, to_apply=%region_5.5 | all-reduce | flops 16384 | bytes 65536 | tf_op jit(solution)/shard_map/while/body/eval_jaxpr/psum | solution.py:74
  1284.3 45.7 %psum.39 = bf16[64,256]{1,0:T(8,128)(2,1)S(1)} all-reduce(bf16[64,256]{1,0:T(8,128)(2,1)S(1)} %convolution_convert_fusion.6), channel_id=1, replica_groups=mesh['sub'=4,'row'=16,'col'=4] {'row'}, use_global_device_ids=true, to_apply=%region_5.5 | all-reduce | flops 16384 | bytes 65536 | tf_op jit(solution)/shard_map/while/body/eval_jaxpr/psum | solution.py:74
  1332.1 45.7 %psum.39 = bf16[64,256]{1,0:T(8,128)(2,1)S(1)} all-reduce(bf16[64,256]{1,0:T(8,128)(2,1)S(1)} %convolution_convert_fusion.6), channel_id=1, replica_groups=mesh['sub'=4,'row'=16,'col'=4] {'row'}, use_global_device_ids=true, to_apply=%region_5.5 | all-reduce | flops 16384 | bytes 65536 | tf_op jit(solution)/shard_map/while/body/eval_jaxpr/psum | solution.py:74
  1380.0 45.7 %psum.39 = bf16[64,256]{1,0:T(8,128)(2,1)S(1)} all-reduce(bf16[64,256]{1,0:T(8,128)(2,1)S(1)} %convolution_convert_fusion.6), channel_id=1, replica_groups=mesh['sub'=4,'row'=16,'col'=4] {'row'}, use_global_device_ids=true, to_apply=%region_5.5 | all-reduce | flops 16384 | bytes 65536 | tf_op jit(solution)/shard_map/while/body/eval_jaxpr/psum | solution.py:74
  1427.8 45.7 %psum.39 = bf16[64,256]{1,0:T(8,128)(2,1)S(1)} all-reduce(bf16[64,256]{1,0:T(8,128)(2,1)S(1)} %convolution_convert_fusion.6), channel_id=1, replica_groups=mesh['sub'=4,'row'=16,'col'=4] {'row'}, use_global_device_ids=true, to_apply=%region_5.5 | all-reduce | flops 16384 | bytes 65536 | tf_op jit(solution)/shard_map/while/body/eval_jaxpr/psum | solution.py:74
  1475.6 45.7 %psum.39 = bf16[64,256]{1,0:T(8,128)(2,1)S(1)} all-reduce(bf16[64,256]{1,0:T(8,128)(2,1)S(1)} %convolution_convert_fusion.6), channel_id=1, replica_groups=mesh['sub'=4,'row'=16,'col'=4] {'row'}, use_global_device_ids=true, to_apply=%region_5.5 | all-reduce | flops 16384 | bytes 65536 | tf_op jit(solution)/shard_map/while/body/eval_jaxpr/psum | solution.py:74
  1523.5 45.7 %psum.39 = bf16[64,256]{1,0:T(8,128)(2,1)S(1)} all-reduce(bf16[64,256]{1,0:T(8,128)(2,1)S(1)} %convolution_convert_fusion.6), channel_id=1, replica_groups=mesh['sub'=4,'row'=16,'col'=4] {'row'}, use_global_device_ids=true, to_apply=%region_5.5 | all-reduce | flops 16384 | bytes 65536 | tf_op jit(solution)/shard_map/while/body/eval_jaxpr/psum | solution.py:74
  1571.3 45.7 %psum.39 = bf16[64,256]{1,0:T(8,128)(2,1)S(1)} all-reduce(bf16[64,256]{1,0:T(8,128)(2,1)S(1)} %convolution_convert_fusion.6), channel_id=1, replica_groups=mesh['sub'=4,'row'=16,'col'=4] {'row'}, use_global_device_ids=true, to_apply=%region_5.5 | all-reduce | flops 16384 | bytes 65536 | tf_op jit(solution)/shard_map/while/body/eval_jaxpr/psum | solution.py:74
  1619.2 45.7 %psum.39 = bf16[64,256]{1,0:T(8,128)(2,1)S(1)} all-reduce(bf16[64,256]{1,0:T(8,128)(2,1)S(1)} %convolution_convert_fusion.6), channel_id=1, replica_groups=mesh['sub'=4,'row'=16,'col'=4] {'row'}, use_global_device_ids=true, to_apply=%region_5.5 | all-reduce | flops 16384 | bytes 65536 | tf_op jit(solution)/shard_map/while/body/eval_jaxpr/psum | solution.py:74
  1673.0 53.1 %reduce-scatter.2.cloned.1.call-done = bf16[4,64,256]{2,1,0:T(8,128)(2,1)} async-done(((bf16[64,64,256]{2,1,0:T(8,128)(2,1)}), bf16[4,64,256]{2,1,0:T(8,128)(2,1)}) %reduce-scatter.2.cloned.1.call-update) | async-done | bytes 131088 | tf_op jit(solution)/shard_map/reduce_scatter | solution.py:88
  (118 shorter events, 680.3 us)
Async XLA Ops:
  7.2 0.9 copy-start
  7.2 47.2 %all-gather.5.cloned.1.call-start = ((), (), s32[]{:S(2)}) async-start(), calls=%async_computation.2 | async-start | bytes 2228224 | tf_op jit(solution)/shard_map/all_gather | solution.py:27
  10.1 111.7 %all-gather.3.cloned.1.call-start = ((), (), s32[]{:S(2)}) async-start(), calls=%async_computation.1 | async-start | bytes 2621440 | tf_op jit(solution)/shard_map/all_gather | solution.py:35
  10.8 1715.3 %reduce-scatter.2.cloned.1.call-start = ((), (), s32[]{:S(2)}) async-start(), calls=%async_computation.3 | async-start | bytes 2228224 | tf_op jit(solution)/shard_map/reduce_scatter | solution.py:88
  1672.3 53.7 %copy-start.1 = (bf16[4,64,256]{2,1,0:T(8,128)(2,1)S(1)}, bf16[4,64,256]{2,1,0:T(8,128)(2,1)}, u32[]{:S(2)}) copy-start(bf16[4,64,256]{2,1,0:T(8,128)(2,1)} %fusion.50) | copy-start | bytes 393220
  1672.4 53.7 %copy-start.2 = (bf16[1,4,1,256,256]{4,3,2,1,0:T(8,128)(2,1)S(1)}, bf16[1,4,1,256,256]{4,3,2,1,0:T(8,128)(2,1)}, u32[]{:S(2)}) copy-start(bf16[1,4,1,256,256]{4,3,2,1,0:T(8,128)(2,1)} %param.12) | copy-start | bytes 1572868
Sparse Core Ops, SparseCore 0:
  10.4 43.9 all-gather.4
  56.2 31.6 all-gather.2
  1672.5 53.5 reduce-scatter.1
where the time goes:
time: 1740 us; the launch traced here: 1730 us
  blocking collectives  1530 us (88%)
  waiting for transfers between devices  96.7 us (6%)
  matrix products  85.4 us (5%)
    psum x16, blocking collectives, spread(): return lax.psum(block, axis)  742 us
    psum x16, blocking collectives, backward_step(): summed = lax.psum(term.astype(jnp.bfloat16), 'row').astype(jnp.float32)  732 us
    psum x1, blocking collectives, local(): lax.psum(partial_value.astype(jnp.bfloat16), ('sub', 'col'))  60.7 us
    reduce_scatter x1, waiting for transfers between devices, local(): lax.psum_scatter(jnp.einsum('aine,aieb->inb', scaled, block_slice, prefer...  53.1 us
    all_gather x1, waiting for transfers between devices, local(): lax.all_gather(leaf_forward, 'row', axis=0, tiled=True)[None]  42.8 us
  transfers between devices with their start and end apart: 3, of which 2 were waited for; matrix products, arithmetic and copies ran while one was open for 0% of the time, Pallas kernels for 0%

commit v1 on v0

v1 whole, which is shorter than its diff:
```python
import jax
import jax.numpy as jnp
from jax import lax
from jax.experimental import pallas as pl
from jax.experimental.pallas import tpu as pltpu
from jax.sharding import Mesh, PartitionSpec as P

BF = jnp.bfloat16
F32 = jnp.float32
ROW = ("z", "core")
SWAP = [(0, 1), (1, 0)]
NT = (((1,), (1,)), ((), ()))
NN = (((1,), (0,)), ((), ()))


def slot(a, b, rows, cols, per):
    c, j = divmod(b, per)
    half = per // 2
    if j < half:
        return (a * cols + c) * half + j
    return ((rows - 1 - a) * cols + cols - 1 - c) * half + j - half


def top_kernel(slots, r_ref, u_ref, g_ref, f_ref, x_ref, zs):
    count = r_ref.shape[0]

    def dot(a, b, dims):
        return lax.dot_general(a, b, dims, preferred_element_type=F32)

    def rhs(k):
        return r_ref[k].astype(F32) - u_ref[k].astype(F32)

    summed = rhs(0)
    for k in range(count):
        z = dot(summed.astype(BF), g_ref[k], NT).astype(BF)
        zs[k] = z
        if k + 1 < count:
            later = rhs(k + 1)
            for b in range(k):
                later -= dot(zs[b], f_ref[slots[k + 1, b]], NT)
            summed = later - dot(z, f_ref[slots[k + 1, k]], NT)
    summed = zs[count - 1].astype(F32)
    for k in reversed(range(count)):
        x = dot(summed.astype(BF), g_ref[k], NN).astype(BF)
        x_ref[k] = x
        if k > 0:
            later = zs[k - 1].astype(F32)
            for a in range(count - 1, k, -1):
                later -= dot(x_ref[a], f_ref[slots[a, k - 1]], NN)
            summed = later - dot(x, f_ref[slots[k, k - 1]], NN)


def top_solve(slots, rhs, updates, inverse, factor):
    whole = pl.BlockSpec(memory_space=pltpu.VMEM)
    return pl.pallas_call(
        lambda *refs: top_kernel(slots, *refs),
        out_shape=jax.ShapeDtypeStruct(rhs.shape, BF),
        in_specs=[whole] * 4,
        out_specs=whole,
        scratch_shapes=[pltpu.VMEM(rhs.shape, BF)],
        compiler_params=pltpu.CompilerParams(vmem_limit_bytes=56 << 20),
        name="top_solve",
    )(rhs, updates, inverse, factor)


def sum_over(value, axis, size):
    value = value.astype(BF)
    got = [value] + [
        lax.ppermute(value, axis, [(i, (i + k) % size) for i in range(size)])
        for k in range(1, size)
    ]
    got = [g.astype(F32) for g in got]
    return (got[0] + got[2]) + (got[1] + got[3])


def build(mesh):
    subs, zs, cores, cols = mesh.devices.shape

    def local(leaf_rhs, leaf_inverse, coupling, pattern, top_rhs, top_inverse, top_factor):
        core = lax.axis_index("core")
        col = lax.axis_index("col")
        row = lax.axis_index("z") * cores + core
        own_rhs = leaf_rhs[0, :, 0]
        own_inverse = jnp.tril(leaf_inverse[0, :, 0])
        coupled = coupling[0, 0, :, 0]
        weights = pattern[0, 0, :, 0].astype(BF)
        leaves, nrhs, size = own_rhs.shape
        rows = zs * cores
        per = top_factor.shape[1]
        half = per // 2
        slots = {
            (a, b): slot(a, b, rows, cols, per) for a in range(rows) for b in range(a)
        }

        blocks = top_factor[0]
        pairs = [
            (i, rows * cols - 1 - i)
            for i in range(rows * cols)
            if i // cols - per * (i % cols) > half
        ]
        moved = lax.ppermute(blocks[half:], ("z", "core", "col"), pairs)
        shard = jnp.where(row - per * col <= 0, moved, blocks[:half])
        factor = lax.all_gather(shard, ("z", "core", "col"), axis=0, tiled=True)
        top_tri = jnp.tril(top_inverse)

        leaf_forward = jnp.einsum(
            "inb,idb->ind", own_rhs, own_inverse, preferred_element_type=F32
        ).astype(BF)
        mine = lax.all_to_all(
            jnp.broadcast_to(leaf_forward[None], (zs,) + leaf_forward.shape),
            "z", 0, 0, tiled=True,
        )
        other = lax.ppermute(mine, "core", SWAP)
        first = core == 0
        forward = jnp.stack(
            [jnp.where(first, mine, other), jnp.where(first, other, mine)], axis=1
        ).reshape(rows * leaves, nrhs, size)
        partial = jnp.einsum(
            "inb,ieb->ne", forward * weights[:, None, None], coupled,
            preferred_element_type=F32,
        )
        update = sum_over(sum_over(partial, "sub", subs), "col", cols).astype(BF)
        updates = lax.all_gather(update, ROW, axis=0)

        solution = top_solve(slots, top_rhs, updates, top_tri, factor)
        own_top = lax.dynamic_index_in_dim(solution, row, 0, keepdims=False)

        back = jnp.einsum(
            "ine,ieb->inb", own_top[None] * weights[:, None, None], coupled,
            preferred_element_type=F32,
        ).astype(BF).reshape(zs, cores, leaves, nrhs, size)
        mine = jnp.where(first, back[:, 0], back[:, 1])
        other = lax.ppermute(jnp.where(first, back[:, 1], back[:, 0]), "core", SWAP)
        pair = (mine.astype(F32) + other.astype(F32)).astype(BF)
        spread = lax.all_to_all(pair, "z", 0, 0, tiled=True)
        back_sums = jnp.sum(spread.astype(F32), axis=0)
        leaf_residue = (leaf_forward.astype(F32) - back_sums).astype(BF)
        leaf_result = jnp.einsum(
            "inb,ibd->ind", leaf_residue, own_inverse, preferred_element_type=F32
        ).astype(BF)
        return leaf_result[None, :, None], own_top[None]

    return local


def solution(mesh):
    subs, rows, cols = (mesh.shape[name] for name in ("sub", "row", "col"))
    mesh = Mesh(
        mesh.devices.reshape(subs, rows // 2, 2, cols), ("sub", "z", "core", "col")
    )
    placed = (
        P("sub", ROW, "col", None, None),
        P("sub", ROW, "col", None, None),
        P("sub", ROW, None, "col", None, None),
        P("sub", ROW, None, "col"),
        P(),
        P(),
        P(ROW, "col", None, None),
    )
    return jax.shard_map(
        build(mesh),
        mesh=mesh,
        in_specs=placed,
        out_specs=(P("sub", ROW, "col", None, None), P(ROW, None, None)),
        check_vma=False,
    )
```

time: 1740 us -> 212 us (0.12)
  blocking collectives: 1530 us -> 81 us
  matrix products: 85.4 us -> 13.4 us
  waiting for transfers between devices: 96.7 us -> 55.8 us
  starting transfers between devices: 0.12 us -> 20.3 us
  Pallas kernels: 0 us -> 18.2 us
    psum x33 -> x0, blocking collectives: 1530 us -> none  [the longest x16 742 us: spread(): return lax.psum(block, axis)]
    dot_general x67 -> x3, matrix products: 83.6 us -> 12.5 us  [the longest x1 6.16 us: local(): jnp.einsum('inb,ieb->ne', forward * weights[:, None, None], coupled, pref...]
    all_to_all x0 -> x1, blocking collectives: none -> 58.6 us  [local(): lax.all_to_all(jnp.broadcast_to(leaf_forward[None], (zs,) + leaf_forward....]
    reduce_scatter x1 -> x0, waiting for transfers between devices: 53.1 us -> none  [local(): lax.psum_scatter(jnp.einsum('aine,aieb->inb', scaled, block_slice, prefer...]
    all_to_all x0 -> x1, waiting for transfers between devices: none -> 27.9 us  [local(): spread = lax.all_to_all(pair, 'z', 0, 0, tiled=True)]
    all_gather x2 -> x1, waiting for transfers between devices: 42.9 us -> 19.3 us  [local(): factor = lax.all_gather(shard, ('z', 'core', 'col'), axis=0, tiled=True)]
    all_gather x0 -> x1, blocking collectives: none -> 22.5 us  [local(): updates = lax.all_gather(update, ROW, axis=0)]
    pallas_call x0 -> x1, Pallas kernels: none -> 18.2 us  [top_solve(): pl.pallas_call(lambda *refs: top_kernel(slots, *refs), out_shape=jax.Shap...]
  transfers between devices with their start and end apart: 3 -> 11, of which waited for: 2 -> 7; matrix products, arithmetic and copies ran while one was open for 0% -> 5% of each run, Pallas kernels for 0% -> 0%
where the time goes in v1:
time: 212 us
  blocking collectives  81 us (38%)
  waiting for transfers between devices  55.8 us (26%)
  starting transfers between devices  20.3 us (10%)
  Pallas kernels  18.2 us (9%)
  between operations  14.2 us (7%)
  matrix products  13.4 us (6%)
  other arithmetic  5.81 us (3%)
  local copies, waits for them, and re-layouts  3.27 us (2%)
    all_to_all x1, blocking collectives, local(): lax.all_to_all(jnp.broadcast_to(leaf_forward[None], (zs,) + leaf_forward....  58.6 us
    all_to_all x1, waiting for transfers between devices, local(): spread = lax.all_to_all(pair, 'z', 0, 0, tiled=True)  27.9 us
    all_gather x1, blocking collectives, local(): updates = lax.all_gather(update, ROW, axis=0)  22.5 us
    all_gather x1, waiting for transfers between devices, local(): factor = lax.all_gather(shard, ('z', 'core', 'col'), axis=0, tiled=True)  19.3 us
    pallas_call x1, Pallas kernels, top_solve(): pl.pallas_call(lambda *refs: top_kernel(slots, *refs), out_shape=jax.Shap...  18.2 us
    ppermute x6, starting transfers between devices, sum_over(): lax.ppermute(value, axis, [(i, (i + k) % size) for i in range(size)])  13.2 us
    dot_general x1, matrix products, local(): jnp.einsum('inb,ieb->ne', forward * weights[:, None, None], coupled, pref...  6.16 us
    dot_general x1, matrix products, local(): jnp.einsum('ine,ieb->inb', own_top[None] * weights[:, None, None], couple...  5.01 us
  transfers between devices with their start and end apart: 11, of which 7 were waited for; matrix products, arithmetic and copies ran while one was open for 5% of the time, Pallas kernels for 0%

profile of v1, /device:TPU:1, one launch (start us, length us, event | category | flops | bytes accessed | tf_op | source)
XLA Modules:
  0.0 211.9 jit_solution(6203857085825078653)
XLA Ops:
  7.2 1.0 slice_bitcast_fusion
  8.9 1.7 bitcast_select_fusion.5
  10.7 1.3 fusion.11
  12.2 58.6 %all_to_all.10 = bf16[8,4,64,256]{3,2,1,0:T(8,128)(2,1)S(1)} all-to-all(bf16[8,4,64,256]{3,2,1,0:T(8,128)(2,1)S(1)} %broadcast_in_dim.31), channel_id=1, replica_groups=mesh['sub'=4,'z'=8,'core'=2,'col'=4] {'z'}, dimensions={0} | all-to-all | bytes 2097152 | tf_op jit(solution)/shard_map/all_to_all | solution.py:109
  70.7 2.1 collective-permute-start
  72.8 2.3 %collective-permute-done = bf16[8,4,64,256]{3,2,1,0:T(8,128)(2,1)S(1)} collective-permute-done((bf16[8,4,64,256]{3,2,1,0:T(8,128)(2,1)S(1)}, bf16[8,4,64,256]{3,2,1,0:T(8,128)(2,1)S(1)}, u32[]{:S(2)}, u32[]{:S(2)}) %collective-permute-start) | collective-permute-done | bytes 1048608 | tf_op jit(solution)/shard_map/ppermute | solution.py:113
  75.9 6.2 %fusion.16 = bf16[64,256]{1,0:T(8,128)(2,1)S(1)} fusion(bf16[64,64,256]{2,1,0:T(8,128)(2,1)S(1)} %bitcast_multiply_fusion, bf16[1,1,64,1,256,256]{5,4,3,2,1,0:T(8,128)(2,1)} %param.9), kind=kOutput, calls=%fused_computation.18 | convolution fusion | flops 536887296 | bytes 10518528 | tf_op jit(solution)/shard_map/inb,ieb->ne/dot_general | solution.py:118
  82.0 3.1 %collective-permute-start.1 = (bf16[64,256]{1,0:T(8,128)(2,1)S(1)}, bf16[64,256]{1,0:T(8,128)(2,1)S(1)}, u32[]{:S(2)}, u32[]{:S(2)}) collective-permute-start(bf16[64,256]{1,0:T(8,128)(2,1)S(1)} %fusion.16), channel_id=1, source_target_pairs={{0,128},{64,192},{128,0},{192,64},{1,129},{65,193},{129,1},{193,65... | collective-permute-start | bytes 98312 | tf_op jit(solution)/shard_map/ppermute | solution.py:69
  85.1 2.7 %collective-permute-start.3 = (bf16[64,256]{1,0:T(8,128)(2,1)S(1)}, bf16[64,256]{1,0:T(8,128)(2,1)S(1)}, u32[]{:S(2)}, u32[]{:S(2)}) collective-permute-start(bf16[64,256]{1,0:T(8,128)(2,1)S(1)} %fusion.16), channel_id=1, source_target_pairs={{0,192},{64,0},{128,64},{192,128},{1,193},{65,1},{129,65},{193,129... | collective-permute-start | bytes 98312 | tf_op jit(solution)/shard_map/ppermute | solution.py:69
  87.8 1.3 collective-permute-done.2
  89.8 6.7 %collective-permute-start.5 = (bf16[64,256]{1,0:T(8,128)(2,1)S(1)}, bf16[64,256]{1,0:T(8,128)(2,1)S(1)}, u32[]{:S(2)}, u32[]{:S(2)}) collective-permute-start(bf16[64,256]{1,0:T(8,128)(2,1)S(1)} %add_convert_fusion.1), channel_id=1, source_target_pairs={{0,1},{1,2},{2,3},{3,0},{4,5},{5,6},{6,7},{7,4},{8,9},{9,10},{10,1... | collective-permute-start | bytes 98312 | tf_op jit(solution)/shard_map/ppermute | solution.py:69
  96.5 1.5 broadcast_select_fusion.refs_2_
  98.4 2.2 %collective-permute-done.6 = bf16[64,256]{1,0:T(8,128)(2,1)S(1)} collective-permute-done((bf16[64,256]{1,0:T(8,128)(2,1)S(1)}, bf16[64,256]{1,0:T(8,128)(2,1)S(1)}, u32[]{:S(2)}, u32[]{:S(2)}) %collective-permute-start.6) | collective-permute-done | bytes 32800 | tf_op jit(solution)/shard_map/ppermute | solution.py:69
  100.6 22.5 %all-gather = bf16[1024,256]{1,0:T(8,128)(2,1)} all-gather(bf16[64,256]{1,0:T(8,128)(2,1)S(1)} %add_convert_fusion), channel_id=2, replica_groups=mesh['sub'=4,'z'=8,'core'=2,'col'=4] {'z','core'}, dimensions={0}, use_global_device_ids=true | all-gather | bytes 557056 | tf_op jit(solution)/shard_map/all_gather | solution.py:123
  123.0 19.3 %all-gather.3.cloned.1.call-done.refs_3_ = bf16[128,256,256]{2,1,0:T(8,128)(2,1)} async-done(((bf16[2,256,256]{2,1,0:T(8,128)(2,1)}), bf16[128,256,256]{2,1,0:T(8,128)(2,1)}) %all-gather.3.cloned.1.call-update) | async-done | bytes 16777232 | tf_op jit(solution)/shard_map/all_gather | solution.py:103
  142.4 18.2 %top_solve.1 = bf16[16,64,256]{2,1,0:T(8,128)(2,1)} custom-call(bf16[16,64,256]{2,1,0:T(8,128)(2,1)} %refs_0_.1, bf16[16,64,256]{2,1,0:T(8,128)(2,1)} %bitcast.70, bf16[16,256,256]{2,1,0:T(8,128)(2,1)} %broadcast_select_fusion.refs_2_, bf16[128,256,256]{2,1,0:T(8,128)(2,1)} %all-gather.3.cloned.1.call-done.refs_3_), custom_call_target="tpu_custom_call" | custom-call | tf_op jit(solution)/shard_map/top_solve/pallas_call | solution.py:55
  160.6 0.8 fusion.29
  161.4 5.0 %fusion.6 = bf16[64,64,256]{2,1,0:T(8,128)(2,1)S(1)} fusion(bf16[1,1,64,1,256,256]{5,4,3,2,1,0:T(8,128)(2,1)} %param.9, bf16[64,256]{1,0:T(8,128)(2,1)S(1)} %fusion.29, bf16[64]{0:T(256)(128)(2,1)S(1)} %convert_bitcast_fusion), kind=kOutput, calls=%fused_computation.12 | convolution fusion | flops 538968064 | bytes 10518656 | tf_op jit(solution)/shard_map/ine,ieb->inb/dot_general | solution.py:128
  166.8 2.4 %collective-permute-done.8 = bf16[8,4,64,256]{3,2,1,0:T(8,128)(2,1)S(1)} collective-permute-done((bf16[8,4,64,256]{3,2,1,0:T(8,128)(2,1)S(1)}, bf16[8,4,64,256]{3,2,1,0:T(8,128)(2,1)S(1)}, u32[]{:S(2)}, u32[]{:S(2)}) %collective-permute-start.8) | collective-permute-done | bytes 1048608 | tf_op jit(solution)/shard_map/ppermute | solution.py:133
  169.3 1.5 fusion.4
  170.8 4.0 %all-to-all-start.1 = ((bf16[8,4,64,256]{3,2,1,0:T(8,128)(2,1)}), bf16[8,4,64,256]{3,2,1,0:T(8,128)(2,1)S(1)}, u32[]{:S(2)}, u32[]{:S(2)}) async-start(bf16[8,4,64,256]{3,2,1,0:T(8,128)(2,1)} %fusion.4), calls=%async_computation.1 | async-start | bytes 2097152 | tf_op jit(solution)/shard_map/all_to_all | solution.py:135
  174.8 1.4 constant_dynamic-slice_fusion
  176.2 27.9 %all-to-all-done.1 = bf16[8,4,64,256]{3,2,1,0:T(8,128)(2,1)S(1)} async-done(((bf16[8,4,64,256]{3,2,1,0:T(8,128)(2,1)}), bf16[8,4,64,256]{3,2,1,0:T(8,128)(2,1)S(1)}, u32[]{:S(2)}, u32[]{:S(2)}) %all-to-all-start.1) | async-done | bytes 1048608 | tf_op jit(solution)/shard_map/all_to_all | solution.py:135
  204.2 0.9 fusion.12
  (30 shorter events, 3.4 us)
Async XLA Ops:
  7.2 3.5 %copy-start = (bf16[1,4,1,64,256]{4,3,2,1,0:T(8,128)(2,1)S(1)}, bf16[1,4,1,64,256]{4,3,2,1,0:T(8,128)(2,1)}, u32[]{:S(2)}) copy-start(bf16[1,4,1,64,256]{4,3,2,1,0:T(8,128)(2,1)} %param.7) | copy-start | bytes 393220
  7.2 135.2 %all-gather.3.cloned.1.call-start = ((), (), s32[]{:S(2)}) async-start(), calls=%async_computation.2 | async-start | bytes 17039360 | tf_op jit(solution)/shard_map/all_gather | solution.py:103
  8.2 0.7 collective-permute-start.7
  10.7 62.1 %copy-start.3 = (s32[1,1,64,1]{2,3,1,0:T(1,128)S(1)}, s32[1,1,64,1]{2,3,1,0:T(1,128)}, u32[]{:S(2)}) copy-start(s32[1,1,64,1]{2,3,1,0:T(1,128)} %param.10) | copy-start | bytes 772
  70.7 4.3 %collective-permute-start = (bf16[8,4,64,256]{3,2,1,0:T(8,128)(2,1)S(1)}, bf16[8,4,64,256]{3,2,1,0:T(8,128)(2,1)S(1)}, u32[]{:S(2)}, u32[]{:S(2)}) collective-permute-start(bf16[8,4,64,256]{3,2,1,0:T(8,128)(2,1)S(1)} %all_to_all.10), channel_id=1, source_target_pairs={{0,4},{4,0},{1,5},{5,1},{2,6},{6,2},{3,7},{7,3},{8,12},{12,8},{9,1... | collective-permute-start | bytes 3145736 | tf_op jit(solution)/shard_map/ppermute | solution.py:113
  75.9 20.7 %copy-start.1 = (bf16[16,256,256]{2,1,0:T(8,128)(2,1)S(1)}, bf16[16,256,256]{2,1,0:T(8,128)(2,1)}, u32[]{:S(2)}) copy-start(bf16[16,256,256]{2,1,0:T(8,128)(2,1)} %param.12) | copy-start | bytes 6291460
  82.0 5.8 %collective-permute-start.1 = (bf16[64,256]{1,0:T(8,128)(2,1)S(1)}, bf16[64,256]{1,0:T(8,128)(2,1)S(1)}, u32[]{:S(2)}, u32[]{:S(2)}) collective-permute-start(bf16[64,256]{1,0:T(8,128)(2,1)S(1)} %fusion.16), channel_id=1, source_target_pairs={{0,128},{64,192},{128,0},{192,64},{1,129},{65,193},{129,1},{193,65... | collective-permute-start | bytes 98312 | tf_op jit(solution)/shard_map/ppermute | solution.py:69
  85.1 4.0 %collective-permute-start.2 = (bf16[64,256]{1,0:T(8,128)(2,1)S(1)}, bf16[64,256]{1,0:T(8,128)(2,1)S(1)}, u32[]{:S(2)}, u32[]{:S(2)}) collective-permute-start(bf16[64,256]{1,0:T(8,128)(2,1)S(1)} %fusion.16), channel_id=1, source_target_pairs={{0,64},{64,128},{128,192},{192,0},{1,65},{65,129},{129,193},{193,1... | collective-permute-start | bytes 98312 | tf_op jit(solution)/shard_map/ppermute | solution.py:69
  85.1 4.0 %collective-permute-start.3 = (bf16[64,256]{1,0:T(8,128)(2,1)S(1)}, bf16[64,256]{1,0:T(8,128)(2,1)S(1)}, u32[]{:S(2)}, u32[]{:S(2)}) collective-permute-start(bf16[64,256]{1,0:T(8,128)(2,1)S(1)} %fusion.16), channel_id=1, source_target_pairs={{0,192},{64,0},{128,64},{192,128},{1,193},{65,1},{129,65},{193,129... | collective-permute-start | bytes 98312 | tf_op jit(solution)/shard_map/ppermute | solution.py:69
  89.1 8.9 %collective-permute-start.4 = (bf16[64,256]{1,0:T(8,128)(2,1)S(1)}, bf16[64,256]{1,0:T(8,128)(2,1)S(1)}, u32[]{:S(2)}, u32[]{:S(2)}) collective-permute-start(bf16[64,256]{1,0:T(8,128)(2,1)S(1)} %add_convert_fusion.1), channel_id=1, source_target_pairs={{0,2},{1,3},{2,0},{3,1},{4,6},{5,7},{6,4},{7,5},{8,10},{9,11},{10,... | collective-permute-start | bytes 98312 | tf_op jit(solution)/shard_map/ppermute | solution.py:69
  89.8 8.6 %collective-permute-start.5 = (bf16[64,256]{1,0:T(8,128)(2,1)S(1)}, bf16[64,256]{1,0:T(8,128)(2,1)S(1)}, u32[]{:S(2)}, u32[]{:S(2)}) collective-permute-start(bf16[64,256]{1,0:T(8,128)(2,1)S(1)} %add_convert_fusion.1), channel_id=1, source_target_pairs={{0,1},{1,2},{2,3},{3,0},{4,5},{5,6},{6,7},{7,4},{8,9},{9,10},{10,1... | collective-permute-start | bytes 98312 | tf_op jit(solution)/shard_map/ppermute | solution.py:69
  96.5 4.1 %collective-permute-start.6 = (bf16[64,256]{1,0:T(8,128)(2,1)S(1)}, bf16[64,256]{1,0:T(8,128)(2,1)S(1)}, u32[]{:S(2)}, u32[]{:S(2)}) collective-permute-start(bf16[64,256]{1,0:T(8,128)(2,1)S(1)} %add_convert_fusion.1), channel_id=1, source_target_pairs={{0,3},{1,0},{2,1},{3,2},{4,7},{5,4},{6,5},{7,6},{8,11},{9,8},{10,9... | collective-permute-start | bytes 98312 | tf_op jit(solution)/shard_map/ppermute | solution.py:69
  166.5 2.7 %collective-permute-start.8 = (bf16[8,4,64,256]{3,2,1,0:T(8,128)(2,1)S(1)}, bf16[8,4,64,256]{3,2,1,0:T(8,128)(2,1)S(1)}, u32[]{:S(2)}, u32[]{:S(2)}) collective-permute-start(bf16[8,4,64,256]{3,2,1,0:T(8,128)(2,1)S(1)} %fusion.19), channel_id=1, source_target_pairs={{0,4},{4,0},{1,5},{5,1},{2,6},{6,2},{3,7},{7,3},{8,12},{12,8},{9,1... | collective-permute-start | bytes 3145736 | tf_op jit(solution)/shard_map/ppermute | solution.py:133
  170.8 33.4 %copy-start.2 = (bf16[1,4,1,256,256]{4,3,2,1,0:T(8,128)(2,1)S(1)}, bf16[1,4,1,256,256]{4,3,2,1,0:T(8,128)(2,1)}, u32[]{:S(2)}) copy-start(bf16[1,4,1,256,256]{4,3,2,1,0:T(8,128)(2,1)} %param.8) | copy-start | bytes 1572868
  170.8 33.3 %all-to-all-start.1 = ((bf16[8,4,64,256]{3,2,1,0:T(8,128)(2,1)}), bf16[8,4,64,256]{3,2,1,0:T(8,128)(2,1)S(1)}, u32[]{:S(2)}, u32[]{:S(2)}) async-start(bf16[8,4,64,256]{3,2,1,0:T(8,128)(2,1)} %fusion.4), calls=%async_computation.1 | async-start | bytes 2097152 | tf_op jit(solution)/shard_map/all_to_all | solution.py:135
Sparse Core Ops, SparseCore 0:
  10.8 131.5 all-gather.2

commit v2 on v1

--- a/solution.py
+++ b/solution.py
@@ -13,32 +13,43 @@
 NN = (((1,), (0,)), ((), ()))
 
 
-def slot(a, b, rows, cols, per):
-    c, j = divmod(b, per)
-    half = per // 2
-    if j < half:
-        return (a * cols + c) * half + j
-    return ((rows - 1 - a) * cols + cols - 1 - c) * half + j - half
-
-
-def top_kernel(slots, r_ref, u_ref, g_ref, f_ref, x_ref, zs):
+def first_block(a):
+    return a * (a - 1) // 2
+
+
+def top_kernel(units, r_ref, u_ref, g_ref, f_hbm, x_ref, zs, fac, sems):
     count = r_ref.shape[0]
+    half = f_hbm.shape[1]
 
     def dot(a, b, dims):
         return lax.dot_general(a, b, dims, preferred_element_type=F32)
 
     def rhs(k):
         return r_ref[k].astype(F32) - u_ref[k].astype(F32)
+
+    def block(a, b):
+        return fac[first_block(a) + b]
+
+    for a in range(1, count):
+        for b in range(a):
+            for part, unit in enumerate(units(a, b)):
+                pltpu.make_async_copy(
+                    f_hbm.at[unit],
+                    fac.at[first_block(a) + b, pl.ds(part * half, half)],
+                    sems.at[a],
+                ).start()
 
     summed = rhs(0)
     for k in range(count):
         z = dot(summed.astype(BF), g_ref[k], NT).astype(BF)
         zs[k] = z
         if k + 1 < count:
+            row = fac.at[pl.ds(first_block(k + 1), k + 1)]
+            pltpu.make_async_copy(row, row, sems.at[k + 1]).wait()
             later = rhs(k + 1)
             for b in range(k):
-                later -= dot(zs[b], f_ref[slots[k + 1, b]], NT)
-            summed = later - dot(z, f_ref[slots[k + 1, k]], NT)
+                later -= dot(zs[b], block(k + 1, b), NT)
+            summed = later - dot(z, block(k + 1, k), NT)
     summed = zs[count - 1].astype(F32)
     for k in reversed(range(count)):
         x = dot(summed.astype(BF), g_ref[k], NN).astype(BF)
@@ -46,21 +57,60 @@
         if k > 0:
             later = zs[k - 1].astype(F32)
             for a in range(count - 1, k, -1):
-                later -= dot(x_ref[a], f_ref[slots[a, k - 1]], NN)
-            summed = later - dot(x, f_ref[slots[k, k - 1]], NN)
-
-
-def top_solve(slots, rhs, updates, inverse, factor):
+                later -= dot(x_ref[a], block(a, k - 1), NN)
+            summed = later - dot(x, block(k, k - 1), NN)
+
+
+def top_solve(units, rhs, updates, inverse, factor):
     whole = pl.BlockSpec(memory_space=pltpu.VMEM)
+    count, nrhs, size = rhs.shape
     return pl.pallas_call(
-        lambda *refs: top_kernel(slots, *refs),
+        lambda *refs: top_kernel(units, *refs),
         out_shape=jax.ShapeDtypeStruct(rhs.shape, BF),
-        in_specs=[whole] * 4,
+        in_specs=[whole] * 3 + [pl.BlockSpec(memory_space=pl.ANY)],
         out_specs=whole,
-        scratch_shapes=[pltpu.VMEM(rhs.shape, BF)],
-        compiler_params=pltpu.CompilerParams(vmem_limit_bytes=56 << 20),
+        scratch_shapes=[
+            pltpu.VMEM(rhs.shape, BF),
+            pltpu.VMEM((first_block(count), size, size), BF),
+            pltpu.SemaphoreType.DMA((count,)),
+        ],
+        compiler_params=pltpu.CompilerParams(vmem_limit_bytes=40 << 20),
         name="top_solve",
     )(rhs, updates, inverse, factor)
+
+
+def back_kernel(where_ref, w_ref, x_ref, c_ref, mine_ref, other_ref):
+    z = pl.program_id(0)
+    core = where_ref[1]
+    leaves = mine_ref.shape[0]
+    for out, part in ((other_ref, 1 - core), (mine_ref, core)):
+        for leaf in range(leaves):
+            at = part * leaves + leaf
+            weight = w_ref[z * 2 * leaves + at].astype(F32)
+            value = lax.dot_general(
+                x_ref[...], c_ref[at], NN, preferred_element_type=F32
+            )
+            out[leaf] = (value * weight).astype(BF)
+
+
+def back_products(solution, coupled, pattern, row, core, zs, leaves):
+    _, nrhs, size = solution.shape
+    spec = pl.BlockSpec((None, leaves, nrhs, size), lambda z, *_: (z, 0, 0, 0))
+    out = jax.ShapeDtypeStruct((zs, leaves, nrhs, size), BF)
+    return pl.pallas_call(
+        back_kernel,
+        out_shape=(out, out),
+        grid_spec=pltpu.PrefetchScalarGridSpec(
+            num_scalar_prefetch=2,
+            grid=(zs,),
+            in_specs=[
+                pl.BlockSpec((None, nrhs, size), lambda z, at, w: (at[0], 0, 0)),
+                pl.BlockSpec((2 * leaves, size, size), lambda z, *_: (z, 0, 0)),
+            ],
+            out_specs=(spec, spec),
+        ),
+        name="back_products",
+    )(jnp.stack([row, core]), pattern, solution, coupled)
 
 
 def sum_over(value, axis, size):
@@ -86,28 +136,38 @@
         weights = pattern[0, 0, :, 0].astype(BF)
         leaves, nrhs, size = own_rhs.shape
         rows = zs * cores
-        per = top_factor.shape[1]
-        half = per // 2
-        slots = {
-            (a, b): slot(a, b, rows, cols, per) for a in range(rows) for b in range(a)
-        }
-
-        blocks = top_factor[0]
-        pairs = [
-            (i, rows * cols - 1 - i)
-            for i in range(rows * cols)
-            if i // cols - per * (i % cols) > half
-        ]
-        moved = lax.ppermute(blocks[half:], ("z", "core", "col"), pairs)
-        shard = jnp.where(row - per * col <= 0, moved, blocks[:half])
-        factor = lax.all_gather(shard, ("z", "core", "col"), axis=0, tiled=True)
+        assert top_factor.shape[1] == subs
+
+        sub = lax.axis_index("sub")
+        column = subs * col + sub
+        block = lax.dynamic_index_in_dim(top_factor[0], sub, 0, keepdims=False)
+        half = size // 2
+        pairs = []
+        for i in range(subs * rows * cols):
+            s, rest = divmod(i, rows * cols)
+            r, c = divmod(rest, cols)
+            if r > subs * c + s:
+                pairs.append((i, subs * rows * cols - 1 - i))
+        moved = lax.ppermute(block[half:], ("sub", "z", "core", "col"), pairs)
+        unit = jnp.where(row > column, block[:half], moved)
+        ring = lax.all_to_all(
+            jnp.broadcast_to(unit[None], (zs,) + unit.shape), "z", 0, 0, tiled=True
+        )
+
+        def units(a, b):
+            c, s = divmod(b, subs)
+            at = ((s * cols + c) * cores + a % cores) * zs + a // cores
+            return at, subs * rows * cols - 1 - at
+
         top_tri = jnp.tril(top_inverse)
 
         leaf_forward = jnp.einsum(
             "inb,idb->ind", own_rhs, own_inverse, preferred_element_type=F32
         ).astype(BF)
+        leaf_shared, ring = lax.optimization_barrier((leaf_forward, ring))
+        factor = lax.all_gather(ring, ("sub", "col", "core"), axis=0, tiled=True)
         mine = lax.all_to_all(
-            jnp.broadcast_to(leaf_forward[None], (zs,) + leaf_forward.shape),
+            jnp.broadcast_to(leaf_shared[None], (zs,) + leaf_forward.shape),
             "z", 0, 0, tiled=True,
         )
         other = lax.ppermute(mine, "core", SWAP)
@@ -122,15 +182,13 @@
         update = sum_over(sum_over(partial, "sub", subs), "col", cols).astype(BF)
         updates = lax.all_gather(update, ROW, axis=0)
 
-        solution = top_solve(slots, top_rhs, updates, top_tri, factor)
+        solution = top_solve(units, top_rhs, updates, top_tri, factor)
         own_top = lax.dynamic_index_in_dim(solution, row, 0, keepdims=False)
 
-        back = jnp.einsum(
-            "ine,ieb->inb", own_top[None] * weights[:, None, None], coupled,
-            preferred_element_type=F32,
-        ).astype(BF).reshape(zs, cores, leaves, nrhs, size)
-        mine = jnp.where(first, back[:, 0], back[:, 1])
-        other = lax.ppermute(jnp.where(first, back[:, 1], back[:, 0]), "core", SWAP)
+        mine, other = back_products(
+            solution, coupled, pattern[0, 0, :, 0], row, core, zs, leaves
+        )
+        other = lax.ppermute(other, "core", SWAP)
         pair = (mine.astype(F32) + other.astype(F32)).astype(BF)
         spread = lax.all_to_all(pair, "z", 0, 0, tiled=True)
         back_sums = jnp.sum(spread.astype(F32), axis=0)

time: 212 us -> 200 us (0.943)
  blocking collectives: 81 us -> 50.4 us
  starting transfers between devices: 20.3 us -> 35.3 us
  Pallas kernels: 18.2 us -> 22.6 us
  matrix products: 13.4 us -> 9.15 us
    all_to_all x1, blocking collectives: 58.6 us -> 31.4 us  [local(): lax.all_to_all(jnp.broadcast_to(leaf_shared[None], (zs,) + leaf_forward.s...]
    all_gather x1, waiting for transfers between devices: 19.3 us -> 0.01 us  [local(): factor = lax.all_gather(ring, ('sub', 'col', 'core'), axis=0, tiled=True)]
    all_to_all x0 -> x1, waiting for transfers between devices: none -> 16.5 us  [local(): lax.all_to_all(jnp.broadcast_to(unit[None], (zs,) + unit.shape), 'z', 0,...]
    ppermute x2, starting transfers between devices: 1 us -> 13.7 us  [the longest x1 13.5 us: local(): moved = lax.ppermute(block[half:], ('sub', 'z', 'core', 'col'), pairs)]
    dot_general x1 -> x0, matrix products: 5.01 us -> none  [local(): jnp.einsum('ine,ieb->inb', own_top[None] * weights[:, None, None], couple...]
    pallas_call x1 -> x2, Pallas kernels: 18.2 us -> 22.6 us  [the longest x1 14.1 us: top_solve(): pl.pallas_call(lambda *refs: top_kernel(units, *refs), out_shape=jax.Shap...]
    all_to_all x0 -> x1, starting transfers between devices: none -> 4.26 us  [local(): lax.all_to_all(jnp.broadcast_to(unit[None], (zs,) + unit.shape), 'z', 0,...]
    all_gather x1, blocking collectives: 22.5 us -> 19.1 us  [local(): updates = lax.all_gather(update, ROW, axis=0)]
  transfers between devices with their start and end apart: 11 -> 12, of which waited for: 7 -> 9; matrix products, arithmetic and copies ran while one was open for 5% -> 6% of each run, Pallas kernels for 0% -> 0%
where the time goes in v2:
time: 200 us; the launch traced here: 199 us
  waiting for transfers between devices  57.3 us (29%)
  blocking collectives  50.4 us (25%)
  starting transfers between devices  35.3 us (18%)
  Pallas kernels  22.6 us (11%)
  between operations  14.2 us (7%)
  matrix products  9.15 us (5%)
  other arithmetic  5.09 us (3%)
  local copies, waits for them, and re-layouts  4.83 us (2%)
    all_to_all x1, blocking collectives, local(): lax.all_to_all(jnp.broadcast_to(leaf_shared[None], (zs,) + leaf_forward.s...  31.4 us
    all_to_all x1, waiting for transfers between devices, local(): spread = lax.all_to_all(pair, 'z', 0, 0, tiled=True)  27.9 us
    all_gather x1, blocking collectives, local(): updates = lax.all_gather(update, ROW, axis=0)  19.1 us
    all_to_all x1, waiting for transfers between devices, local(): lax.all_to_all(jnp.broadcast_to(unit[None], (zs,) + unit.shape), 'z', 0,...  16.5 us
    pallas_call x1, Pallas kernels, top_solve(): pl.pallas_call(lambda *refs: top_kernel(units, *refs), out_shape=jax.Shap...  14.1 us
    ppermute x1, starting transfers between devices, local(): moved = lax.ppermute(block[half:], ('sub', 'z', 'core', 'col'), pairs)  13.5 us
    ppermute x6, starting transfers between devices, sum_over(): lax.ppermute(value, axis, [(i, (i + k) % size) for i in range(size)])  10.2 us
    pallas_call x1, Pallas kernels, back_products(): pl.pallas_call(back_kernel, out_shape=(out, out), grid_spec=pltpu.Prefetc...  8.46 us
  transfers between devices with their start and end apart: 12, of which 9 were waited for; matrix products, arithmetic and copies ran while one was open for 6% of the time, Pallas kernels for 0%

profile of v2, /device:TPU:1, one launch (start us, length us, event | category | flops | bytes accessed | tf_op | source)
XLA Modules:
  0.0 198.9 jit_solution(5664425885966551585)
XLA Ops:
  7.2 0.9 dynamic-slice_bitcast_fusion
  8.1 13.5 %collective-permute-start = (bf16[128,256]{1,0:T(8,128)(2,1)S(1)}, bf16[128,256]{1,0:T(8,128)(2,1)S(1)}, u32[]{:S(2)}, u32[]{:S(2)}) collective-permute-start(bf16[128,256]{1,0:T(8,128)(2,1)S(1)} %dynamic-slice_bitcast_fusion), channel_id=1, source_target_pairs={{4,251},{8,247},{12,243},{16,239},{20,235},{21,234},{24,231},{25,2... | collective-permute-start | bytes 196616 | tf_op jit(solution)/shard_map/ppermute | solution.py:151
  21.6 1.3 collective-permute-done
  24.6 4.3 %all-to-all-start = ((bf16[8,128,256]{2,1,0:T(8,128)(2,1)}), bf16[8,128,256]{2,1,0:T(8,128)(2,1)S(1)}, u32[]{:S(2)}, u32[]{:S(2)}) async-start(bf16[8,128,256]{2,1,0:T(8,128)(2,1)} %broadcast_in_dim.35), calls=%async_computation | async-start | bytes 1048576 | tf_op jit(solution)/shard_map/all_to_all | solution.py:153
  28.9 1.3 fusion
  30.3 16.5 %all-to-all-done = bf16[8,128,256]{2,1,0:T(8,128)(2,1)S(1)} async-done(((bf16[8,128,256]{2,1,0:T(8,128)(2,1)}), bf16[8,128,256]{2,1,0:T(8,128)(2,1)S(1)}, u32[]{:S(2)}, u32[]{:S(2)}) %all-to-all-start) | async-done | bytes 524320 | tf_op jit(solution)/shard_map/all_to_all | solution.py:153
  47.8 31.4 %all_to_all.15 = bf16[8,4,64,256]{3,2,1,0:T(8,128)(2,1)S(1)} all-to-all(bf16[8,4,64,256]{3,2,1,0:T(8,128)(2,1)S(1)} %broadcast_in_dim.36), channel_id=1, replica_groups=mesh['sub'=4,'z'=8,'core'=2,'col'=4] {'z'}, dimensions={0} | all-to-all | bytes 2097152 | tf_op jit(solution)/shard_map/all_to_all | solution.py:169
  79.9 2.3 %collective-permute-done.1 = bf16[8,4,64,256]{3,2,1,0:T(8,128)(2,1)S(1)} collective-permute-done((bf16[8,4,64,256]{3,2,1,0:T(8,128)(2,1)S(1)}, bf16[8,4,64,256]{3,2,1,0:T(8,128)(2,1)S(1)}, u32[]{:S(2)}, u32[]{:S(2)}) %collective-permute-start.1) | collective-permute-done | bytes 1048608 | tf_op jit(solution)/shard_map/ppermute | solution.py:173
  82.9 7.0 %fusion.2 = bf16[64,256]{1,0:T(8,128)(2,1)S(1)} fusion(bf16[64,64,256]{2,1,0:T(8,128)(2,1)S(1)} %bitcast_multiply_fusion, bf16[1,1,64,1,256,256]{5,4,3,2,1,0:T(8,128)(2,1)} %param.9), kind=kOutput, calls=%fused_computation.10 | convolution fusion | flops 536887296 | bytes 10518528 | tf_op jit(solution)/shard_map/inb,ieb->ne/dot_general | solution.py:178
  90.1 2.7 %collective-permute-start.4 = (bf16[64,256]{1,0:T(8,128)(2,1)S(1)}, bf16[64,256]{1,0:T(8,128)(2,1)S(1)}, u32[]{:S(2)}, u32[]{:S(2)}) collective-permute-start(bf16[64,256]{1,0:T(8,128)(2,1)S(1)} %fusion.2), channel_id=1, source_target_pairs={{0,192},{64,0},{128,64},{192,128},{1,193},{65,1},{129,65},{193,129... | collective-permute-start | bytes 98312 | tf_op jit(solution)/shard_map/ppermute | solution.py:119
  92.9 2.5 %collective-permute-done.2 = bf16[64,256]{1,0:T(8,128)(2,1)S(1)} collective-permute-done((bf16[64,256]{1,0:T(8,128)(2,1)S(1)}, bf16[64,256]{1,0:T(8,128)(2,1)S(1)}, u32[]{:S(2)}, u32[]{:S(2)}) %collective-permute-start.2) | collective-permute-done | bytes 32800 | tf_op jit(solution)/shard_map/ppermute | solution.py:119
  96.0 3.7 %collective-permute-start.5 = (bf16[64,256]{1,0:T(8,128)(2,1)S(1)}, bf16[64,256]{1,0:T(8,128)(2,1)S(1)}, u32[]{:S(2)}, u32[]{:S(2)}) collective-permute-start(bf16[64,256]{1,0:T(8,128)(2,1)S(1)} %add_convert_fusion.2), channel_id=1, source_target_pairs={{0,2},{1,3},{2,0},{3,1},{4,6},{5,7},{6,4},{7,5},{8,10},{9,11},{10,... | collective-permute-start | bytes 98312 | tf_op jit(solution)/shard_map/ppermute | solution.py:119
  99.8 3.6 %collective-permute-start.6 = (bf16[64,256]{1,0:T(8,128)(2,1)S(1)}, bf16[64,256]{1,0:T(8,128)(2,1)S(1)}, u32[]{:S(2)}, u32[]{:S(2)}) collective-permute-start(bf16[64,256]{1,0:T(8,128)(2,1)S(1)} %add_convert_fusion.2), channel_id=1, source_target_pairs={{0,1},{1,2},{2,3},{3,0},{4,5},{5,6},{6,7},{7,4},{8,9},{9,10},{10,1... | collective-permute-start | bytes 98312 | tf_op jit(solution)/shard_map/ppermute | solution.py:119
  103.9 1.3 collective-permute-done.6
  105.3 2.2 %collective-permute-done.7 = bf16[64,256]{1,0:T(8,128)(2,1)S(1)} collective-permute-done((bf16[64,256]{1,0:T(8,128)(2,1)S(1)}, bf16[64,256]{1,0:T(8,128)(2,1)S(1)}, u32[]{:S(2)}, u32[]{:S(2)}) %collective-permute-start.7) | collective-permute-done | bytes 32800 | tf_op jit(solution)/shard_map/ppermute | solution.py:119
  107.5 19.1 %all-gather = bf16[1024,256]{1,0:T(8,128)(2,1)S(1)} all-gather(bf16[64,256]{1,0:T(8,128)(2,1)S(1)} %add_convert_fusion.1), channel_id=2, replica_groups=mesh['sub'=4,'z'=8,'core'=2,'col'=4] {'z','core'}, dimensions={0}, use_global_device_ids=true | all-gather | bytes 557056 | tf_op jit(solution)/shard_map/all_gather | solution.py:183
  126.5 14.1 %top_solve.1.x_ref = bf16[16,64,256]{2,1,0:T(8,128)(2,1)S(1)} custom-call(bf16[16,64,256]{2,1,0:T(8,128)(2,1)S(1)} %copy-done.2, bf16[16,64,256]{2,1,0:T(8,128)(2,1)S(1)} %bitcast.40, bf16[16,256,256]{2,1,0:T(8,128)(2,1)S(1)} %broadcast_select_fusion.refs_2_, bf16[256,128,256]{2,1,0:T(8,128)(2,1)} %all-gather.3.cloned.1.call-done.refs_3_), custom_call_target="tpu_custom_call" | custom-call | tf_op jit(solution)/shard_map/top_solve/pallas_call | solution.py:67
  141.5 8.5 %back_products.1 = (bf16[8,4,64,256]{3,2,1,0:T(8,128)(2,1)}, bf16[8,4,64,256]{3,2,1,0:T(8,128)(2,1)}) custom-call(s32[2]{0:T(128)} %pad_add_fusion.where_ref, s32[64]{0:T(128)} %bitcast.42, bf16[16,64,256]{2,1,0:T(8,128)(2,1)} %copy-done.1, bf16[64,256,256]{2,1,0:T(8,128)(2,1)} %bitcast.41), custom_call_target="tpu_custom_call" | custom-call | tf_op jit(solution)/shard_map/back_products/pallas_call | solution.py:100
  150.1 2.7 %collective-permute-done.8 = bf16[8,4,64,256]{3,2,1,0:T(8,128)(2,1)S(1)} collective-permute-done((bf16[8,4,64,256]{3,2,1,0:T(8,128)(2,1)}, bf16[8,4,64,256]{3,2,1,0:T(8,128)(2,1)S(1)}, u32[]{:S(2)}, u32[]{:S(2)}) %collective-permute-start.8) | collective-permute-done | bytes 1048608 | tf_op jit(solution)/shard_map/ppermute | solution.py:191
  152.8 2.6 %add_convert_fusion = bf16[8,4,64,256]{3,2,1,0:T(8,128)(2,1)} fusion(bf16[8,4,64,256]{3,2,1,0:T(8,128)(2,1)S(1)} %collective-permute-done.8, bf16[8,4,64,256]{3,2,1,0:T(8,128)(2,1)} %get-tuple-element.8), kind=kLoop, calls=%fused_computation.3 | loop fusion | flops 2097152 | bytes 3145728 | tf_op jit(solution)/shard_map/convert_element_type | solution.py:192
  155.4 6.4 %all-to-all-start.2 = ((bf16[8,4,64,256]{3,2,1,0:T(8,128)(2,1)}), bf16[8,4,64,256]{3,2,1,0:T(8,128)(2,1)S(1)}, u32[]{:S(2)}, u32[]{:S(2)}) async-start(bf16[8,4,64,256]{3,2,1,0:T(8,128)(2,1)} %add_convert_fusion), calls=%async_computation.2 | async-start | bytes 2097152 | tf_op jit(solution)/shard_map/all_to_all | solution.py:193
  161.8 1.4 constant_dynamic-slice_fusion
  163.1 27.9 %all-to-all-done.2 = bf16[8,4,64,256]{3,2,1,0:T(8,128)(2,1)S(1)} async-done(((bf16[8,4,64,256]{3,2,1,0:T(8,128)(2,1)}), bf16[8,4,64,256]{3,2,1,0:T(8,128)(2,1)S(1)}, u32[]{:S(2)}, u32[]{:S(2)}) %all-to-all-start.2) | async-done | bytes 1048608 | tf_op jit(solution)/shard_map/all_to_all | solution.py:193
  191.1 0.9 fusion.1
  (38 shorter events, 6.8 us)
Async XLA Ops:
  7.2 21.8 %copy-start = (bf16[1,4,1,64,256]{4,3,2,1,0:T(8,128)(2,1)S(1)}, bf16[1,4,1,64,256]{4,3,2,1,0:T(8,128)(2,1)}, u32[]{:S(2)}) copy-start(bf16[1,4,1,64,256]{4,3,2,1,0:T(8,128)(2,1)} %param.7) | copy-start | bytes 393220
  8.1 14.8 %collective-permute-start = (bf16[128,256]{1,0:T(8,128)(2,1)S(1)}, bf16[128,256]{1,0:T(8,128)(2,1)S(1)}, u32[]{:S(2)}, u32[]{:S(2)}) collective-permute-start(bf16[128,256]{1,0:T(8,128)(2,1)S(1)} %dynamic-slice_bitcast_fusion), channel_id=1, source_target_pairs={{4,251},{8,247},{12,243},{16,239},{20,235},{21,234},{24,231},{25,2... | collective-permute-start | bytes 196616 | tf_op jit(solution)/shard_map/ppermute | solution.py:151
  24.6 22.2 %all-to-all-start = ((bf16[8,128,256]{2,1,0:T(8,128)(2,1)}), bf16[8,128,256]{2,1,0:T(8,128)(2,1)S(1)}, u32[]{:S(2)}, u32[]{:S(2)}) async-start(bf16[8,128,256]{2,1,0:T(8,128)(2,1)} %broadcast_in_dim.35), calls=%async_computation | async-start | bytes 1048576 | tf_op jit(solution)/shard_map/all_to_all | solution.py:153
  28.8 97.7 %all-gather.3.cloned.1.call-start = ((), (), s32[]{:S(2)}) async-start(), calls=%async_computation.3 | async-start | bytes 17301504 | tf_op jit(solution)/shard_map/all_gather | solution.py:168
  30.3 49.6 %copy-start.5 = (s32[1,1,64,1]{2,3,1,0:T(1,128)S(1)}, s32[1,1,64,1]{2,3,1,0:T(1,128)}, u32[]{:S(2)}) copy-start(s32[1,1,64,1]{2,3,1,0:T(1,128)} %param.10) | copy-start | bytes 772
  46.8 0.8 copy-start.4
  79.1 3.0 %collective-permute-start.1 = (bf16[8,4,64,256]{3,2,1,0:T(8,128)(2,1)S(1)}, bf16[8,4,64,256]{3,2,1,0:T(8,128)(2,1)S(1)}, u32[]{:S(2)}, u32[]{:S(2)}) collective-permute-start(bf16[8,4,64,256]{3,2,1,0:T(8,128)(2,1)S(1)} %all_to_all.15), channel_id=1, source_target_pairs={{0,4},{4,0},{1,5},{5,1},{2,6},{6,2},{3,7},{7,3},{8,12},{12,8},{9,1... | collective-permute-start | bytes 3145736 | tf_op jit(solution)/shard_map/ppermute | solution.py:173
  82.9 9.9 %copy-start.3 = (bf16[16,256,256]{2,1,0:T(8,128)(2,1)S(1)}, bf16[16,256,256]{2,1,0:T(8,128)(2,1)}, u32[]{:S(2)}) copy-start(bf16[16,256,256]{2,1,0:T(8,128)(2,1)} %param.12) | copy-start | bytes 6291460
  89.9 36.6 %copy-start.2 = (bf16[16,64,256]{2,1,0:T(8,128)(2,1)S(1)}, bf16[16,64,256]{2,1,0:T(8,128)(2,1)}, u32[]{:S(2)}) copy-start(bf16[16,64,256]{2,1,0:T(8,128)(2,1)} %refs_0_.1) | copy-start | bytes 1572868
  89.9 5.5 %collective-permute-start.2 = (bf16[64,256]{1,0:T(8,128)(2,1)S(1)}, bf16[64,256]{1,0:T(8,128)(2,1)S(1)}, u32[]{:S(2)}, u32[]{:S(2)}) collective-permute-start(bf16[64,256]{1,0:T(8,128)(2,1)S(1)} %fusion.2), channel_id=1, source_target_pairs={{0,128},{64,192},{128,0},{192,64},{1,129},{65,193},{129,1},{193,65... | collective-permute-start | bytes 98312 | tf_op jit(solution)/shard_map/ppermute | solution.py:119
  90.0 6.0 %collective-permute-start.3 = (bf16[64,256]{1,0:T(8,128)(2,1)S(1)}, bf16[64,256]{1,0:T(8,128)(2,1)S(1)}, u32[]{:S(2)}, u32[]{:S(2)}) collective-permute-start(bf16[64,256]{1,0:T(8,128)(2,1)S(1)} %fusion.2), channel_id=1, source_target_pairs={{0,64},{64,128},{128,192},{192,0},{1,65},{65,129},{129,193},{193,1... | collective-permute-start | bytes 98312 | tf_op jit(solution)/shard_map/ppermute | solution.py:119
  90.1 5.9 %collective-permute-start.4 = (bf16[64,256]{1,0:T(8,128)(2,1)S(1)}, bf16[64,256]{1,0:T(8,128)(2,1)S(1)}, u32[]{:S(2)}, u32[]{:S(2)}) collective-permute-start(bf16[64,256]{1,0:T(8,128)(2,1)S(1)} %fusion.2), channel_id=1, source_target_pairs={{0,192},{64,0},{128,64},{192,128},{1,193},{65,1},{129,65},{193,129... | collective-permute-start | bytes 98312 | tf_op jit(solution)/shard_map/ppermute | solution.py:119
  96.0 7.9 %collective-permute-start.5 = (bf16[64,256]{1,0:T(8,128)(2,1)S(1)}, bf16[64,256]{1,0:T(8,128)(2,1)S(1)}, u32[]{:S(2)}, u32[]{:S(2)}) collective-permute-start(bf16[64,256]{1,0:T(8,128)(2,1)S(1)} %add_convert_fusion.2), channel_id=1, source_target_pairs={{0,2},{1,3},{2,0},{3,1},{4,6},{5,7},{6,4},{7,5},{8,10},{9,11},{10,... | collective-permute-start | bytes 98312 | tf_op jit(solution)/shard_map/ppermute | solution.py:119
  99.8 5.5 %collective-permute-start.6 = (bf16[64,256]{1,0:T(8,128)(2,1)S(1)}, bf16[64,256]{1,0:T(8,128)(2,1)S(1)}, u32[]{:S(2)}, u32[]{:S(2)}) collective-permute-start(bf16[64,256]{1,0:T(8,128)(2,1)S(1)} %add_convert_fusion.2), channel_id=1, source_target_pairs={{0,1},{1,2},{2,3},{3,0},{4,5},{5,6},{6,7},{7,4},{8,9},{9,10},{10,1... | collective-permute-start | bytes 98312 | tf_op jit(solution)/shard_map/ppermute | solution.py:119
  103.4 4.1 %collective-permute-start.7 = (bf16[64,256]{1,0:T(8,128)(2,1)S(1)}, bf16[64,256]{1,0:T(8,128)(2,1)S(1)}, u32[]{:S(2)}, u32[]{:S(2)}) collective-permute-start(bf16[64,256]{1,0:T(8,128)(2,1)S(1)} %add_convert_fusion.2), channel_id=1, source_target_pairs={{0,3},{1,0},{2,1},{3,2},{4,7},{5,4},{6,5},{7,6},{8,11},{9,8},{10,9... | collective-permute-start | bytes 98312 | tf_op jit(solution)/shard_map/ppermute | solution.py:119
  140.7 0.8 copy-start.1
  149.9 2.9 %collective-permute-start.8 = (bf16[8,4,64,256]{3,2,1,0:T(8,128)(2,1)}, bf16[8,4,64,256]{3,2,1,0:T(8,128)(2,1)S(1)}, u32[]{:S(2)}, u32[]{:S(2)}) collective-permute-start(bf16[8,4,64,256]{3,2,1,0:T(8,128)(2,1)} %get-tuple-element.9), channel_id=1, source_target_pairs={{0,4},{4,0},{1,5},{5,1},{2,6},{6,2},{3,7},{7,3},{8,12},{12,8},{9,1... | collective-permute-start | bytes 3145736 | tf_op jit(solution)/shard_map/ppermute | solution.py:191
  155.3 35.8 %copy-start.6 = (bf16[1,4,1,256,256]{4,3,2,1,0:T(8,128)(2,1)S(1)}, bf16[1,4,1,256,256]{4,3,2,1,0:T(8,128)(2,1)}, u32[]{:S(2)}) copy-start(bf16[1,4,1,256,256]{4,3,2,1,0:T(8,128)(2,1)} %param.8) | copy-start | bytes 1572868
  155.4 35.6 %all-to-all-start.2 = ((bf16[8,4,64,256]{3,2,1,0:T(8,128)(2,1)}), bf16[8,4,64,256]{3,2,1,0:T(8,128)(2,1)S(1)}, u32[]{:S(2)}, u32[]{:S(2)}) async-start(bf16[8,4,64,256]{3,2,1,0:T(8,128)(2,1)} %add_convert_fusion), calls=%async_computation.2 | async-start | bytes 2097152 | tf_op jit(solution)/shard_map/all_to_all | solution.py:193
Sparse Core Ops, SparseCore 0:
  47.8 78.2 all-gather.2

commit v3 on v2

--- a/solution.py
+++ b/solution.py
@@ -17,9 +17,13 @@
     return a * (a - 1) // 2
 
 
-def top_kernel(units, r_ref, u_ref, g_ref, f_hbm, x_ref, zs, fac, sems):
+def top_kernel(
+    units, at_ref, w_ref, r_ref, u_ref, g_ref, f_hbm, c_hbm,
+    top_ref, mine_ref, other_ref, zs, xs, fac, coup, sems, coup_sem,
+):
     count = r_ref.shape[0]
     half = f_hbm.shape[1]
+    chips, leaves = mine_ref.shape[:2]
 
     def dot(a, b, dims):
         return lax.dot_general(a, b, dims, preferred_element_type=F32)
@@ -38,6 +42,8 @@
                     fac.at[first_block(a) + b, pl.ds(part * half, half)],
                     sems.at[a],
                 ).start()
+    coupling = pltpu.make_async_copy(c_hbm, coup, coup_sem)
+    coupling.start()
 
     summed = rhs(0)
     for k in range(count):
@@ -53,64 +59,47 @@
     summed = zs[count - 1].astype(F32)
     for k in reversed(range(count)):
         x = dot(summed.astype(BF), g_ref[k], NN).astype(BF)
-        x_ref[k] = x
+        xs[k] = x
         if k > 0:
             later = zs[k - 1].astype(F32)
             for a in range(count - 1, k, -1):
-                later -= dot(x_ref[a], block(a, k - 1), NN)
+                later -= dot(xs[a], block(a, k - 1), NN)
             summed = later - dot(x, block(k, k - 1), NN)
 
-
-def top_solve(units, rhs, updates, inverse, factor):
+    own = xs[at_ref[0]]
+    top_ref[...] = own
+    core = at_ref[1]
+    coupling.wait()
+    for out, part in ((other_ref, 1 - core), (mine_ref, core)):
+        for chip in range(chips):
+            for leaf in range(leaves):
+                at = (2 * chip + part) * leaves + leaf
+                weight = w_ref[at].astype(F32)
+                out[chip, leaf] = (dot(own, coup[at], NN) * weight).astype(BF)
+
+
+def top_solve(units, at, pattern, rhs, updates, inverse, factor, coupled, chips, leaves):
     whole = pl.BlockSpec(memory_space=pltpu.VMEM)
+    scalars = pl.BlockSpec(memory_space=pltpu.SMEM)
+    placed = pl.BlockSpec(memory_space=pltpu.HBM)
     count, nrhs, size = rhs.shape
+    part = jax.ShapeDtypeStruct((chips, leaves, nrhs, size), BF)
     return pl.pallas_call(
         lambda *refs: top_kernel(units, *refs),
-        out_shape=jax.ShapeDtypeStruct(rhs.shape, BF),
-        in_specs=[whole] * 3 + [pl.BlockSpec(memory_space=pl.ANY)],
-        out_specs=whole,
+        out_shape=(jax.ShapeDtypeStruct((nrhs, size), BF), part, part),
+        in_specs=[scalars] * 2 + [whole] * 3 + [placed] * 2,
+        out_specs=(whole,) * 3,
         scratch_shapes=[
             pltpu.VMEM(rhs.shape, BF),
+            pltpu.VMEM(rhs.shape, BF),
             pltpu.VMEM((first_block(count), size, size), BF),
+            pltpu.VMEM(coupled.shape, BF),
             pltpu.SemaphoreType.DMA((count,)),
+            pltpu.SemaphoreType.DMA,
         ],
         compiler_params=pltpu.CompilerParams(vmem_limit_bytes=40 << 20),
         name="top_solve",
-    )(rhs, updates, inverse, factor)
-
-
-def back_kernel(where_ref, w_ref, x_ref, c_ref, mine_ref, other_ref):
-    z = pl.program_id(0)
-    core = where_ref[1]
-    leaves = mine_ref.shape[0]
-    for out, part in ((other_ref, 1 - core), (mine_ref, core)):
-        for leaf in range(leaves):
-            at = part * leaves + leaf
-            weight = w_ref[z * 2 * leaves + at].astype(F32)
-            value = lax.dot_general(
-                x_ref[...], c_ref[at], NN, preferred_element_type=F32
-            )
-            out[leaf] = (value * weight).astype(BF)
-
-
-def back_products(solution, coupled, pattern, row, core, zs, leaves):
-    _, nrhs, size = solution.shape
-    spec = pl.BlockSpec((None, leaves, nrhs, size), lambda z, *_: (z, 0, 0, 0))
-    out = jax.ShapeDtypeStruct((zs, leaves, nrhs, size), BF)
-    return pl.pallas_call(
-        back_kernel,
-        out_shape=(out, out),
-        grid_spec=pltpu.PrefetchScalarGridSpec(
-            num_scalar_prefetch=2,
-            grid=(zs,),
-            in_specs=[
-                pl.BlockSpec((None, nrhs, size), lambda z, at, w: (at[0], 0, 0)),
-                pl.BlockSpec((2 * leaves, size, size), lambda z, *_: (z, 0, 0)),
-            ],
-            out_specs=(spec, spec),
-        ),
-        name="back_products",
-    )(jnp.stack([row, core]), pattern, solution, coupled)
+    )(at, pattern, rhs, updates, inverse, factor, coupled)
 
 
 def sum_over(value, axis, size):
@@ -149,10 +138,13 @@
             if r > subs * c + s:
                 pairs.append((i, subs * rows * cols - 1 - i))
         moved = lax.ppermute(block[half:], ("sub", "z", "core", "col"), pairs)
-        unit = jnp.where(row > column, block[:half], moved)
-        ring = lax.all_to_all(
-            jnp.broadcast_to(unit[None], (zs,) + unit.shape), "z", 0, 0, tiled=True
-        )
+        eight = (zs,) + moved.shape
+        unit = jnp.where(
+            row > column,
+            jnp.broadcast_to(block[None, :half], eight),
+            jnp.broadcast_to(moved[None], eight),
+        )
+        ring = lax.all_to_all(unit, "z", 0, 0, tiled=True)
 
         def units(a, b):
             c, s = divmod(b, subs)
@@ -182,11 +174,9 @@
         update = sum_over(sum_over(partial, "sub", subs), "col", cols).astype(BF)
         updates = lax.all_gather(update, ROW, axis=0)
 
-        solution = top_solve(units, top_rhs, updates, top_tri, factor)
-        own_top = lax.dynamic_index_in_dim(solution, row, 0, keepdims=False)
-
-        mine, other = back_products(
-            solution, coupled, pattern[0, 0, :, 0], row, core, zs, leaves
+        own_top, mine, other = top_solve(
+            units, jnp.stack([row, core]), pattern[0, 0, :, 0], top_rhs, updates,
+            top_tri, factor, coupled, zs, leaves,
         )
         other = lax.ppermute(other, "core", SWAP)
         pair = (mine.astype(F32) + other.astype(F32)).astype(BF)

time: 200 us -> 193 us (0.965)
  blocking collectives: 50.4 us -> 84.3 us
  waiting for transfers between devices: 57.3 us -> 31.7 us
  starting transfers between devices: 35.3 us -> 28 us
  Pallas kernels: 22.6 us -> 16.9 us
  other arithmetic: 5.09 us -> 2.42 us
    all_to_all x0 -> x1, blocking collectives: none -> 33.5 us  [local(): spread = lax.all_to_all(pair, 'z', 0, 0, tiled=True)]
    all_to_all x2 -> x1, waiting for transfers between devices: 44.4 us -> 16.5 us  [local(): ring = lax.all_to_all(unit, 'z', 0, 0, tiled=True)]
    all_to_all x2 -> x1, starting transfers between devices: 10.7 us -> 4.26 us  [local(): ring = lax.all_to_all(unit, 'z', 0, 0, tiled=True)]
    pallas_call x2 -> x1, Pallas kernels: 22.6 us -> 16.9 us  [top_solve(): pl.pallas_call(lambda *refs: top_kernel(units, *refs), out_shape=(jax.Sha...]
    unnamed x14, local copies, waits for them, and re-layouts: 1.62 us -> 4.21 us
    ppermute x6, waiting for transfers between devices: 6.58 us -> 9.08 us  [sum_over(): lax.ppermute(value, axis, [(i, (i + k) % size) for i in range(size)])]
    convert_element_type x1, other arithmetic: 2.56 us -> 0.37 us  [local(): pair = (mine.astype(F32) + other.astype(F32)).astype(BF)]
  transfers between devices with their start and end apart: 12 -> 11, of which waited for: 9 -> 9; matrix products, arithmetic and copies ran while one was open for 6% -> 5% of each run, Pallas kernels for 0% -> 0%
where the time goes in v3:
time: 193 us
  blocking collectives  84.3 us (44%)
  waiting for transfers between devices  31.7 us (16%)
  starting transfers between devices  28 us (15%)
  Pallas kernels  16.9 us (9%)
  between operations  14.2 us (7%)
  matrix products  9.16 us (5%)
  local copies, waits for them, and re-layouts  6.03 us (3%)
  other arithmetic  2.42 us (1%)
    all_to_all x1, blocking collectives, local(): spread = lax.all_to_all(pair, 'z', 0, 0, tiled=True)  33.5 us
    all_to_all x1, blocking collectives, local(): lax.all_to_all(jnp.broadcast_to(leaf_shared[None], (zs,) + leaf_forward.s...  31.4 us
    all_gather x1, blocking collectives, local(): updates = lax.all_gather(update, ROW, axis=0)  19.4 us
    pallas_call x1, Pallas kernels, top_solve(): pl.pallas_call(lambda *refs: top_kernel(units, *refs), out_shape=(jax.Sha...  16.9 us
    all_to_all x1, waiting for transfers between devices, local(): ring = lax.all_to_all(unit, 'z', 0, 0, tiled=True)  16.5 us
    ppermute x1, starting transfers between devices, local(): moved = lax.ppermute(block[half:], ('sub', 'z', 'core', 'col'), pairs)  13.5 us
    ppermute x6, starting transfers between devices, sum_over(): lax.ppermute(value, axis, [(i, (i + k) % size) for i in range(size)])  9.27 us
    ppermute x6, waiting for transfers between devices, sum_over(): lax.ppermute(value, axis, [(i, (i + k) % size) for i in range(size)])  9.08 us
  transfers between devices with their start and end apart: 11, of which 9 were waited for; matrix products, arithmetic and copies ran while one was open for 5% of the time, Pallas kernels for 0%

profile of v3, /device:TPU:1, one launch (start us, length us, event | category | flops | bytes accessed | tf_op | source)
XLA Modules:
  0.0 192.7 jit_solution(2839376329016353701)
XLA Ops:
  7.2 0.9 dynamic-slice_bitcast_fusion
  8.1 13.5 %collective-permute-start = (bf16[128,256]{1,0:T(8,128)(2,1)S(1)}, bf16[128,256]{1,0:T(8,128)(2,1)S(1)}, u32[]{:S(2)}, u32[]{:S(2)}) collective-permute-start(bf16[128,256]{1,0:T(8,128)(2,1)S(1)} %dynamic-slice_bitcast_fusion), channel_id=1, source_target_pairs={{4,251},{8,247},{12,243},{16,239},{20,235},{21,234},{24,231},{25,2... | collective-permute-start | bytes 196616 | tf_op jit(solution)/shard_map/ppermute | solution.py:140
  21.6 1.3 collective-permute-done
  22.9 0.8 fusion.6
  23.7 0.8 broadcast_in_dim.44
  24.6 4.3 %all-to-all-start = ((bf16[8,128,256]{2,1,0:T(8,128)(2,1)}), bf16[8,128,256]{2,1,0:T(8,128)(2,1)S(1)}, u32[]{:S(2)}, u32[]{:S(2)}) async-start(bf16[8,128,256]{2,1,0:T(8,128)(2,1)} %broadcast_in_dim.44), calls=%async_computation | async-start | bytes 1048576 | tf_op jit(solution)/shard_map/all_to_all | solution.py:147
  28.9 1.3 fusion
  30.3 16.5 %all-to-all-done = bf16[8,128,256]{2,1,0:T(8,128)(2,1)S(1)} async-done(((bf16[8,128,256]{2,1,0:T(8,128)(2,1)}), bf16[8,128,256]{2,1,0:T(8,128)(2,1)S(1)}, u32[]{:S(2)}, u32[]{:S(2)}) %all-to-all-start) | async-done | bytes 524320 | tf_op jit(solution)/shard_map/all_to_all | solution.py:147
  47.7 31.4 %all_to_all.15 = bf16[8,4,64,256]{3,2,1,0:T(8,128)(2,1)S(1)} all-to-all(bf16[8,4,64,256]{3,2,1,0:T(8,128)(2,1)S(1)} %broadcast_in_dim.45), channel_id=1, replica_groups=mesh['sub'=4,'z'=8,'core'=2,'col'=4] {'z'}, dimensions={0} | all-to-all | bytes 2097152 | tf_op jit(solution)/shard_map/all_to_all | solution.py:161
  79.8 2.3 %collective-permute-done.1 = bf16[8,4,64,256]{3,2,1,0:T(8,128)(2,1)S(1)} collective-permute-done((bf16[8,4,64,256]{3,2,1,0:T(8,128)(2,1)S(1)}, bf16[8,4,64,256]{3,2,1,0:T(8,128)(2,1)S(1)}, u32[]{:S(2)}, u32[]{:S(2)}) %collective-permute-start.1) | collective-permute-done | bytes 1048608 | tf_op jit(solution)/shard_map/ppermute | solution.py:165
  82.9 7.0 %fusion.2 = bf16[64,256]{1,0:T(8,128)(2,1)S(1)} fusion(bf16[64,64,256]{2,1,0:T(8,128)(2,1)S(1)} %bitcast_multiply_fusion, bf16[1,1,64,1,256,256]{5,4,3,2,1,0:T(8,128)(2,1)} %param.9), kind=kOutput, calls=%fused_computation.10 | convolution fusion | flops 536887296 | bytes 10518528 | tf_op jit(solution)/shard_map/inb,ieb->ne/dot_general | solution.py:170
  90.0 1.5 collective-permute-start.3
  91.6 2.4 %collective-permute-done.4 = bf16[64,256]{1,0:T(8,128)(2,1)S(1)} collective-permute-done((bf16[64,256]{1,0:T(8,128)(2,1)S(1)}, bf16[64,256]{1,0:T(8,128)(2,1)S(1)}, u32[]{:S(2)}, u32[]{:S(2)}) %collective-permute-start.4) | collective-permute-done | bytes 32800 | tf_op jit(solution)/shard_map/ppermute | solution.py:108
  94.0 1.3 collective-permute-done.3
  95.3 1.4 collective-permute-done.2
  96.7 6.5 %collective-permute-start.7 = (bf16[64,256]{1,0:T(8,128)(2,1)S(1)}, bf16[64,256]{1,0:T(8,128)(2,1)S(1)}, u32[]{:S(2)}, u32[]{:S(2)}) collective-permute-start(bf16[64,256]{1,0:T(8,128)(2,1)S(1)} %add_convert_fusion.2), channel_id=1, source_target_pairs={{0,3},{1,0},{2,1},{3,2},{4,7},{5,4},{6,5},{7,6},{8,11},{9,8},{10,9... | collective-permute-start | bytes 98312 | tf_op jit(solution)/shard_map/ppermute | solution.py:108
  103.2 1.3 collective-permute-start.5
  104.7 3.8 %collective-permute-done.6 = bf16[64,256]{1,0:T(8,128)(2,1)S(1)} collective-permute-done((bf16[64,256]{1,0:T(8,128)(2,1)S(1)}, bf16[64,256]{1,0:T(8,128)(2,1)S(1)}, u32[]{:S(2)}, u32[]{:S(2)}) %collective-permute-start.6) | collective-permute-done | bytes 32800 | tf_op jit(solution)/shard_map/ppermute | solution.py:108
  108.5 19.4 %all-gather = bf16[1024,256]{1,0:T(8,128)(2,1)S(1)} all-gather(bf16[64,256]{1,0:T(8,128)(2,1)S(1)} %add_convert_fusion.1), channel_id=2, replica_groups=mesh['sub'=4,'z'=8,'core'=2,'col'=4] {'z','core'}, dimensions={0}, use_global_device_ids=true | all-gather | bytes 557056 | tf_op jit(solution)/shard_map/all_gather | solution.py:175
  127.9 3.4 %copy-done.1 = bf16[1,1,64,1,256,256]{5,4,3,2,1,0:T(8,128)(2,1)S(1)} copy-done((bf16[1,1,64,1,256,256]{5,4,3,2,1,0:T(8,128)(2,1)S(1)}, bf16[1,1,64,1,256,256]{5,4,3,2,1,0:T(8,128)(2,1)}, u32[]{:S(2)}) %copy-start.1) | copy-done | bytes 8388632
  131.3 16.9 %top_solve.1 = (bf16[64,256]{1,0:T(8,128)(2,1)}, bf16[8,4,64,256]{3,2,1,0:T(8,128)(2,1)S(1)}, bf16[8,4,64,256]{3,2,1,0:T(8,128)(2,1)S(1)}) custom-call(s32[2]{0:T(128)S(1)} %pad_add_fusion.refs_0_, s32[64]{0:T(128)S(1)} %bitcast.43, bf16[16,64,256]{2,1,0:T(8,128)(2,1)S(1)} %copy-done.2, bf16[16,64,256]{2,1,0:T(8,128)(2,1)S(1)} %bitcast.42, ...), custom_call_target="tpu_custom_call" | custom-call | tf_op jit(solution)/shard_map/top_solve/pallas_call | solution.py:87
  148.4 2.5 %collective-permute-done.8 = bf16[8,4,64,256]{3,2,1,0:T(8,128)(2,1)S(1)} collective-permute-done((bf16[8,4,64,256]{3,2,1,0:T(8,128)(2,1)S(1)}, bf16[8,4,64,256]{3,2,1,0:T(8,128)(2,1)S(1)}, u32[]{:S(2)}, u32[]{:S(2)}) %collective-permute-start.8) | collective-permute-done | bytes 1048608 | tf_op jit(solution)/shard_map/ppermute | solution.py:181
  151.3 33.5 %all_to_all.16 = bf16[8,4,64,256]{3,2,1,0:T(8,128)(2,1)S(1)} all-to-all(bf16[8,4,64,256]{3,2,1,0:T(8,128)(2,1)S(1)} %add_convert_fusion), channel_id=1, replica_groups=mesh['sub'=4,'z'=8,'core'=2,'col'=4] {'z'}, dimensions={0} | all-to-all | bytes 2097152 | tf_op jit(solution)/shard_map/all_to_all | solution.py:183
  185.0 0.9 fusion.1
  (35 shorter events, 3.8 us)
Async XLA Ops:
  7.2 21.8 %copy-start = (bf16[1,4,1,64,256]{4,3,2,1,0:T(8,128)(2,1)S(1)}, bf16[1,4,1,64,256]{4,3,2,1,0:T(8,128)(2,1)}, u32[]{:S(2)}) copy-start(bf16[1,4,1,64,256]{4,3,2,1,0:T(8,128)(2,1)} %param.7) | copy-start | bytes 393220
  8.1 14.8 %collective-permute-start = (bf16[128,256]{1,0:T(8,128)(2,1)S(1)}, bf16[128,256]{1,0:T(8,128)(2,1)S(1)}, u32[]{:S(2)}, u32[]{:S(2)}) collective-permute-start(bf16[128,256]{1,0:T(8,128)(2,1)S(1)} %dynamic-slice_bitcast_fusion), channel_id=1, source_target_pairs={{4,251},{8,247},{12,243},{16,239},{20,235},{21,234},{24,231},{25,2... | collective-permute-start | bytes 196616 | tf_op jit(solution)/shard_map/ppermute | solution.py:140
  24.6 22.2 %all-to-all-start = ((bf16[8,128,256]{2,1,0:T(8,128)(2,1)}), bf16[8,128,256]{2,1,0:T(8,128)(2,1)S(1)}, u32[]{:S(2)}, u32[]{:S(2)}) async-start(bf16[8,128,256]{2,1,0:T(8,128)(2,1)} %broadcast_in_dim.44), calls=%async_computation | async-start | bytes 1048576 | tf_op jit(solution)/shard_map/all_to_all | solution.py:147
  28.8 99.1 %all-gather.3.cloned.1.call-start = ((), (), s32[]{:S(2)}) async-start(), calls=%async_computation.3 | async-start | bytes 17301504 | tf_op jit(solution)/shard_map/all_gather | solution.py:160
  30.2 49.6 %copy-start.3 = (s32[1,1,64,1]{2,3,1,0:T(1,128)S(1)}, s32[1,1,64,1]{2,3,1,0:T(1,128)}, u32[]{:S(2)}) copy-start(s32[1,1,64,1]{2,3,1,0:T(1,128)} %param.10) | copy-start | bytes 772
  46.8 0.8 copy-start.5
  79.1 3.0 %collective-permute-start.1 = (bf16[8,4,64,256]{3,2,1,0:T(8,128)(2,1)S(1)}, bf16[8,4,64,256]{3,2,1,0:T(8,128)(2,1)S(1)}, u32[]{:S(2)}, u32[]{:S(2)}) collective-permute-start(bf16[8,4,64,256]{3,2,1,0:T(8,128)(2,1)S(1)} %all_to_all.15), channel_id=1, source_target_pairs={{0,4},{4,0},{1,5},{5,1},{2,6},{6,2},{3,7},{7,3},{8,12},{12,8},{9,1... | collective-permute-start | bytes 3145736 | tf_op jit(solution)/shard_map/ppermute | solution.py:165
  82.9 8.5 %copy-start.4 = (bf16[16,256,256]{2,1,0:T(8,128)(2,1)S(1)}, bf16[16,256,256]{2,1,0:T(8,128)(2,1)}, u32[]{:S(2)}) copy-start(bf16[16,256,256]{2,1,0:T(8,128)(2,1)} %param.12) | copy-start | bytes 6291460
  89.9 38.1 %copy-start.2 = (bf16[16,64,256]{2,1,0:T(8,128)(2,1)S(1)}, bf16[16,64,256]{2,1,0:T(8,128)(2,1)}, u32[]{:S(2)}) copy-start(bf16[16,64,256]{2,1,0:T(8,128)(2,1)} %refs_2_.1) | copy-start | bytes 1572868
  89.9 4.1 %collective-permute-start.4 = (bf16[64,256]{1,0:T(8,128)(2,1)S(1)}, bf16[64,256]{1,0:T(8,128)(2,1)S(1)}, u32[]{:S(2)}, u32[]{:S(2)}) collective-permute-start(bf16[64,256]{1,0:T(8,128)(2,1)S(1)} %fusion.2), channel_id=1, source_target_pairs={{0,192},{64,0},{128,64},{192,128},{1,193},{65,1},{129,65},{193,129... | collective-permute-start | bytes 98312 | tf_op jit(solution)/shard_map/ppermute | solution.py:108
  90.0 5.3 %collective-permute-start.3 = (bf16[64,256]{1,0:T(8,128)(2,1)S(1)}, bf16[64,256]{1,0:T(8,128)(2,1)S(1)}, u32[]{:S(2)}, u32[]{:S(2)}) collective-permute-start(bf16[64,256]{1,0:T(8,128)(2,1)S(1)} %fusion.2), channel_id=1, source_target_pairs={{0,64},{64,128},{128,192},{192,0},{1,65},{65,129},{129,193},{193,1... | collective-permute-start | bytes 98312 | tf_op jit(solution)/shard_map/ppermute | solution.py:108
  91.4 5.3 %collective-permute-start.2 = (bf16[64,256]{1,0:T(8,128)(2,1)S(1)}, bf16[64,256]{1,0:T(8,128)(2,1)S(1)}, u32[]{:S(2)}, u32[]{:S(2)}) collective-permute-start(bf16[64,256]{1,0:T(8,128)(2,1)S(1)} %fusion.2), channel_id=1, source_target_pairs={{0,128},{64,192},{128,0},{192,64},{1,129},{65,193},{129,1},{193,65... | collective-permute-start | bytes 98312 | tf_op jit(solution)/shard_map/ppermute | solution.py:108
  96.7 8.0 %collective-permute-start.7 = (bf16[64,256]{1,0:T(8,128)(2,1)S(1)}, bf16[64,256]{1,0:T(8,128)(2,1)S(1)}, u32[]{:S(2)}, u32[]{:S(2)}) collective-permute-start(bf16[64,256]{1,0:T(8,128)(2,1)S(1)} %add_convert_fusion.2), channel_id=1, source_target_pairs={{0,3},{1,0},{2,1},{3,2},{4,7},{5,4},{6,5},{7,6},{8,11},{9,8},{10,9... | collective-permute-start | bytes 98312 | tf_op jit(solution)/shard_map/ppermute | solution.py:108
  103.2 5.3 %collective-permute-start.6 = (bf16[64,256]{1,0:T(8,128)(2,1)S(1)}, bf16[64,256]{1,0:T(8,128)(2,1)S(1)}, u32[]{:S(2)}, u32[]{:S(2)}) collective-permute-start(bf16[64,256]{1,0:T(8,128)(2,1)S(1)} %add_convert_fusion.2), channel_id=1, source_target_pairs={{0,1},{1,2},{2,3},{3,0},{4,5},{5,6},{6,7},{7,4},{8,9},{9,10},{10,1... | collective-permute-start | bytes 98312 | tf_op jit(solution)/shard_map/ppermute | solution.py:108
  103.2 5.3 %collective-permute-start.5 = (bf16[64,256]{1,0:T(8,128)(2,1)S(1)}, bf16[64,256]{1,0:T(8,128)(2,1)S(1)}, u32[]{:S(2)}, u32[]{:S(2)}) collective-permute-start(bf16[64,256]{1,0:T(8,128)(2,1)S(1)} %add_convert_fusion.2), channel_id=1, source_target_pairs={{0,2},{1,3},{2,0},{3,1},{4,6},{5,7},{6,4},{7,5},{8,10},{9,11},{10,... | collective-permute-start | bytes 98312 | tf_op jit(solution)/shard_map/ppermute | solution.py:108
  127.9 3.4 %copy-start.1 = (bf16[1,1,64,1,256,256]{5,4,3,2,1,0:T(8,128)(2,1)S(1)}, bf16[1,1,64,1,256,256]{5,4,3,2,1,0:T(8,128)(2,1)}, u32[]{:S(2)}) copy-start(bf16[1,1,64,1,256,256]{5,4,3,2,1,0:T(8,128)(2,1)} %param.9) | copy-start | bytes 25165828
  148.2 2.7 %collective-permute-start.8 = (bf16[8,4,64,256]{3,2,1,0:T(8,128)(2,1)S(1)}, bf16[8,4,64,256]{3,2,1,0:T(8,128)(2,1)S(1)}, u32[]{:S(2)}, u32[]{:S(2)}) collective-permute-start(bf16[8,4,64,256]{3,2,1,0:T(8,128)(2,1)S(1)} %get-tuple-element.10), channel_id=1, source_target_pairs={{0,4},{4,0},{1,5},{5,1},{2,6},{6,2},{3,7},{7,3},{8,12},{12,8},{9,1... | collective-permute-start | bytes 3145736 | tf_op jit(solution)/shard_map/ppermute | solution.py:181
  151.3 33.7 %copy-start.6 = (bf16[1,4,1,256,256]{4,3,2,1,0:T(8,128)(2,1)S(1)}, bf16[1,4,1,256,256]{4,3,2,1,0:T(8,128)(2,1)}, u32[]{:S(2)}) copy-start(bf16[1,4,1,256,256]{4,3,2,1,0:T(8,128)(2,1)} %param.8) | copy-start | bytes 1572868
Sparse Core Ops, SparseCore 0:
  47.7 78.2 all-gather.2

commit v4 on v3

--- a/solution.py
+++ b/solution.py
@@ -13,6 +13,67 @@
 NN = (((1,), (0,)), ((), ()))
 
 
+def hop(size):
+    return [
+        (2 * z + core, 2 * ((z + 1 - 2 * core) % size) + core)
+        for z in range(size)
+        for core in range(2)
+    ]
+
+
+def update_kernel(count, base_ref, w_ref, *refs):
+    parts, (c_hbm, out_ref, coup, sems) = refs[:-4], refs[-4:]
+    leaves = coup.shape[1]
+
+    def fetch(i):
+        return pltpu.make_async_copy(
+            c_hbm.at[pl.ds(base_ref[i], leaves)], coup.at[i], sems.at[i]
+        )
+
+    for i in range(count):
+        fetch(i).start()
+    total = None
+    i = 0
+    for part in parts:
+        groups = [part] if len(part.shape) == 3 else [part.at[0], part.at[1]]
+        for group in groups:
+            fetch(i).wait()
+            for leaf in range(leaves):
+                weight = w_ref[base_ref[i] + leaf].astype(F32)
+                term = weight * lax.dot_general(
+                    group[leaf], coup[i, leaf], NT, preferred_element_type=F32
+                )
+                total = term if total is None else total + term
+            i += 1
+    out_ref[...] = total
+
+
+def update_products(base, pattern, parts, coupled):
+    count = sum(1 if part.ndim == 3 else 2 for part in parts)
+    leaves, nrhs, size = parts[0].shape[-3:]
+    whole = pl.BlockSpec(memory_space=pltpu.VMEM)
+    scalars = pl.BlockSpec(memory_space=pltpu.SMEM)
+    return pl.pallas_call(
+        lambda *refs: update_kernel(count, *refs),
+        out_shape=jax.ShapeDtypeStruct((nrhs, size), F32),
+        in_specs=[scalars] * 2
+        + [whole] * len(parts)
+        + [pl.BlockSpec(memory_space=pltpu.HBM)],
+        out_specs=whole,
+        scratch_shapes=[
+            pltpu.VMEM((count, leaves, size, size), BF),
+            pltpu.SemaphoreType.DMA((count,)),
+        ],
+        compiler_params=pltpu.CompilerParams(vmem_limit_bytes=58 << 20),
+        cost_estimate=pl.CostEstimate(
+            flops=2 * count * leaves * nrhs * size * size,
+            bytes_accessed=2 * count * leaves * size * (size + nrhs),
+            transcendentals=0,
+        ),
+        name="update_products",
+    )(base, pattern, *parts, coupled)
+
+
 def first_block(a):
     return a * (a - 1) // 2
 
@@ -22,7 +83,7 @@
     top_ref, mine_ref, other_ref, zs, xs, fac, coup, sems, coup_sem,
 ):
     count = r_ref.shape[0]
-    half = f_hbm.shape[1]
+    half = f_hbm.shape[2]
     chips, leaves = mine_ref.shape[:2]
 
     def dot(a, b, dims):
@@ -36,9 +97,9 @@
 
     for a in range(1, count):
         for b in range(a):
-            for part, unit in enumerate(units(a, b)):
+            for part, (group, chip) in enumerate(units(a, b)):
                 pltpu.make_async_copy(
-                    f_hbm.at[unit],
+                    f_hbm.at[group, chip],
                     fac.at[first_block(a) + b, pl.ds(part * half, half)],
                     sems.at[a],
                 ).start()
@@ -78,7 +139,9 @@
                 out[chip, leaf] = (dot(own, coup[at], NN) * weight).astype(BF)
 
 
-def top_solve(units, at, pattern, rhs, updates, inverse, factor, coupled, chips, leaves):
+def top_solve(
+    units, at, pattern, rhs, updates, inverse, factor, coupled, chips, leaves
+):
     whole = pl.BlockSpec(memory_space=pltpu.VMEM)
     scalars = pl.BlockSpec(memory_space=pltpu.SMEM)
     placed = pl.BlockSpec(memory_space=pltpu.HBM)
@@ -97,7 +160,7 @@
             pltpu.SemaphoreType.DMA((count,)),
             pltpu.SemaphoreType.DMA,
         ],
-        compiler_params=pltpu.CompilerParams(vmem_limit_bytes=40 << 20),
+        compiler_params=pltpu.CompilerParams(vmem_limit_bytes=58 << 20),
         name="top_solve",
     )(at, pattern, rhs, updates, inverse, factor, coupled)
 
@@ -122,7 +185,6 @@
         own_rhs = leaf_rhs[0, :, 0]
         own_inverse = jnp.tril(leaf_inverse[0, :, 0])
         coupled = coupling[0, 0, :, 0]
-        weights = pattern[0, 0, :, 0].astype(BF)
         leaves, nrhs, size = own_rhs.shape
         rows = zs * cores
         assert top_factor.shape[1] == subs
@@ -148,34 +210,48 @@
 
         def units(a, b):
             c, s = divmod(b, subs)
-            at = ((s * cols + c) * cores + a % cores) * zs + a // cores
-            return at, subs * rows * cols - 1 - at
+            z, group_core = divmod(a, cores)
+            group = (s * cols + c) * cores + group_core
+            return (group, z), (subs * cols * cores - 1 - group, zs - 1 - z)
 
         top_tri = jnp.tril(top_inverse)
+        present = pattern[0, 0, :, 0]
 
         leaf_forward = jnp.einsum(
             "inb,idb->ind", own_rhs, own_inverse, preferred_element_type=F32
         ).astype(BF)
-        leaf_shared, ring = lax.optimization_barrier((leaf_forward, ring))
-        factor = lax.all_gather(ring, ("sub", "col", "core"), axis=0, tiled=True)
-        mine = lax.all_to_all(
-            jnp.broadcast_to(leaf_shared[None], (zs,) + leaf_forward.shape),
-            "z", 0, 0, tiled=True,
-        )
-        other = lax.ppermute(mine, "core", SWAP)
-        first = core == 0
-        forward = jnp.stack(
-            [jnp.where(first, mine, other), jnp.where(first, other, mine)], axis=1
-        ).reshape(rows * leaves, nrhs, size)
-        partial = jnp.einsum(
-            "inb,ieb->ne", forward * weights[:, None, None], coupled,
-            preferred_element_type=F32,
-        )
+        steps = hop(zs)
+        swapped = lax.ppermute(leaf_forward, "core", SWAP)
+        shard = jnp.stack([leaf_forward, swapped])
+        early, late = [leaf_forward, swapped], []
+        for step in range(1, zs // 2):
+            shard = lax.ppermute(shard, ROW, steps)
+            (late if step == zs // 2 - 1 else early).extend(
+                [shard, lax.ppermute(shard, "core", SWAP)]
+            )
+        last = lax.ppermute(shard[0], ROW, steps)
+        late.extend([last, lax.ppermute(last, "core", SWAP)])
+        away = jnp.array(
+            [0, 0]
+            + [d for k in range(1, zs // 2) for d in (-k, -k, k, k)]
+            + [zs // 2] * 2
+        )
+        flip = jnp.array([0, 1] + [0, 1, 1, 0] * (zs // 2 - 1) + [0, 1])
+        chip = (lax.axis_index("z") + (1 - 2 * core) * away + zs) % zs
+        part = jnp.where(flip == 1, 1 - core, core)
+        base = ((chip * cores + part) * leaves).astype(jnp.int32)
+        cut = sum(1 if part.ndim == 3 else 2 for part in early)
+
+        ring, _ = lax.optimization_barrier((ring, shard))
+        factor = lax.all_gather(ring, ("sub", "col", "core"), axis=0)
+
+        partial = update_products(base[:cut], present, early, coupled)
+        partial += update_products(base[cut:], present, late, coupled)
         update = sum_over(sum_over(partial, "sub", subs), "col", cols).astype(BF)
         updates = lax.all_gather(update, ROW, axis=0)
 
         own_top, mine, other = top_solve(
-            units, jnp.stack([row, core]), pattern[0, 0, :, 0], top_rhs, updates,
+            units, jnp.stack([row, core]), present, top_rhs, updates,
             top_tri, factor, coupled, zs, leaves,
         )
         other = lax.ppermute(other, "core", SWAP)

time: 193 us -> 211 us (1.093)
  blocking collectives: 84.3 us -> 55.3 us
  waiting for transfers between devices: 31.7 us -> 52.3 us
  starting transfers between devices: 28 us -> 45.7 us
  Pallas kernels: 16.9 us -> 29.5 us
  matrix products: 9.16 us -> 2.19 us
  other arithmetic: 2.42 us -> 5.72 us
    all_to_all x1 -> x0, blocking collectives: 31.4 us -> none  [local(): lax.all_to_all(jnp.broadcast_to(leaf_shared[None], (zs,) + leaf_forward.s...]
    all_gather x1, waiting for transfers between devices: 0.01 us -> 22.7 us  [local(): factor = lax.all_gather(ring, ('sub', 'col', 'core'), axis=0)]
    ppermute x1 -> x9, waiting for transfers between devices: 2.28 us -> 21.6 us  [the longest x3 21.6 us: local(): shard = lax.ppermute(shard, ROW, steps)]
    ppermute x1 -> x9, starting transfers between devices: 0.72 us -> 18.4 us  [the longest x3 6.15 us: local(): shard = lax.ppermute(shard, ROW, steps)]
    all_to_all x1, waiting for transfers between devices: 16.5 us -> 0.01 us  [local(): ring = lax.all_to_all(unit, 'z', 0, 0, tiled=True)]
    pallas_call x0 -> x2, Pallas kernels: none -> 10.6 us  [update_products(): pl.pallas_call(lambda *refs: update_kernel(count, *refs), out_shape=jax.S...]
    dot_general x1 -> x0, matrix products: 6.97 us -> none  [local(): jnp.einsum('inb,ieb->ne', forward * weights[:, None, None], coupled, pref...]
    ppermute x6, waiting for transfers between devices: 9.08 us -> 5.39 us  [sum_over(): lax.ppermute(value, axis, [(i, (i + k) % size) for i in range(size)])]
  transfers between devices with their start and end apart: 11 -> 19, of which waited for: 9 -> 10; matrix products, arithmetic and copies ran while one was open for 5% -> 3% of each run, Pallas kernels for 0% -> 5%
where the time goes in v4:
time: 211 us; the launch traced here: 210 us
  blocking collectives  55.3 us (26%)
  waiting for transfers between devices  52.3 us (25%)
  starting transfers between devices  45.7 us (22%)
  Pallas kernels  29.5 us (14%)
  between operations  14.4 us (7%)
  other arithmetic  5.72 us (3%)
  local copies, waits for them, and re-layouts  5.26 us (2%)
  matrix products  2.19 us (1%)
    all_to_all x1, blocking collectives, local(): spread = lax.all_to_all(pair, 'z', 0, 0, tiled=True)  35.4 us
    all_gather x1, waiting for transfers between devices, local(): factor = lax.all_gather(ring, ('sub', 'col', 'core'), axis=0)  22.7 us
    ppermute x3, waiting for transfers between devices, local(): shard = lax.ppermute(shard, ROW, steps)  21.6 us
    all_gather x1, blocking collectives, local(): updates = lax.all_gather(update, ROW, axis=0)  19.9 us
    pallas_call x1, Pallas kernels, top_solve(): pl.pallas_call(lambda *refs: top_kernel(units, *refs), out_shape=(jax.Sha...  19 us
    ppermute x1, starting transfers between devices, local(): moved = lax.ppermute(block[half:], ('sub', 'z', 'core', 'col'), pairs)  13.5 us
    pallas_call x2, Pallas kernels, update_products(): pl.pallas_call(lambda *refs: update_kernel(count, *refs), out_shape=jax.S...  10.6 us
    ppermute x6, starting transfers between devices, sum_over(): lax.ppermute(value, axis, [(i, (i + k) % size) for i in range(size)])  9.43 us
  transfers between devices with their start and end apart: 19, of which 10 were waited for; matrix products, arithmetic and copies ran while one was open for 3% of the time, Pallas kernels for 5%

profile of v4, /device:TPU:1, one launch (start us, length us, event | category | flops | bytes accessed | tf_op | source)
XLA Modules:
  0.0 210.4 jit_solution(5815508700421794051)
XLA Ops:
  8.1 13.5 %collective-permute-start.15 = (bf16[128,256]{1,0:T(8,128)(2,1)S(1)}, bf16[128,256]{1,0:T(8,128)(2,1)S(1)}, u32[]{:S(2)}, u32[]{:S(2)}) collective-permute-start(bf16[128,256]{1,0:T(8,128)(2,1)S(1)} %dynamic-slice_bitcast_fusion), channel_id=1, source_target_pairs={{4,251},{8,247},{12,243},{16,239},{20,235},{21,234},{24,231},{25,2... | collective-permute-start | bytes 196616 | tf_op jit(solution)/shard_map/ppermute | solution.py:202
  21.7 1.3 convolution_convert_fusion.1
  24.8 4.0 %all-to-all-start = ((bf16[8,128,256]{2,1,0:T(8,128)(2,1)}), bf16[8,128,256]{2,1,0:T(8,128)(2,1)S(1)}, u32[]{:S(2)}, u32[]{:S(2)}) async-start(bf16[8,128,256]{2,1,0:T(8,128)(2,1)} %broadcast_in_dim.49), calls=%async_computation | async-start | bytes 1048576 | tf_op jit(solution)/shard_map/all_to_all | solution.py:209
  28.9 2.7 %collective-permute-start.1 = (bf16[2,4,64,256]{3,2,1,0:T(8,128)(2,1)S(1)}, bf16[2,4,64,256]{3,2,1,0:T(8,128)(2,1)S(1)}, u32[]{:S(2)}, u32[]{:S(2)}) collective-permute-start(bf16[2,4,64,256]{3,2,1,0:T(8,128)(2,1)S(1)} %pad_maximum_fusion), channel_id=1, source_target_pairs={{0,8},{4,60},{8,16},{12,4},{16,24},{20,12},{24,32},{28,20},{32,40}... | collective-permute-start | bytes 786440 | tf_op jit(solution)/shard_map/ppermute | solution.py:228
  31.6 14.2 %collective-permute-done.1.refs_4_ = bf16[2,4,64,256]{3,2,1,0:T(8,128)(2,1)S(1)} collective-permute-done((bf16[2,4,64,256]{3,2,1,0:T(8,128)(2,1)S(1)}, bf16[2,4,64,256]{3,2,1,0:T(8,128)(2,1)S(1)}, u32[]{:S(2)}, u32[]{:S(2)}) %collective-permute-start.1) | collective-permute-done | bytes 262176 | tf_op jit(solution)/shard_map/ppermute | solution.py:228
  46.9 4.1 %collective-permute-done.3.refs_6_ = bf16[2,4,64,256]{3,2,1,0:T(8,128)(2,1)S(1)} collective-permute-done((bf16[2,4,64,256]{3,2,1,0:T(8,128)(2,1)S(1)}, bf16[2,4,64,256]{3,2,1,0:T(8,128)(2,1)S(1)}, u32[]{:S(2)}, u32[]{:S(2)}) %collective-permute-start.3) | collective-permute-done | bytes 262176 | tf_op jit(solution)/shard_map/ppermute | solution.py:228
  51.0 2.3 %collective-permute-start.5 = (bf16[2,4,64,256]{3,2,1,0:T(8,128)(2,1)S(1)}, bf16[2,4,64,256]{3,2,1,0:T(8,128)(2,1)S(1)}, u32[]{:S(2)}, u32[]{:S(2)}) collective-permute-start(bf16[2,4,64,256]{3,2,1,0:T(8,128)(2,1)S(1)} %collective-permute-done.3.refs_6_), channel_id=1, source_target_pairs={{0,8},{4,60},{8,16},{12,4},{16,24},{20,12},{24,32},{28,20},{32,40}... | collective-permute-start | bytes 786440 | tf_op jit(solution)/shard_map/ppermute | solution.py:228
  53.3 3.3 %collective-permute-done.5.refs_2_ = bf16[2,4,64,256]{3,2,1,0:T(8,128)(2,1)S(1)} collective-permute-done((bf16[2,4,64,256]{3,2,1,0:T(8,128)(2,1)S(1)}, bf16[2,4,64,256]{3,2,1,0:T(8,128)(2,1)S(1)}, u32[]{:S(2)}, u32[]{:S(2)}) %collective-permute-start.5) | collective-permute-done | bytes 262176 | tf_op jit(solution)/shard_map/ppermute | solution.py:228
  57.5 3.2 %collective-permute-start.7 = (bf16[4,64,256]{2,1,0:T(8,128)(2,1)S(1)}, bf16[4,64,256]{2,1,0:T(8,128)(2,1)S(1)}, u32[]{:S(2)}, u32[]{:S(2)}) collective-permute-start(bf16[4,64,256]{2,1,0:T(8,128)(2,1)S(1)} %slice_bitcast_fusion), channel_id=1, source_target_pairs={{0,8},{4,60},{8,16},{12,4},{16,24},{20,12},{24,32},{28,20},{32,40}... | collective-permute-start | bytes 393224 | tf_op jit(solution)/shard_map/ppermute | solution.py:232
  60.7 2.9 %collective-permute-start.2 = (bf16[2,4,64,256]{3,2,1,0:T(8,128)(2,1)S(1)}, bf16[2,4,64,256]{3,2,1,0:T(8,128)(2,1)S(1)}, u32[]{:S(2)}, u32[]{:S(2)}) collective-permute-start(bf16[2,4,64,256]{3,2,1,0:T(8,128)(2,1)S(1)} %collective-permute-done.1.refs_4_), channel_id=1, source_target_pairs={{0,4},{4,0},{1,5},{5,1},{2,6},{6,2},{3,7},{7,3},{8,12},{12,8},{9,1... | collective-permute-start | bytes 786440 | tf_op jit(solution)/shard_map/ppermute | solution.py:230
  64.1 5.6 %collective-permute-start.8 = (bf16[4,64,256]{2,1,0:T(8,128)(2,1)S(1)}, bf16[4,64,256]{2,1,0:T(8,128)(2,1)S(1)}, u32[]{:S(2)}, u32[]{:S(2)}) collective-permute-start(bf16[4,64,256]{2,1,0:T(8,128)(2,1)S(1)} %collective-permute-done.7.refs_4_), channel_id=1, source_target_pairs={{0,4},{4,0},{1,5},{5,1},{2,6},{6,2},{3,7},{7,3},{8,12},{12,8},{9,1... | collective-permute-start | bytes 393224 | tf_op jit(solution)/shard_map/ppermute | solution.py:233
  71.1 5.9 %update_products.2 = f32[64,256]{1,0:T(8,128)} custom-call(s32[10]{0:T(128)} %bitcast.47, s32[64]{0:T(128)} %bitcast.44, bf16[4,64,256]{2,1,0:T(8,128)(2,1)} %bitcast.42, bf16[4,64,256]{2,1,0:T(8,128)(2,1)} %copy-done.6, bf16[2,4,64,256]{3,2,1,0:T(8,128)(2,1)} %copy-done.8, bf16[2,4,64,256]{3,2,1,0:T(8,128)(2,1)} %copy-done.11, ...), custom_call_target="tpu_custom_call" | custom-call | flops 335544320 | bytes 6553600 | tf_op jit(solution)/shard_map/update_products/pallas_call | solution.py:56
  78.5 4.6 %update_products.3 = f32[64,256]{1,0:T(8,128)} custom-call(s32[6]{0:T(128)} %slice.20.refs_0_, s32[64]{0:T(128)} %bitcast.45, bf16[2,4,64,256]{3,2,1,0:T(8,128)(2,1)} %copy-done.3, bf16[2,4,64,256]{3,2,1,0:T(8,128)(2,1)} %copy-done.10, bf16[4,64,256]{2,1,0:T(8,128)(2,1)} %copy-done.13, bf16[4,64,256]{2,1,0:T(8,128)(2,1)} %copy-done.14, ...), custom_call_target="tpu_custom_call" | custom-call | flops 201326592 | bytes 3932160 | tf_op jit(solution)/shard_map/update_products/pallas_call | solution.py:56
  86.0 1.5 broadcast_select_fusion.refs_4_
  89.3 1.5 collective-permute-done.9
  90.8 5.9 %collective-permute-start.14 = (bf16[64,256]{1,0:T(8,128)(2,1)S(1)}, bf16[64,256]{1,0:T(8,128)(2,1)S(1)}, u32[]{:S(2)}, u32[]{:S(2)}) collective-permute-start(bf16[64,256]{1,0:T(8,128)(2,1)S(1)} %add_convert_fusion.2), channel_id=1, source_target_pairs={{0,3},{1,0},{2,1},{3,2},{4,7},{5,4},{6,5},{7,6},{8,11},{9,8},{10,9... | collective-permute-start | bytes 98312 | tf_op jit(solution)/shard_map/ppermute | solution.py:171
  96.7 1.5 collective-permute-start.12
  98.8 1.9 collective-permute-done.13
  101.0 19.9 %all-gather = bf16[1024,256]{1,0:T(8,128)(2,1)} all-gather(bf16[64,256]{1,0:T(8,128)(2,1)S(1)} %add_convert_fusion.1), channel_id=2, replica_groups=mesh['sub'=4,'z'=8,'core'=2,'col'=4] {'z','core'}, dimensions={0}, use_global_device_ids=true | all-gather | bytes 557056 | tf_op jit(solution)/shard_map/all_gather | solution.py:251
  120.9 22.7 %all-gather.4.cloned.1.call-done = bf16[256,128,256]{2,1,0:T(8,128)(2,1)} async-done(((bf16[8,128,256]{2,1,0:T(8,128)(2,1)}), bf16[256,128,256]{2,1,0:T(8,128)(2,1)}) %all-gather.4.cloned.1.call-update) | async-done | bytes 16777232 | tf_op jit(solution)/shard_map/all_gather | solution.py:246
  143.6 19.0 %top_solve.1 = (bf16[64,256]{1,0:T(8,128)(2,1)}, bf16[8,4,64,256]{3,2,1,0:T(8,128)(2,1)}, bf16[8,4,64,256]{3,2,1,0:T(8,128)(2,1)}) custom-call(s32[2]{0:T(128)} %pad_add_fusion.refs_0_, s32[64]{0:T(128)} %bitcast.46, bf16[16,64,256]{2,1,0:T(8,128)(2,1)} %refs_2_.1, bf16[16,64,256]{2,1,0:T(8,128)(2,1)} %bitcast.39, ...), custom_call_target="tpu_custom_call" | custom-call | tf_op jit(solution)/shard_map/top_solve/pallas_call | solution.py:150
  162.9 2.6 %collective-permute-done.16 = bf16[8,4,64,256]{3,2,1,0:T(8,128)(2,1)S(1)} collective-permute-done((bf16[8,4,64,256]{3,2,1,0:T(8,128)(2,1)}, bf16[8,4,64,256]{3,2,1,0:T(8,128)(2,1)S(1)}, u32[]{:S(2)}, u32[]{:S(2)}) %collective-permute-start.16) | collective-permute-done | bytes 1048608 | tf_op jit(solution)/shard_map/ppermute | solution.py:257
  165.5 1.6 add_convert_fusion
  167.2 35.4 %all_to_all.10 = bf16[8,4,64,256]{3,2,1,0:T(8,128)(2,1)S(1)} all-to-all(bf16[8,4,64,256]{3,2,1,0:T(8,128)(2,1)S(1)} %add_convert_fusion), channel_id=1, replica_groups=mesh['sub'=4,'z'=8,'core'=2,'col'=4] {'z'}, dimensions={0} | all-to-all | bytes 2097152 | tf_op jit(solution)/shard_map/all_to_all | solution.py:259
  (75 shorter events, 15.0 us)
Async XLA Ops:
  8.1 15.0 %collective-permute-start.15 = (bf16[128,256]{1,0:T(8,128)(2,1)S(1)}, bf16[128,256]{1,0:T(8,128)(2,1)S(1)}, u32[]{:S(2)}, u32[]{:S(2)}) collective-permute-start(bf16[128,256]{1,0:T(8,128)(2,1)S(1)} %dynamic-slice_bitcast_fusion), channel_id=1, source_target_pairs={{4,251},{8,247},{12,243},{16,239},{20,235},{21,234},{24,231},{25,2... | collective-permute-start | bytes 196616 | tf_op jit(solution)/shard_map/ppermute | solution.py:202
  21.6 48.1 %copy-start.16 = (pred[16]{0:T(512)(128)(4,1)S(1)}, pred[16]{0:T(512)(128)(4,1)}, u32[]{:S(2)}) copy-start(pred[16]{0:T(512)(128)(4,1)} %constant.65) | copy-start | bytes 52
  21.6 48.1 %copy-start.17 = (s32[16]{0:T(128)S(1)}, s32[16]{0:T(128)}, u32[]{:S(2)}) copy-start(s32[16]{0:T(128)} %constant.58.clone) | copy-start | bytes 196
  23.0 47.4 %copy-start.4 = (bf16[4,256,64]{1,2,0:T(8,128)(2,1)}, bf16[4,256,64]{1,2,0:T(8,128)(2,1)S(1)}, u32[]{:S(2)}) copy-start(bf16[4,256,64]{1,2,0:T(8,128)(2,1)S(1)} %convolution_convert_fusion.1) | copy-start | bytes 393220
  23.0 5.9 %collective-permute-start = (bf16[4,64,256]{2,1,0:T(8,128)(2,1)S(1)}, bf16[4,64,256]{2,1,0:T(8,128)(2,1)S(1)}, u32[]{:S(2)}, u32[]{:S(2)}) collective-permute-start(bf16[4,64,256]{2,1,0:T(8,128)(2,1)S(1)} %bitcast.40), channel_id=1, source_target_pairs={{0,4},{4,0},{1,5},{5,1},{2,6},{6,2},{3,7},{7,3},{8,12},{12,8},{9,1... | collective-permute-start | bytes 393224 | tf_op jit(solution)/shard_map/ppermute | solution.py:224
  24.8 31.9 %all-to-all-start = ((bf16[8,128,256]{2,1,0:T(8,128)(2,1)}), bf16[8,128,256]{2,1,0:T(8,128)(2,1)S(1)}, u32[]{:S(2)}, u32[]{:S(2)}) async-start(bf16[8,128,256]{2,1,0:T(8,128)(2,1)} %broadcast_in_dim.49), calls=%async_computation | async-start | bytes 1048576 | tf_op jit(solution)/shard_map/all_to_all | solution.py:209
  28.8 114.8 %all-gather.4.cloned.1.call-start = ((), (), s32[]{:S(2)}) async-start(), calls=%async_computation.2 | async-start | bytes 17301504 | tf_op jit(solution)/shard_map/all_gather | solution.py:246
  28.9 41.5 %copy-start.6 = (bf16[4,64,256]{2,1,0:T(8,128)(2,1)}, bf16[4,64,256]{2,1,0:T(8,128)(2,1)S(1)}, u32[]{:S(2)}) copy-start(bf16[4,64,256]{2,1,0:T(8,128)(2,1)S(1)} %collective-permute-done.refs_3_) | copy-start | bytes 393220
  28.9 16.9 %collective-permute-start.1 = (bf16[2,4,64,256]{3,2,1,0:T(8,128)(2,1)S(1)}, bf16[2,4,64,256]{3,2,1,0:T(8,128)(2,1)S(1)}, u32[]{:S(2)}, u32[]{:S(2)}) collective-permute-start(bf16[2,4,64,256]{3,2,1,0:T(8,128)(2,1)S(1)} %pad_maximum_fusion), channel_id=1, source_target_pairs={{0,8},{4,60},{8,16},{12,4},{16,24},{20,12},{24,32},{28,20},{32,40}... | collective-permute-start | bytes 786440 | tf_op jit(solution)/shard_map/ppermute | solution.py:228
  45.8 5.2 %collective-permute-start.3 = (bf16[2,4,64,256]{3,2,1,0:T(8,128)(2,1)S(1)}, bf16[2,4,64,256]{3,2,1,0:T(8,128)(2,1)S(1)}, u32[]{:S(2)}, u32[]{:S(2)}) collective-permute-start(bf16[2,4,64,256]{3,2,1,0:T(8,128)(2,1)S(1)} %collective-permute-done.1.refs_4_), channel_id=1, source_target_pairs={{0,8},{4,60},{8,16},{12,4},{16,24},{20,12},{24,32},{28,20},{32,40}... | collective-permute-start | bytes 786440 | tf_op jit(solution)/shard_map/ppermute | solution.py:228
  51.0 5.6 %collective-permute-start.5 = (bf16[2,4,64,256]{3,2,1,0:T(8,128)(2,1)S(1)}, bf16[2,4,64,256]{3,2,1,0:T(8,128)(2,1)S(1)}, u32[]{:S(2)}, u32[]{:S(2)}) collective-permute-start(bf16[2,4,64,256]{3,2,1,0:T(8,128)(2,1)S(1)} %collective-permute-done.3.refs_6_), channel_id=1, source_target_pairs={{0,8},{4,60},{8,16},{12,4},{16,24},{20,12},{24,32},{28,20},{32,40}... | collective-permute-start | bytes 786440 | tf_op jit(solution)/shard_map/ppermute | solution.py:228
  57.5 6.6 %collective-permute-start.7 = (bf16[4,64,256]{2,1,0:T(8,128)(2,1)S(1)}, bf16[4,64,256]{2,1,0:T(8,128)(2,1)S(1)}, u32[]{:S(2)}, u32[]{:S(2)}) collective-permute-start(bf16[4,64,256]{2,1,0:T(8,128)(2,1)S(1)} %slice_bitcast_fusion), channel_id=1, source_target_pairs={{0,8},{4,60},{8,16},{12,4},{16,24},{20,12},{24,32},{28,20},{32,40}... | collective-permute-start | bytes 393224 | tf_op jit(solution)/shard_map/ppermute | solution.py:232
  60.7 9.6 %collective-permute-start.2 = (bf16[2,4,64,256]{3,2,1,0:T(8,128)(2,1)S(1)}, bf16[2,4,64,256]{3,2,1,0:T(8,128)(2,1)S(1)}, u32[]{:S(2)}, u32[]{:S(2)}) collective-permute-start(bf16[2,4,64,256]{3,2,1,0:T(8,128)(2,1)S(1)} %collective-permute-done.1.refs_4_), channel_id=1, source_target_pairs={{0,4},{4,0},{1,5},{5,1},{2,6},{6,2},{3,7},{7,3},{8,12},{12,8},{9,1... | collective-permute-start | bytes 786440 | tf_op jit(solution)/shard_map/ppermute | solution.py:230
  63.6 6.7 %collective-permute-start.4 = (bf16[2,4,64,256]{3,2,1,0:T(8,128)(2,1)S(1)}, bf16[2,4,64,256]{3,2,1,0:T(8,128)(2,1)S(1)}, u32[]{:S(2)}, u32[]{:S(2)}) collective-permute-start(bf16[2,4,64,256]{3,2,1,0:T(8,128)(2,1)S(1)} %collective-permute-done.3.refs_6_), channel_id=1, source_target_pairs={{0,4},{4,0},{1,5},{5,1},{2,6},{6,2},{3,7},{7,3},{8,12},{12,8},{9,1... | collective-permute-start | bytes 786440 | tf_op jit(solution)/shard_map/ppermute | solution.py:230
  63.7 13.4 %collective-permute-start.6 = (bf16[2,4,64,256]{3,2,1,0:T(8,128)(2,1)S(1)}, bf16[2,4,64,256]{3,2,1,0:T(8,128)(2,1)S(1)}, u32[]{:S(2)}, u32[]{:S(2)}) collective-permute-start(bf16[2,4,64,256]{3,2,1,0:T(8,128)(2,1)S(1)} %collective-permute-done.5.refs_2_), channel_id=1, source_target_pairs={{0,4},{4,0},{1,5},{5,1},{2,6},{6,2},{3,7},{7,3},{8,12},{12,8},{9,1... | collective-permute-start | bytes 786440 | tf_op jit(solution)/shard_map/ppermute | solution.py:230
  64.1 13.0 %collective-permute-start.8 = (bf16[4,64,256]{2,1,0:T(8,128)(2,1)S(1)}, bf16[4,64,256]{2,1,0:T(8,128)(2,1)S(1)}, u32[]{:S(2)}, u32[]{:S(2)}) collective-permute-start(bf16[4,64,256]{2,1,0:T(8,128)(2,1)S(1)} %collective-permute-done.7.refs_4_), channel_id=1, source_target_pairs={{0,4},{4,0},{1,5},{5,1},{2,6},{6,2},{3,7},{7,3},{8,12},{12,8},{9,1... | collective-permute-start | bytes 393224 | tf_op jit(solution)/shard_map/ppermute | solution.py:233
  83.9 4.2 %collective-permute-start.11 = (bf16[64,256]{1,0:T(8,128)(2,1)S(1)}, bf16[64,256]{1,0:T(8,128)(2,1)S(1)}, u32[]{:S(2)}, u32[]{:S(2)}) collective-permute-start(bf16[64,256]{1,0:T(8,128)(2,1)S(1)} %add_convert_fusion.3), channel_id=1, source_target_pairs={{0,192},{64,0},{128,64},{192,128},{1,193},{65,1},{129,65},{193,129... | collective-permute-start | bytes 98312 | tf_op jit(solution)/shard_map/ppermute | solution.py:171
  84.2 5.0 %collective-permute-start.10 = (bf16[64,256]{1,0:T(8,128)(2,1)S(1)}, bf16[64,256]{1,0:T(8,128)(2,1)S(1)}, u32[]{:S(2)}, u32[]{:S(2)}) collective-permute-start(bf16[64,256]{1,0:T(8,128)(2,1)S(1)} %add_convert_fusion.3), channel_id=1, source_target_pairs={{0,64},{64,128},{128,192},{192,0},{1,65},{65,129},{129,193},{193,1... | collective-permute-start | bytes 98312 | tf_op jit(solution)/shard_map/ppermute | solution.py:171
  85.5 5.2 %collective-permute-start.9 = (bf16[64,256]{1,0:T(8,128)(2,1)S(1)}, bf16[64,256]{1,0:T(8,128)(2,1)S(1)}, u32[]{:S(2)}, u32[]{:S(2)}) collective-permute-start(bf16[64,256]{1,0:T(8,128)(2,1)S(1)} %add_convert_fusion.3), channel_id=1, source_target_pairs={{0,128},{64,192},{128,0},{192,64},{1,129},{65,193},{129,1},{193,65... | collective-permute-start | bytes 98312 | tf_op jit(solution)/shard_map/ppermute | solution.py:171
  90.8 8.0 %collective-permute-start.14 = (bf16[64,256]{1,0:T(8,128)(2,1)S(1)}, bf16[64,256]{1,0:T(8,128)(2,1)S(1)}, u32[]{:S(2)}, u32[]{:S(2)}) collective-permute-start(bf16[64,256]{1,0:T(8,128)(2,1)S(1)} %add_convert_fusion.2), channel_id=1, source_target_pairs={{0,3},{1,0},{2,1},{3,2},{4,7},{5,4},{6,5},{7,6},{8,11},{9,8},{10,9... | collective-permute-start | bytes 98312 | tf_op jit(solution)/shard_map/ppermute | solution.py:171
  96.7 4.0 %collective-permute-start.13 = (bf16[64,256]{1,0:T(8,128)(2,1)S(1)}, bf16[64,256]{1,0:T(8,128)(2,1)S(1)}, u32[]{:S(2)}, u32[]{:S(2)}) collective-permute-start(bf16[64,256]{1,0:T(8,128)(2,1)S(1)} %add_convert_fusion.2), channel_id=1, source_target_pairs={{0,1},{1,2},{2,3},{3,0},{4,5},{5,6},{6,7},{7,4},{8,9},{9,10},{10,1... | collective-permute-start | bytes 98312 | tf_op jit(solution)/shard_map/ppermute | solution.py:171
  96.7 4.3 %collective-permute-start.12 = (bf16[64,256]{1,0:T(8,128)(2,1)S(1)}, bf16[64,256]{1,0:T(8,128)(2,1)S(1)}, u32[]{:S(2)}, u32[]{:S(2)}) collective-permute-start(bf16[64,256]{1,0:T(8,128)(2,1)S(1)} %add_convert_fusion.2), channel_id=1, source_target_pairs={{0,2},{1,3},{2,0},{3,1},{4,6},{5,7},{6,4},{7,5},{8,10},{9,11},{10,... | collective-permute-start | bytes 98312 | tf_op jit(solution)/shard_map/ppermute | solution.py:171
  162.6 3.0 %collective-permute-start.16 = (bf16[8,4,64,256]{3,2,1,0:T(8,128)(2,1)}, bf16[8,4,64,256]{3,2,1,0:T(8,128)(2,1)S(1)}, u32[]{:S(2)}, u32[]{:S(2)}) collective-permute-start(bf16[8,4,64,256]{3,2,1,0:T(8,128)(2,1)} %get-tuple-element.8), channel_id=1, source_target_pairs={{0,4},{4,0},{1,5},{5,1},{2,6},{6,2},{3,7},{7,3},{8,12},{12,8},{9,1... | collective-permute-start | bytes 3145736 | tf_op jit(solution)/shard_map/ppermute | solution.py:257
  167.1 35.5 %copy-start.5 = (bf16[4,256,64]{1,2,0:T(8,128)(2,1)S(1)}, bf16[4,256,64]{1,2,0:T(8,128)(2,1)}, u32[]{:S(2)}) copy-start(bf16[4,256,64]{1,2,0:T(8,128)(2,1)} %copy-done.4) | copy-start | bytes 393220
  (14 other events, 146.7 us)
Sparse Core Ops, SparseCore 0:
  57.6 85.9 all-gather.3

commit v5 on v3

--- a/solution.py
+++ b/solution.py
@@ -13,17 +13,135 @@
 NN = (((1,), (0,)), ((), ()))
 
 
+def hop(size, far):
+    return [
+        (2 * z + core, 2 * ((z + far * (1 - 2 * core)) % size) + core)
+        for z in range(size)
+        for core in range(2)
+    ]
+
+
+def update_kernel(
+    at_ref, w_ref, mine_ref, other_ref, c_hbm, out_ref, coup_ref, sems
+):
+    chips, leaves = mine_ref.shape[:2]
+    per_chip = 2 * leaves
+    core = at_ref[1]
+
+    def fetch(chip):
+        piece = pl.ds(chip * per_chip, per_chip)
+        return pltpu.make_async_copy(
+            c_hbm.at[piece], coup_ref.at[piece], sems.at[chip]
+        )
+
+    for chip in range(chips):
+        fetch(chip).start()
+    total = None
+    for chip in range(chips):
+        fetch(chip).wait()
+        for rows, part in ((mine_ref, core), (other_ref, 1 - core)):
+            for leaf in range(leaves):
+                at = (2 * chip + part) * leaves + leaf
+                weight = w_ref[at].astype(F32)
+                term = weight * lax.dot_general(
+                    rows[chip, leaf], coup_ref[at], NT, preferred_element_type=F32
+                )
+                total = term if total is None else total + term
+    out_ref[...] = total
+
+
+def update_products(at, pattern, mine, other, coupled):
+    chips, leaves, nrhs, size = mine.shape
+    whole = pl.BlockSpec(memory_space=pltpu.VMEM)
+    scalars = pl.BlockSpec(memory_space=pltpu.SMEM)
+    return pl.pallas_call(
+        update_kernel,
+        out_shape=jax.ShapeDtypeStruct((nrhs, size), F32),
+        in_specs=[scalars] * 2
+        + [whole] * 2
+        + [pl.BlockSpec(memory_space=pltpu.HBM)],
+        out_specs=whole,
+        scratch_shapes=[
+            pltpu.VMEM(coupled.shape, BF),
+            pltpu.SemaphoreType.DMA((chips,)),
+        ],
+        compiler_params=pltpu.CompilerParams(vmem_limit_bytes=16 << 20),
+        name="update_products",
+    )(
+        at, pattern, mine, other,
+        pltpu.with_memory_space_constraint(coupled, pltpu.HBM),
+    )
+
+
 def first_block(a):
     return a * (a - 1) // 2
 
 
+def group_fetches(base_ref, c_hbm, coup, sems):
+    groups, leaves = coup.shape[:2]
+    return [
+        pltpu.make_async_copy(
+            c_hbm.at[pl.ds(base_ref[i], leaves)], coup.at[i], sems.at[i]
+        )
+        for i in range(groups)
+    ]
+
+
+def group_products(own, base_ref, w_ref, fetch, coup, outs):
+    leaves = coup.shape[1]
+    i = 0
+    for out in outs:
+        for group in range(out.shape[0]):
+            fetch[i].wait()
+            for leaf in range(leaves):
+                weight = w_ref[base_ref[i] + leaf].astype(F32)
+                value = lax.dot_general(
+                    own, coup[i, leaf], NN, preferred_element_type=F32
+                )
+                out[group, leaf] = (value * weight).astype(BF)
+            i += 1
+
+
+def near_kernel(base_ref, w_ref, own_ref, c_hbm, keep_ref, give_ref, coup, sems):
+    fetch = group_fetches(base_ref, c_hbm, coup, sems)
+    for copy in fetch:
+        copy.start()
+    group_products(
+        own_ref[...], base_ref, w_ref, fetch, coup, (give_ref, keep_ref)
+    )
+
+
+def near_products(base, pattern, own, coupled, leaves):
+    nrhs, size = own.shape
+    groups = base.shape[0]
+    whole = pl.BlockSpec(memory_space=pltpu.VMEM)
+    scalars = pl.BlockSpec(memory_space=pltpu.SMEM)
+    part = jax.ShapeDtypeStruct((groups // 2, leaves, nrhs, size), BF)
+    return pl.pallas_call(
+        near_kernel,
+        out_shape=(part, part),
+        in_specs=[scalars] * 2 + [whole, pl.BlockSpec(memory_space=pltpu.HBM)],
+        out_specs=(whole,) * 2,
+        scratch_shapes=[
+            pltpu.VMEM((groups, leaves, size, size), BF),
+            pltpu.SemaphoreType.DMA((groups,)),
+        ],
+        compiler_params=pltpu.CompilerParams(vmem_limit_bytes=16 << 20),
+        cost_estimate=pl.CostEstimate(
+            flops=2 * groups * leaves * nrhs * size * size,
+            bytes_accessed=2 * groups * leaves * size * (size + nrhs),
+            transcendentals=0,
+        ),
+        name="near_products",
+    )(base, pattern, own, pltpu.with_memory_space_constraint(coupled, pltpu.HBM))
+
+
 def top_kernel(
-    units, at_ref, w_ref, r_ref, u_ref, g_ref, f_hbm, c_hbm,
-    top_ref, mine_ref, other_ref, zs, xs, fac, coup, sems, coup_sem,
+    units, at_ref, base_ref, w_ref, r_ref, u_ref, g_ref, f_hbm, c_hbm,
+    top_ref, keep_ref, give_ref, zs, xs, fac, coup, sems, coup_sems,
 ):
     count = r_ref.shape[0]
     half = f_hbm.shape[1]
-    chips, leaves = mine_ref.shape[:2]
 
     def dot(a, b, dims):
         return lax.dot_general(a, b, dims, preferred_element_type=F32)
@@ -42,8 +160,6 @@
                     fac.at[first_block(a) + b, pl.ds(part * half, half)],
                     sems.at[a],
                 ).start()
-    coupling = pltpu.make_async_copy(c_hbm, coup, coup_sem)
-    coupling.start()
 
     summed = rhs(0)
     for k in range(count):
@@ -56,6 +172,9 @@
             for b in range(k):
                 later -= dot(zs[b], block(k + 1, b), NT)
             summed = later - dot(z, block(k + 1, k), NT)
+    fetch = group_fetches(base_ref, c_hbm, coup, coup_sems)
+    for copy in fetch:
+        copy.start()
     summed = zs[count - 1].astype(F32)
     for k in reversed(range(count)):
         x = dot(summed.astype(BF), g_ref[k], NN).astype(BF)
@@ -68,38 +187,37 @@
 
     own = xs[at_ref[0]]
     top_ref[...] = own
-    core = at_ref[1]
-    coupling.wait()
-    for out, part in ((other_ref, 1 - core), (mine_ref, core)):
-        for chip in range(chips):
-            for leaf in range(leaves):
-                at = (2 * chip + part) * leaves + leaf
-                weight = w_ref[at].astype(F32)
-                out[chip, leaf] = (dot(own, coup[at], NN) * weight).astype(BF)
-
-
-def top_solve(units, at, pattern, rhs, updates, inverse, factor, coupled, chips, leaves):
+    group_products(own, base_ref, w_ref, fetch, coup, (give_ref, keep_ref))
+
+
+def top_solve(units, at, base, pattern, rhs, updates, inverse, factor, coupled, leaves):
     whole = pl.BlockSpec(memory_space=pltpu.VMEM)
     scalars = pl.BlockSpec(memory_space=pltpu.SMEM)
-    placed = pl.BlockSpec(memory_space=pltpu.HBM)
     count, nrhs, size = rhs.shape
-    part = jax.ShapeDtypeStruct((chips, leaves, nrhs, size), BF)
+    groups = base.shape[0]
+    part = jax.ShapeDtypeStruct((groups // 2, leaves, nrhs, size), BF)
     return pl.pallas_call(
         lambda *refs: top_kernel(units, *refs),
         out_shape=(jax.ShapeDtypeStruct((nrhs, size), BF), part, part),
-        in_specs=[scalars] * 2 + [whole] * 3 + [placed] * 2,
+        in_specs=[scalars] * 3
+        + [whole] * 3
+        + [pl.BlockSpec(memory_space=pltpu.HBM)] * 2,
         out_specs=(whole,) * 3,
         scratch_shapes=[
             pltpu.VMEM(rhs.shape, BF),
             pltpu.VMEM(rhs.shape, BF),
             pltpu.VMEM((first_block(count), size, size), BF),
-            pltpu.VMEM(coupled.shape, BF),
+            pltpu.VMEM((groups, leaves, size, size), BF),
             pltpu.SemaphoreType.DMA((count,)),
-            pltpu.SemaphoreType.DMA,
+            pltpu.SemaphoreType.DMA((groups,)),
         ],
-        compiler_params=pltpu.CompilerParams(vmem_limit_bytes=40 << 20),
+        compiler_params=pltpu.CompilerParams(vmem_limit_bytes=32 << 20),
         name="top_solve",
-    )(at, pattern, rhs, updates, inverse, factor, coupled)
+    )(
+        at, base, pattern, rhs, updates, inverse,
+        pltpu.with_memory_space_constraint(factor, pltpu.HBM),
+        pltpu.with_memory_space_constraint(coupled, pltpu.HBM),
+    )
 
 
 def sum_over(value, axis, size):
@@ -122,7 +240,6 @@
         own_rhs = leaf_rhs[0, :, 0]
         own_inverse = jnp.tril(leaf_inverse[0, :, 0])
         coupled = coupling[0, 0, :, 0]
-        weights = pattern[0, 0, :, 0].astype(BF)
         leaves, nrhs, size = own_rhs.shape
         rows = zs * cores
         assert top_factor.shape[1] == subs
@@ -163,25 +280,54 @@
             "z", 0, 0, tiled=True,
         )
         other = lax.ppermute(mine, "core", SWAP)
-        first = core == 0
-        forward = jnp.stack(
-            [jnp.where(first, mine, other), jnp.where(first, other, mine)], axis=1
-        ).reshape(rows * leaves, nrhs, size)
-        partial = jnp.einsum(
-            "inb,ieb->ne", forward * weights[:, None, None], coupled,
-            preferred_element_type=F32,
-        )
+        at = jnp.stack([row, core])
+        present = pattern[0, 0, :, 0]
+        partial = update_products(at, present, mine, other, coupled)
         update = sum_over(sum_over(partial, "sub", subs), "col", cols).astype(BF)
         updates = lax.all_gather(update, ROW, axis=0)
 
-        own_top, mine, other = top_solve(
-            units, jnp.stack([row, core]), pattern[0, 0, :, 0], top_rhs, updates,
-            top_tri, factor, coupled, zs, leaves,
-        )
-        other = lax.ppermute(other, "core", SWAP)
-        pair = (mine.astype(F32) + other.astype(F32)).astype(BF)
-        spread = lax.all_to_all(pair, "z", 0, 0, tiled=True)
-        back_sums = jnp.sum(spread.astype(F32), axis=0)
+        chip = lax.axis_index("z")
+        turn = 1 - 2 * core
+        other_core = 1 - core
+
+        def base(groups):
+            starts = [
+                ((chip + away * turn + zs) % zs * cores + part) * leaves
+                for away, part in groups
+            ]
+            return jnp.stack(starts).astype(jnp.int32)
+
+        far_base = base(
+            [(-3, 0), (-3, 1), (4, other_core), (3, 0), (3, 1), (4, core)]
+        )
+        near_base = base(
+            [(-1, 0), (-1, 1), (-2, 0), (-2, 1), (0, other_core)]
+            + [(1, 0), (1, 1), (2, 0), (2, 1), (0, core)]
+        )
+
+        own_top, keep, give = top_solve(
+            units, at, far_base, present, top_rhs, updates, top_tri, factor,
+            coupled, leaves,
+        )
+        got = lax.ppermute(give, "core", SWAP)
+        sent = (keep.astype(F32) + got.astype(F32)).astype(BF)
+        own_late, sent = lax.optimization_barrier((own_top, sent))
+        passed = lax.ppermute(sent, ROW, hop(zs, 2)).astype(F32)
+        keep, give = near_products(near_base, present, own_late, coupled, leaves)
+        near = [
+            keep[i:j].astype(F32) + lax.ppermute(give[i:j], "core", SWAP).astype(F32)
+            for i, j in ((0, 2), (2, 4), (4, 5))
+        ]
+        upper = jnp.arange(cores)[:, None, None, None] == core
+        one = (near[0] + passed[0:2]).astype(BF)
+        two = (near[1] + jnp.where(upper, passed[2][None], 0.0)).astype(BF)
+        arrived = lax.ppermute(one, ROW, hop(zs, 1)).astype(F32) + lax.ppermute(
+            two, ROW, hop(zs, 2)
+        ).astype(F32)
+        first = core == 0
+        rest = jnp.where(first, arrived[1], arrived[0]).astype(BF)
+        rest = lax.ppermute(rest, "core", SWAP).astype(F32)
+        back_sums = near[2][0] + jnp.where(first, arrived[0], arrived[1]) + rest
         leaf_residue = (leaf_forward.astype(F32) - back_sums).astype(BF)
         leaf_result = jnp.einsum(
             "inb,ibd->ind", leaf_residue, own_inverse, preferred_element_type=F32

time: 193 us -> 184 us (0.953)
  blocking collectives: 84.3 us -> 50.8 us
  starting transfers between devices: 28 us -> 41.2 us
  waiting for transfers between devices: 31.7 us -> 41.7 us
  Pallas kernels: 16.9 us -> 26.5 us
  matrix products: 9.16 us -> 3.28 us
  local copies, waits for them, and re-layouts: 6.03 us -> 3.71 us
    all_to_all x1 -> x0, blocking collectives: 33.5 us -> none  [local(): spread = lax.all_to_all(pair, 'z', 0, 0, tiled=True)]
    ppermute x1 -> x8, starting transfers between devices: 0.25 us -> 11.5 us  [the longest x1 3.33 us: local(): passed = lax.ppermute(sent, ROW, hop(zs, 2)).astype(F32)]
    ppermute x1 -> x8, waiting for transfers between devices: 2.5 us -> 13.5 us  [the longest x1 5.59 us: local(): lax.ppermute(two, ROW, hop(zs, 2)).astype(F32)]
    pallas_call x0 -> x2, Pallas kernels: none -> 9.28 us  [the longest x1 5.49 us: update_products(): pl.pallas_call(update_kernel, out_shape=jax.ShapeDtypeStruct((nrhs, size)...]
    dot_general x1 -> x0, matrix products: 6.97 us -> none  [local(): jnp.einsum('inb,ieb->ne', forward * weights[:, None, None], coupled, pref...]
    unnamed x14 -> x12, local copies, waits for them, and re-layouts: 4.21 us -> 1.61 us
    ppermute x6, starting transfers between devices: 9.27 us -> 11.2 us  [sum_over(): lax.ppermute(value, axis, [(i, (i + k) % size) for i in range(size)])]
  transfers between devices with their start and end apart: 11 -> 18, of which waited for: 9 -> 11; matrix products, arithmetic and copies ran while one was open for 5% -> 1% of each run, Pallas kernels for 0% -> 5%
where the time goes in v5:
time: 184 us; the launch traced here: 183 us
  blocking collectives  50.8 us (28%)
  waiting for transfers between devices  41.7 us (23%)
  starting transfers between devices  41.2 us (22%)
  Pallas kernels  26.5 us (14%)
  between operations  14.3 us (8%)
  local copies, waits for them, and re-layouts  3.71 us (2%)
  matrix products  3.28 us (2%)
    all_to_all x1, blocking collectives, local(): lax.all_to_all(jnp.broadcast_to(leaf_shared[None], (zs,) + leaf_forward.s...  31.4 us
    all_gather x1, blocking collectives, local(): updates = lax.all_gather(update, ROW, axis=0)  19.4 us
    pallas_call x1, Pallas kernels, top_solve(): pl.pallas_call(lambda *refs: top_kernel(units, *refs), out_shape=(jax.Sha...  17.3 us
    all_to_all x1, waiting for transfers between devices, local(): ring = lax.all_to_all(unit, 'z', 0, 0, tiled=True)  16.5 us
    ppermute x1, starting transfers between devices, local(): moved = lax.ppermute(block[half:], ('sub', 'z', 'core', 'col'), pairs)  13.5 us
    ppermute x6, starting transfers between devices, sum_over(): lax.ppermute(value, axis, [(i, (i + k) % size) for i in range(size)])  11.2 us
    ppermute x6, waiting for transfers between devices, sum_over(): lax.ppermute(value, axis, [(i, (i + k) % size) for i in range(size)])  8.09 us
    ppermute x1, waiting for transfers between devices, local(): lax.ppermute(two, ROW, hop(zs, 2)).astype(F32)  5.59 us
  transfers between devices with their start and end apart: 18, of which 11 were waited for; matrix products, arithmetic and copies ran while one was open for 1% of the time, Pallas kernels for 5%

profile of v5, /device:TPU:1, one launch (start us, length us, event | category | flops | bytes accessed | tf_op | source)
XLA Modules:
  0.0 183.2 jit_solution(18378113362862665239)
XLA Ops:
  8.1 13.5 %collective-permute-start = (bf16[128,256]{1,0:T(8,128)(2,1)S(1)}, bf16[128,256]{1,0:T(8,128)(2,1)S(1)}, u32[]{:S(2)}, u32[]{:S(2)}) collective-permute-start(bf16[128,256]{1,0:T(8,128)(2,1)S(1)} %dynamic-slice_bitcast_fusion), channel_id=1, source_target_pairs={{4,251},{8,247},{12,243},{16,239},{20,235},{21,234},{24,231},{25,2... | collective-permute-start | bytes 196616 | tf_op jit(solution)/shard_map/ppermute | solution.py:257
  21.6 1.3 collective-permute-done
  24.6 4.3 %all-to-all-start = ((bf16[8,128,256]{2,1,0:T(8,128)(2,1)}), bf16[8,128,256]{2,1,0:T(8,128)(2,1)S(1)}, u32[]{:S(2)}, u32[]{:S(2)}) async-start(bf16[8,128,256]{2,1,0:T(8,128)(2,1)} %broadcast_in_dim.66), calls=%async_computation | async-start | bytes 1048576 | tf_op jit(solution)/shard_map/all_to_all | solution.py:264
  29.0 1.3 fusion
  30.3 16.5 %all-to-all-done = bf16[8,128,256]{2,1,0:T(8,128)(2,1)S(1)} async-done(((bf16[8,128,256]{2,1,0:T(8,128)(2,1)}), bf16[8,128,256]{2,1,0:T(8,128)(2,1)S(1)}, u32[]{:S(2)}, u32[]{:S(2)}) %all-to-all-start) | async-done | bytes 524320 | tf_op jit(solution)/shard_map/all_to_all | solution.py:264
  47.8 31.4 %all_to_all.10.mine_ref = bf16[8,4,64,256]{3,2,1,0:T(8,128)(2,1)S(1)} all-to-all(bf16[8,4,64,256]{3,2,1,0:T(8,128)(2,1)S(1)} %broadcast_in_dim.67), channel_id=1, replica_groups=mesh['sub'=4,'z'=8,'core'=2,'col'=4] {'z'}, dimensions={0} | all-to-all | bytes 2097152 | tf_op jit(solution)/shard_map/all_to_all | solution.py:278
  80.0 2.2 %collective-permute-done.1.other_ref = bf16[8,4,64,256]{3,2,1,0:T(8,128)(2,1)S(1)} collective-permute-done((bf16[8,4,64,256]{3,2,1,0:T(8,128)(2,1)S(1)}, bf16[8,4,64,256]{3,2,1,0:T(8,128)(2,1)S(1)}, u32[]{:S(2)}, u32[]{:S(2)}) %collective-permute-start.1) | collective-permute-done | bytes 1048608 | tf_op jit(solution)/shard_map/ppermute | solution.py:282
  82.2 5.5 %update_products.1 = f32[64,256]{1,0:T(8,128)S(1)} custom-call(s32[2]{0:T(128)S(1)} %pad_add_fusion.at_ref.refs_0_, s32[64]{0:T(128)S(1)} %bitcast.54, bf16[8,4,64,256]{3,2,1,0:T(8,128)(2,1)S(1)} %all_to_all.10.mine_ref, bf16[8,4,64,256]{3,2,1,0:T(8,128)(2,1)S(1)} %collective-permute-done.1.other_ref, bf16[64,256,256]{2,1,0:T(8,128)(2,1)} %bitcast.57), custom_call_target="tpu_custom_call" | custom-call | tf_op jit(solution)/shard_map/update_products/pallas_call | solution.py:57
  87.8 1.4 collective-permute-start.2
  90.5 2.9 %collective-permute-done.3 = bf16[64,256]{1,0:T(8,128)(2,1)S(1)} collective-permute-done((bf16[64,256]{1,0:T(8,128)(2,1)S(1)}, bf16[64,256]{1,0:T(8,128)(2,1)S(1)}, u32[]{:S(2)}, u32[]{:S(2)}) %collective-permute-start.3) | collective-permute-done | bytes 32800 | tf_op jit(solution)/shard_map/ppermute | solution.py:226
  93.3 1.5 collective-permute-done.4
  94.8 7.2 %collective-permute-start.7 = (bf16[64,256]{1,0:T(8,128)(2,1)S(1)}, bf16[64,256]{1,0:T(8,128)(2,1)S(1)}, u32[]{:S(2)}, u32[]{:S(2)}) collective-permute-start(bf16[64,256]{1,0:T(8,128)(2,1)S(1)} %add_convert_fusion.3), channel_id=1, source_target_pairs={{0,3},{1,0},{2,1},{3,2},{4,7},{5,4},{6,5},{7,6},{8,11},{9,8},{10,9... | collective-permute-start | bytes 98312 | tf_op jit(solution)/shard_map/ppermute | solution.py:226
  103.6 3.8 %collective-permute-done.6 = bf16[64,256]{1,0:T(8,128)(2,1)S(1)} collective-permute-done((bf16[64,256]{1,0:T(8,128)(2,1)S(1)}, bf16[64,256]{1,0:T(8,128)(2,1)S(1)}, u32[]{:S(2)}, u32[]{:S(2)}) %collective-permute-start.6) | collective-permute-done | bytes 32800 | tf_op jit(solution)/shard_map/ppermute | solution.py:226
  107.4 19.4 %all-gather = bf16[1024,256]{1,0:T(8,128)(2,1)S(1)} all-gather(bf16[64,256]{1,0:T(8,128)(2,1)S(1)} %add_convert_fusion.2), channel_id=2, replica_groups=mesh['sub'=4,'z'=8,'core'=2,'col'=4] {'z','core'}, dimensions={0}, use_global_device_ids=true | all-gather | bytes 557056 | tf_op jit(solution)/shard_map/all_gather | solution.py:287
  126.8 17.3 %top_solve.1 = (bf16[64,256]{1,0:T(8,128)(2,1)}, bf16[3,4,64,256]{3,2,1,0:T(8,128)(2,1)S(1)}, bf16[3,4,64,256]{3,2,1,0:T(8,128)(2,1)S(1)}) custom-call(s32[2]{0:T(128)S(1)} %pad_add_fusion.at_ref.refs_0_, s32[6]{0:T(128)S(1)} %stack.83.refs_1_, s32[64]{0:T(128)S(1)} %bitcast.55, bf16[16,64,256]{2,1,0:T(8,128)(2,1)S(1)} %copy-done.1, ...), custom_call_target="tpu_custom_call" | custom-call | tf_op jit(solution)/shard_map/top_solve/pallas_call | solution.py:199
  144.3 1.6 collective-permute-done.8
  146.0 3.3 %collective-permute-start.11 = (bf16[3,4,64,256]{3,2,1,0:T(8,128)(2,1)S(1)}, bf16[3,4,64,256]{3,2,1,0:T(8,128)(2,1)S(1)}, u32[]{:S(2)}, u32[]{:S(2)}) collective-permute-start(bf16[3,4,64,256]{3,2,1,0:T(8,128)(2,1)S(1)} %add_convert_fusion), channel_id=1, source_target_pairs={{0,16},{4,52},{8,24},{12,60},{16,32},{20,4},{24,40},{28,12},{32,48... | collective-permute-start | bytes 1179656 | tf_op jit(solution)/shard_map/ppermute | solution.py:315
  150.2 3.8 %near_products.1 = (bf16[5,4,64,256]{3,2,1,0:T(8,128)(2,1)S(1)}, bf16[5,4,64,256]{3,2,1,0:T(8,128)(2,1)S(1)}) custom-call(s32[10]{0:T(128)S(1)} %stack.73.base_ref, s32[64]{0:T(128)S(1)} %bitcast.56, bf16[64,256]{1,0:T(8,128)(2,1)S(1)} %copy-done.2, bf16[64,256,256]{2,1,0:T(8,128)(2,1)} %bitcast.59), custom_call_target="tpu_custom_call" | custom-call | flops 335544320 | bytes 6553600 | tf_op jit(solution)/shard_map/near_products/pallas_call | solution.py:120
  154.6 3.6 %collective-permute-done.11 = bf16[3,4,64,256]{3,2,1,0:T(8,128)(2,1)S(1)} collective-permute-done((bf16[3,4,64,256]{3,2,1,0:T(8,128)(2,1)S(1)}, bf16[3,4,64,256]{3,2,1,0:T(8,128)(2,1)S(1)}, u32[]{:S(2)}, u32[]{:S(2)}) %collective-permute-start.11) | collective-permute-done | bytes 393248 | tf_op jit(solution)/shard_map/ppermute | solution.py:315
  158.6 3.2 %collective-permute-start.12 = (bf16[2,4,64,256]{3,2,1,0:T(8,128)(2,1)S(1)}, bf16[2,4,64,256]{3,2,1,0:T(8,128)(2,1)S(1)}, u32[]{:S(2)}, u32[]{:S(2)}) collective-permute-start(bf16[2,4,64,256]{3,2,1,0:T(8,128)(2,1)S(1)} %get-tuple-element.24), channel_id=1, source_target_pairs={{0,8},{4,60},{8,16},{12,4},{16,24},{20,12},{24,32},{28,20},{32,40}... | collective-permute-start | bytes 786440 | tf_op jit(solution)/shard_map/ppermute | solution.py:324
  163.4 1.8 collective-permute-done.12
  165.1 5.6 %collective-permute-done.14 = bf16[2,4,64,256]{3,2,1,0:T(8,128)(2,1)S(1)} collective-permute-done((bf16[2,4,64,256]{3,2,1,0:T(8,128)(2,1)S(1)}, bf16[2,4,64,256]{3,2,1,0:T(8,128)(2,1)S(1)}, u32[]{:S(2)}, u32[]{:S(2)}) %collective-permute-start.14) | collective-permute-done | bytes 262176 | tf_op jit(solution)/shard_map/ppermute | solution.py:324
  170.8 2.6 %collective-permute-start.15 = (bf16[4,64,256]{2,1,0:T(8,128)(2,1)S(1)}, bf16[4,64,256]{2,1,0:T(8,128)(2,1)S(1)}, u32[]{:S(2)}, u32[]{:S(2)}) collective-permute-start(bf16[4,64,256]{2,1,0:T(8,128)(2,1)S(1)} %fusion.7), channel_id=1, source_target_pairs={{0,4},{4,0},{1,5},{5,1},{2,6},{6,2},{3,7},{7,3},{8,12},{12,8},{9,1... | collective-permute-start | bytes 393224 | tf_op jit(solution)/shard_map/ppermute | solution.py:329
  174.4 2.0 %fusion.1 = bf16[1,4,1,64,256]{4,3,2,1,0:T(8,128)(2,1)} fusion(bf16[1,4,1,256,256]{4,3,2,1,0:T(8,128)(2,1)} %param.8, pred[256,256]{1,0:T(8,128)(4,1)S(1)} %iota_compare_fusion, bf16[4,64,256]{2,1,0:T(8,128)(2,1)S(1)} %collective-permute-done.15, bf16[1,4,64,256]{3,2,1,0:T(8,128)(2,1)S(1)} %collective-permute-done.9, bf16[4,64,256]{2,1,0:T(8,128)(2,1)S(1)} %fusion, ...), kind=kOutput, calls=%fused_computation.4 | convolution fusion | flops 34537472 | bytes 1769473 | tf_op jit(solution)/shard_map/inb,ibd->ind/dot_general | solution.py:332
  (53 shorter events, 12.2 us)
Async XLA Ops:
  7.2 21.8 %copy-start = (bf16[1,4,1,64,256]{4,3,2,1,0:T(8,128)(2,1)S(1)}, bf16[1,4,1,64,256]{4,3,2,1,0:T(8,128)(2,1)}, u32[]{:S(2)}) copy-start(bf16[1,4,1,64,256]{4,3,2,1,0:T(8,128)(2,1)} %param.7) | copy-start | bytes 393220
  8.1 14.8 %collective-permute-start = (bf16[128,256]{1,0:T(8,128)(2,1)S(1)}, bf16[128,256]{1,0:T(8,128)(2,1)S(1)}, u32[]{:S(2)}, u32[]{:S(2)}) collective-permute-start(bf16[128,256]{1,0:T(8,128)(2,1)S(1)} %dynamic-slice_bitcast_fusion), channel_id=1, source_target_pairs={{4,251},{8,247},{12,243},{16,239},{20,235},{21,234},{24,231},{25,2... | collective-permute-start | bytes 196616 | tf_op jit(solution)/shard_map/ppermute | solution.py:257
  24.6 22.2 %all-to-all-start = ((bf16[8,128,256]{2,1,0:T(8,128)(2,1)}), bf16[8,128,256]{2,1,0:T(8,128)(2,1)S(1)}, u32[]{:S(2)}, u32[]{:S(2)}) async-start(bf16[8,128,256]{2,1,0:T(8,128)(2,1)} %broadcast_in_dim.66), calls=%async_computation | async-start | bytes 1048576 | tf_op jit(solution)/shard_map/all_to_all | solution.py:264
  28.9 97.9 %all-gather.3.cloned.1.call-start = ((), (), s32[]{:S(2)}) async-start(), calls=%async_computation.2 | async-start | bytes 17301504 | tf_op jit(solution)/shard_map/all_gather | solution.py:277
  30.3 51.9 %copy-start.3 = (s32[1,1,64,1]{2,3,1,0:T(1,128)S(1)}, s32[1,1,64,1]{2,3,1,0:T(1,128)}, u32[]{:S(2)}) copy-start(s32[1,1,64,1]{2,3,1,0:T(1,128)} %param.10) | copy-start | bytes 772
  46.8 0.8 copy-start.5
  79.2 3.0 %collective-permute-start.1 = (bf16[8,4,64,256]{3,2,1,0:T(8,128)(2,1)S(1)}, bf16[8,4,64,256]{3,2,1,0:T(8,128)(2,1)S(1)}, u32[]{:S(2)}, u32[]{:S(2)}) collective-permute-start(bf16[8,4,64,256]{3,2,1,0:T(8,128)(2,1)S(1)} %all_to_all.10.mine_ref), channel_id=1, source_target_pairs={{0,4},{4,0},{1,5},{5,1},{2,6},{6,2},{3,7},{7,3},{8,12},{12,8},{9,1... | collective-permute-start | bytes 3145736 | tf_op jit(solution)/shard_map/ppermute | solution.py:282
  82.2 21.1 %copy-start.4 = (bf16[16,256,256]{2,1,0:T(8,128)(2,1)S(1)}, bf16[16,256,256]{2,1,0:T(8,128)(2,1)}, u32[]{:S(2)}) copy-start(bf16[16,256,256]{2,1,0:T(8,128)(2,1)} %param.12) | copy-start | bytes 6291460
  87.7 5.6 %collective-permute-start.3 = (bf16[64,256]{1,0:T(8,128)(2,1)S(1)}, bf16[64,256]{1,0:T(8,128)(2,1)S(1)}, u32[]{:S(2)}, u32[]{:S(2)}) collective-permute-start(bf16[64,256]{1,0:T(8,128)(2,1)S(1)} %convert_element_type.102), channel_id=1, source_target_pairs={{0,64},{64,128},{128,192},{192,0},{1,65},{65,129},{129,193},{193,1... | collective-permute-start | bytes 98312 | tf_op jit(solution)/shard_map/ppermute | solution.py:226
  87.8 5.5 %collective-permute-start.2 = (bf16[64,256]{1,0:T(8,128)(2,1)S(1)}, bf16[64,256]{1,0:T(8,128)(2,1)S(1)}, u32[]{:S(2)}, u32[]{:S(2)}) collective-permute-start(bf16[64,256]{1,0:T(8,128)(2,1)S(1)} %convert_element_type.102), channel_id=1, source_target_pairs={{0,128},{64,192},{128,0},{192,64},{1,129},{65,193},{129,1},{193,65... | collective-permute-start | bytes 98312 | tf_op jit(solution)/shard_map/ppermute | solution.py:226
  89.2 5.6 %collective-permute-start.4 = (bf16[64,256]{1,0:T(8,128)(2,1)S(1)}, bf16[64,256]{1,0:T(8,128)(2,1)S(1)}, u32[]{:S(2)}, u32[]{:S(2)}) collective-permute-start(bf16[64,256]{1,0:T(8,128)(2,1)S(1)} %convert_element_type.102), channel_id=1, source_target_pairs={{0,192},{64,0},{128,64},{192,128},{1,193},{65,1},{129,65},{193,129... | collective-permute-start | bytes 98312 | tf_op jit(solution)/shard_map/ppermute | solution.py:226
  94.8 32.0 %copy-start.1 = (bf16[16,64,256]{2,1,0:T(8,128)(2,1)S(1)}, bf16[16,64,256]{2,1,0:T(8,128)(2,1)}, u32[]{:S(2)}) copy-start(bf16[16,64,256]{2,1,0:T(8,128)(2,1)} %refs_3_.1) | copy-start | bytes 1572868
  94.8 8.8 %collective-permute-start.7 = (bf16[64,256]{1,0:T(8,128)(2,1)S(1)}, bf16[64,256]{1,0:T(8,128)(2,1)S(1)}, u32[]{:S(2)}, u32[]{:S(2)}) collective-permute-start(bf16[64,256]{1,0:T(8,128)(2,1)S(1)} %add_convert_fusion.3), channel_id=1, source_target_pairs={{0,3},{1,0},{2,1},{3,2},{4,7},{5,4},{6,5},{7,6},{8,11},{9,8},{10,9... | collective-permute-start | bytes 98312 | tf_op jit(solution)/shard_map/ppermute | solution.py:226
  102.0 5.3 %collective-permute-start.6 = (bf16[64,256]{1,0:T(8,128)(2,1)S(1)}, bf16[64,256]{1,0:T(8,128)(2,1)S(1)}, u32[]{:S(2)}, u32[]{:S(2)}) collective-permute-start(bf16[64,256]{1,0:T(8,128)(2,1)S(1)} %add_convert_fusion.3), channel_id=1, source_target_pairs={{0,1},{1,2},{2,3},{3,0},{4,5},{5,6},{6,7},{7,4},{8,9},{9,10},{10,1... | collective-permute-start | bytes 98312 | tf_op jit(solution)/shard_map/ppermute | solution.py:226
  102.0 5.3 %collective-permute-start.5 = (bf16[64,256]{1,0:T(8,128)(2,1)S(1)}, bf16[64,256]{1,0:T(8,128)(2,1)S(1)}, u32[]{:S(2)}, u32[]{:S(2)}) collective-permute-start(bf16[64,256]{1,0:T(8,128)(2,1)S(1)} %add_convert_fusion.3), channel_id=1, source_target_pairs={{0,2},{1,3},{2,0},{3,1},{4,6},{5,7},{6,4},{7,5},{8,10},{9,11},{10,... | collective-permute-start | bytes 98312 | tf_op jit(solution)/shard_map/ppermute | solution.py:226
  144.0 1.8 collective-permute-start.8
  146.0 12.3 %collective-permute-start.11 = (bf16[3,4,64,256]{3,2,1,0:T(8,128)(2,1)S(1)}, bf16[3,4,64,256]{3,2,1,0:T(8,128)(2,1)S(1)}, u32[]{:S(2)}, u32[]{:S(2)}) collective-permute-start(bf16[3,4,64,256]{3,2,1,0:T(8,128)(2,1)S(1)} %add_convert_fusion), channel_id=1, source_target_pairs={{0,16},{4,52},{8,24},{12,60},{16,32},{20,4},{24,40},{28,12},{32,48... | collective-permute-start | bytes 1179656 | tf_op jit(solution)/shard_map/ppermute | solution.py:315
  149.4 0.8 copy-start.2
  154.0 4.3 %collective-permute-start.10 = (bf16[2,4,64,256]{3,2,1,0:T(8,128)(2,1)S(1)}, bf16[2,4,64,256]{3,2,1,0:T(8,128)(2,1)S(1)}, u32[]{:S(2)}, u32[]{:S(2)}) collective-permute-start(bf16[2,4,64,256]{3,2,1,0:T(8,128)(2,1)S(1)} %get-tuple-element.26), channel_id=1, source_target_pairs={{0,4},{4,0},{1,5},{5,1},{2,6},{6,2},{3,7},{7,3},{8,12},{12,8},{9,1... | collective-permute-start | bytes 786440 | tf_op jit(solution)/shard_map/ppermute | solution.py:318
  154.1 4.3 %collective-permute-start.13 = (bf16[2,4,64,256]{3,2,1,0:T(8,128)(2,1)S(1)}, bf16[2,4,64,256]{3,2,1,0:T(8,128)(2,1)S(1)}, u32[]{:S(2)}, u32[]{:S(2)}) collective-permute-start(bf16[2,4,64,256]{3,2,1,0:T(8,128)(2,1)S(1)} %get-tuple-element.27), channel_id=1, source_target_pairs={{0,4},{4,0},{1,5},{5,1},{2,6},{6,2},{3,7},{7,3},{8,12},{12,8},{9,1... | collective-permute-start | bytes 786440 | tf_op jit(solution)/shard_map/ppermute | solution.py:318
  158.6 6.5 %collective-permute-start.12 = (bf16[2,4,64,256]{3,2,1,0:T(8,128)(2,1)S(1)}, bf16[2,4,64,256]{3,2,1,0:T(8,128)(2,1)S(1)}, u32[]{:S(2)}, u32[]{:S(2)}) collective-permute-start(bf16[2,4,64,256]{3,2,1,0:T(8,128)(2,1)S(1)} %get-tuple-element.24), channel_id=1, source_target_pairs={{0,8},{4,60},{8,16},{12,4},{16,24},{20,12},{24,32},{28,20},{32,40}... | collective-permute-start | bytes 786440 | tf_op jit(solution)/shard_map/ppermute | solution.py:324
  161.8 8.9 %collective-permute-start.14 = (bf16[2,4,64,256]{3,2,1,0:T(8,128)(2,1)S(1)}, bf16[2,4,64,256]{3,2,1,0:T(8,128)(2,1)S(1)}, u32[]{:S(2)}, u32[]{:S(2)}) collective-permute-start(bf16[2,4,64,256]{3,2,1,0:T(8,128)(2,1)S(1)} %get-tuple-element.25), channel_id=1, source_target_pairs={{0,16},{4,52},{8,24},{12,60},{16,32},{20,4},{24,40},{28,12},{32,48... | collective-permute-start | bytes 786440 | tf_op jit(solution)/shard_map/ppermute | solution.py:324
  163.0 10.4 %collective-permute-start.9 = (bf16[1,4,64,256]{3,2,1,0:T(8,128)(2,1)S(1)}, bf16[1,4,64,256]{3,2,1,0:T(8,128)(2,1)S(1)}, u32[]{:S(2)}, u32[]{:S(2)}) collective-permute-start(bf16[1,4,64,256]{3,2,1,0:T(8,128)(2,1)S(1)} %slice.46), channel_id=1, source_target_pairs={{0,4},{4,0},{1,5},{5,1},{2,6},{6,2},{3,7},{7,3},{8,12},{12,8},{9,1... | collective-permute-start | bytes 393224 | tf_op jit(solution)/shard_map/ppermute | solution.py:318
  170.8 3.6 %collective-permute-start.15 = (bf16[4,64,256]{2,1,0:T(8,128)(2,1)S(1)}, bf16[4,64,256]{2,1,0:T(8,128)(2,1)S(1)}, u32[]{:S(2)}, u32[]{:S(2)}) collective-permute-start(bf16[4,64,256]{2,1,0:T(8,128)(2,1)S(1)} %fusion.7), channel_id=1, source_target_pairs={{0,4},{4,0},{1,5},{5,1},{2,6},{6,2},{3,7},{7,3},{8,12},{12,8},{9,1... | collective-permute-start | bytes 393224 | tf_op jit(solution)/shard_map/ppermute | solution.py:329
Sparse Core Ops, SparseCore 0:
  47.8 78.2 all-gather.2

commit v6 on v5

--- a/solution.py
+++ b/solution.py
@@ -21,54 +21,51 @@
     ]
 
 
-def update_kernel(
-    at_ref, w_ref, mine_ref, other_ref, c_hbm, out_ref, coup_ref, sems
-):
-    chips, leaves = mine_ref.shape[:2]
-    per_chip = 2 * leaves
-    core = at_ref[1]
-
-    def fetch(chip):
-        piece = pl.ds(chip * per_chip, per_chip)
-        return pltpu.make_async_copy(
-            c_hbm.at[piece], coup_ref.at[piece], sems.at[chip]
-        )
-
-    for chip in range(chips):
-        fetch(chip).start()
+def update_kernel(base_ref, w_ref, *refs):
+    parts, (c_hbm, out_ref, coup, sems) = refs[:-4], refs[-4:]
+    fetch = group_fetches(base_ref, c_hbm, coup, sems)
+    for copy in fetch:
+        copy.start()
     total = None
-    for chip in range(chips):
-        fetch(chip).wait()
-        for rows, part in ((mine_ref, core), (other_ref, 1 - core)):
-            for leaf in range(leaves):
-                at = (2 * chip + part) * leaves + leaf
-                weight = w_ref[at].astype(F32)
+    i = 0
+    for part in parts:
+        for group in range(part.shape[0]):
+            fetch[i].wait()
+            for leaf in range(coup.shape[1]):
+                weight = w_ref[base_ref[i] + leaf].astype(F32)
                 term = weight * lax.dot_general(
-                    rows[chip, leaf], coup_ref[at], NT, preferred_element_type=F32
+                    part[group, leaf], coup[i, leaf], NT, preferred_element_type=F32
                 )
                 total = term if total is None else total + term
+            i += 1
     out_ref[...] = total
 
 
-def update_products(at, pattern, mine, other, coupled):
-    chips, leaves, nrhs, size = mine.shape
+def update_products(base, pattern, parts, coupled):
+    groups = base.shape[0]
+    leaves, nrhs, size = parts[0].shape[1:]
     whole = pl.BlockSpec(memory_space=pltpu.VMEM)
     scalars = pl.BlockSpec(memory_space=pltpu.SMEM)
     return pl.pallas_call(
         update_kernel,
         out_shape=jax.ShapeDtypeStruct((nrhs, size), F32),
         in_specs=[scalars] * 2
-        + [whole] * 2
+        + [whole] * len(parts)
         + [pl.BlockSpec(memory_space=pltpu.HBM)],
         out_specs=whole,
         scratch_shapes=[
-            pltpu.VMEM(coupled.shape, BF),
-            pltpu.SemaphoreType.DMA((chips,)),
+            pltpu.VMEM((groups, leaves, size, size), BF),
+            pltpu.SemaphoreType.DMA((groups,)),
         ],
         compiler_params=pltpu.CompilerParams(vmem_limit_bytes=16 << 20),
+        cost_estimate=pl.CostEstimate(
+            flops=2 * groups * leaves * nrhs * size * size,
+            bytes_accessed=2 * groups * leaves * size * (size + nrhs),
+            transcendentals=0,
+        ),
         name="update_products",
     )(
-        at, pattern, mine, other,
+        base, pattern, *parts,
         pltpu.with_memory_space_constraint(coupled, pltpu.HBM),
     )
 
@@ -89,10 +86,11 @@
 
 def group_products(own, base_ref, w_ref, fetch, coup, outs):
     leaves = coup.shape[1]
+    for copy in fetch:
+        copy.wait()
     i = 0
     for out in outs:
         for group in range(out.shape[0]):
-            fetch[i].wait()
             for leaf in range(leaves):
                 weight = w_ref[base_ref[i] + leaf].astype(F32)
                 value = lax.dot_general(
@@ -160,6 +158,9 @@
                     fac.at[first_block(a) + b, pl.ds(part * half, half)],
                     sems.at[a],
                 ).start()
+    fetch = group_fetches(base_ref, c_hbm, coup, coup_sems)
+    for copy in fetch:
+        copy.start()
 
     summed = rhs(0)
     for k in range(count):
@@ -172,9 +173,6 @@
             for b in range(k):
                 later -= dot(zs[b], block(k + 1, b), NT)
             summed = later - dot(z, block(k + 1, k), NT)
-    fetch = group_fetches(base_ref, c_hbm, coup, coup_sems)
-    for copy in fetch:
-        copy.start()
     summed = zs[count - 1].astype(F32)
     for k in reversed(range(count)):
         x = dot(summed.astype(BF), g_ref[k], NN).astype(BF)
@@ -273,19 +271,12 @@
         leaf_forward = jnp.einsum(
             "inb,idb->ind", own_rhs, own_inverse, preferred_element_type=F32
         ).astype(BF)
-        leaf_shared, ring = lax.optimization_barrier((leaf_forward, ring))
+        swapped = lax.ppermute(leaf_forward, "core", SWAP)
+        shared, ring = lax.optimization_barrier(
+            (jnp.stack([leaf_forward, swapped]), ring)
+        )
+        ring = pltpu.with_memory_space_constraint(ring, pltpu.HBM)
         factor = lax.all_gather(ring, ("sub", "col", "core"), axis=0, tiled=True)
-        mine = lax.all_to_all(
-            jnp.broadcast_to(leaf_shared[None], (zs,) + leaf_forward.shape),
-            "z", 0, 0, tiled=True,
-        )
-        other = lax.ppermute(mine, "core", SWAP)
-        at = jnp.stack([row, core])
-        present = pattern[0, 0, :, 0]
-        partial = update_products(at, present, mine, other, coupled)
-        update = sum_over(sum_over(partial, "sub", subs), "col", cols).astype(BF)
-        updates = lax.all_gather(update, ROW, axis=0)
-
         chip = lax.axis_index("z")
         turn = 1 - 2 * core
         other_core = 1 - core
@@ -296,6 +287,30 @@
                 for away, part in groups
             ]
             return jnp.stack(starts).astype(jnp.int32)
+
+        at = jnp.stack([row, core])
+        present = pattern[0, 0, :, 0]
+        one = lax.ppermute(shared, ROW, hop(zs, 1))
+        two = lax.ppermute(shared, ROW, hop(zs, 2))
+        far = lax.ppermute(jnp.concatenate([one, two[:1]]), ROW, hop(zs, 2))
+        early = [shared, one, two] + [
+            lax.ppermute(part, "core", SWAP) for part in (one, two)
+        ]
+        late = [far] + [
+            lax.ppermute(part, "core", SWAP) for part in (far[:2], far[2:])
+        ]
+        own, opp = core, other_core
+        early_base = base(
+            [(0, own), (0, opp), (-1, own), (-1, opp), (-2, own), (-2, opp)]
+            + [(1, opp), (1, own), (2, opp), (2, own)]
+        )
+        late_base = base(
+            [(-3, own), (-3, opp), (4, own), (3, opp), (3, own), (4, opp)]
+        )
+        partial = update_products(early_base, present, early, coupled)
+        partial += update_products(late_base, present, late, coupled)
+        update = sum_over(sum_over(partial, "sub", subs), "col", cols).astype(BF)
+        updates = lax.all_gather(update, ROW, axis=0)
 
         far_base = base(
             [(-3, 0), (-3, 1), (4, other_core), (3, 0), (3, 1), (4, core)]

time: 184 us -> 182 us (0.989)
  blocking collectives: 50.8 us -> 18.1 us
  starting transfers between devices: 41.2 us -> 56.2 us
  waiting for transfers between devices: 41.7 us -> 56.2 us
    all_to_all x1 -> x0, blocking collectives: 31.4 us -> none  [local(): lax.all_to_all(jnp.broadcast_to(leaf_shared[None], (zs,) + leaf_forward.s...]
    ppermute x1 -> x8, waiting for transfers between devices: 2.21 us -> 15.9 us  [the longest x1 6.56 us: local(): far = lax.ppermute(jnp.concatenate([one, two[:1]]), ROW, hop(zs, 2))]
    ppermute x1 -> x8, starting transfers between devices: 0.72 us -> 13.8 us  [the longest x4 12.3 us: local(): lax.ppermute(part, 'core', SWAP)]
    all_gather x1, waiting for transfers between devices: 0.01 us -> 4.86 us  [local(): factor = lax.all_gather(ring, ('sub', 'col', 'core'), axis=0, tiled=True)]
    pallas_call x1 -> x2, Pallas kernels: 5.49 us -> 7.95 us  [update_products(): pl.pallas_call(update_kernel, out_shape=jax.ShapeDtypeStruct((nrhs, size)...]
    all_to_all x1, waiting for transfers between devices: 16.5 us -> 14.6 us  [local(): ring = lax.all_to_all(unit, 'z', 0, 0, tiled=True)]
  transfers between devices with their start and end apart: 18 -> 25, of which waited for: 11 -> 17; matrix products, arithmetic and copies ran while one was open for 1% -> 1% of each run, Pallas kernels for 5% -> 7%
where the time goes in v6:
time: 182 us
  starting transfers between devices  56.2 us (31%)
  waiting for transfers between devices  56.2 us (31%)
  Pallas kernels  28 us (15%)
  blocking collectives  18.1 us (10%)
  between operations  14.4 us (8%)
  local copies, waits for them, and re-layouts  3.74 us (2%)
  matrix products  3.29 us (2%)
    all_gather x1, blocking collectives, local(): updates = lax.all_gather(update, ROW, axis=0)  18.1 us
    pallas_call x1, Pallas kernels, top_solve(): pl.pallas_call(lambda *refs: top_kernel(units, *refs), out_shape=(jax.Sha...  15.9 us
    all_to_all x1, waiting for transfers between devices, local(): ring = lax.all_to_all(unit, 'z', 0, 0, tiled=True)  14.6 us
    ppermute x1, starting transfers between devices, local(): moved = lax.ppermute(block[half:], ('sub', 'z', 'core', 'col'), pairs)  13.5 us
    ppermute x4, starting transfers between devices, local(): lax.ppermute(part, 'core', SWAP)  12.3 us
    ppermute x6, starting transfers between devices, sum_over(): lax.ppermute(value, axis, [(i, (i + k) % size) for i in range(size)])  11.2 us
    pallas_call x2, Pallas kernels, update_products(): pl.pallas_call(update_kernel, out_shape=jax.ShapeDtypeStruct((nrhs, size)...  7.95 us
    ppermute x6, waiting for transfers between devices, sum_over(): lax.ppermute(value, axis, [(i, (i + k) % size) for i in range(size)])  7.91 us
  transfers between devices with their start and end apart: 25, of which 17 were waited for; matrix products, arithmetic and copies ran while one was open for 1% of the time, Pallas kernels for 7%

profile of v6, /device:TPU:1, one launch (start us, length us, event | category | flops | bytes accessed | tf_op | source)
XLA Modules:
  0.0 181.7 jit_solution(8939194794958985610)
XLA Ops:
  8.1 13.5 %collective-permute-start.1 = (bf16[128,256]{1,0:T(8,128)(2,1)S(1)}, bf16[128,256]{1,0:T(8,128)(2,1)S(1)}, u32[]{:S(2)}, u32[]{:S(2)}) collective-permute-start(bf16[128,256]{1,0:T(8,128)(2,1)S(1)} %dynamic-slice_bitcast_fusion), channel_id=1, source_target_pairs={{4,251},{8,247},{12,243},{16,239},{20,235},{21,234},{24,231},{25,2... | collective-permute-start | bytes 196616 | tf_op jit(solution)/shard_map/ppermute | solution.py:255
  24.6 4.3 %all-to-all-start = ((bf16[8,128,256]{2,1,0:T(8,128)(2,1)}), bf16[8,128,256]{2,1,0:T(8,128)(2,1)S(1)}, u32[]{:S(2)}, u32[]{:S(2)}) async-start(bf16[8,128,256]{2,1,0:T(8,128)(2,1)} %broadcast_in_dim.60), calls=%async_computation | async-start | bytes 1048576 | tf_op jit(solution)/shard_map/all_to_all | solution.py:262
  32.2 14.6 %all-to-all-done = bf16[8,128,256]{2,1,0:T(8,128)(2,1)S(1)} async-done(((bf16[8,128,256]{2,1,0:T(8,128)(2,1)}), bf16[8,128,256]{2,1,0:T(8,128)(2,1)S(1)}, u32[]{:S(2)}, u32[]{:S(2)}) %all-to-all-start) | async-done | bytes 524320 | tf_op jit(solution)/shard_map/all_to_all | solution.py:262
  47.8 6.4 %collective-permute-done.3.refs_2_ = bf16[2,4,64,256]{3,2,1,0:T(8,128)(2,1)S(1)} collective-permute-done((bf16[2,4,64,256]{3,2,1,0:T(8,128)(2,1)S(1)}, bf16[2,4,64,256]{3,2,1,0:T(8,128)(2,1)S(1)}, u32[]{:S(2)}, u32[]{:S(2)}) %collective-permute-start.3) | collective-permute-done | bytes 262176 | tf_op jit(solution)/shard_map/ppermute | solution.py:294
  54.2 1.9 %collective-permute-done.2.refs_1_ = bf16[2,4,64,256]{3,2,1,0:T(8,128)(2,1)S(1)} collective-permute-done((bf16[2,4,64,256]{3,2,1,0:T(8,128)(2,1)S(1)}, bf16[2,4,64,256]{3,2,1,0:T(8,128)(2,1)S(1)}, u32[]{:S(2)}, u32[]{:S(2)}) %collective-permute-start.2) | collective-permute-done | bytes 262176 | tf_op jit(solution)/shard_map/ppermute | solution.py:293
  56.5 5.1 %collective-permute-start.5 = (bf16[2,4,64,256]{3,2,1,0:T(8,128)(2,1)S(1)}, bf16[2,4,64,256]{3,2,1,0:T(8,128)(2,1)S(1)}, u32[]{:S(2)}, u32[]{:S(2)}) collective-permute-start(bf16[2,4,64,256]{3,2,1,0:T(8,128)(2,1)S(1)} %collective-permute-done.3.refs_2_), channel_id=1, source_target_pairs={{0,4},{4,0},{1,5},{5,1},{2,6},{6,2},{3,7},{7,3},{8,12},{12,8},{9,1... | collective-permute-start | bytes 786440 | tf_op jit(solution)/shard_map/ppermute | solution.py:297
  61.7 6.6 %collective-permute-done.6.refs_0_ = bf16[3,4,64,256]{3,2,1,0:T(8,128)(2,1)S(1)} collective-permute-done((bf16[3,4,64,256]{3,2,1,0:T(8,128)(2,1)S(1)}, bf16[3,4,64,256]{3,2,1,0:T(8,128)(2,1)S(1)}, u32[]{:S(2)}, u32[]{:S(2)}) %collective-permute-start.6) | collective-permute-done | bytes 393248 | tf_op jit(solution)/shard_map/ppermute | solution.py:295
  68.3 7.0 %collective-permute-start.7 = (bf16[2,4,64,256]{3,2,1,0:T(8,128)(2,1)S(1)}, bf16[2,4,64,256]{3,2,1,0:T(8,128)(2,1)S(1)}, u32[]{:S(2)}, u32[]{:S(2)}) collective-permute-start(bf16[2,4,64,256]{3,2,1,0:T(8,128)(2,1)S(1)} %slice.68), channel_id=1, source_target_pairs={{0,4},{4,0},{1,5},{5,1},{2,6},{6,2},{3,7},{7,3},{8,12},{12,8},{9,1... | collective-permute-start | bytes 786440 | tf_op jit(solution)/shard_map/ppermute | solution.py:300
  75.7 4.5 %update_products.2 = f32[64,256]{1,0:T(8,128)S(1)} custom-call(s32[10]{0:T(128)S(1)} %stack.147.base_ref, s32[64]{0:T(128)S(1)} %bitcast.72, bf16[2,4,64,256]{3,2,1,0:T(8,128)(2,1)S(1)} %pad_maximum_fusion.1.refs_0_, bf16[2,4,64,256]{3,2,1,0:T(8,128)(2,1)S(1)} %collective-permute-done.2.refs_1_, bf16[2,4,64,256]{3,2,1,0:T(8,128)(2,1)S(1)} %collective-permute-done.3.refs_2_, ...), custom_call_target="tpu_custom_call" | custom-call | flops 335544320 | bytes 6553600 | tf_op jit(solution)/shard_map/update_products/pallas_call | solution.py:49
  80.3 3.4 %update_products.3 = f32[64,256]{1,0:T(8,128)S(1)} custom-call(s32[6]{0:T(128)S(1)} %stack.155.base_ref, s32[64]{0:T(128)S(1)} %bitcast.73, bf16[3,4,64,256]{3,2,1,0:T(8,128)(2,1)S(1)} %collective-permute-done.6.refs_0_, bf16[2,4,64,256]{3,2,1,0:T(8,128)(2,1)S(1)} %collective-permute-done.7.refs_1_, ...), custom_call_target="tpu_custom_call" | custom-call | flops 201326592 | bytes 3932160 | tf_op jit(solution)/shard_map/update_products/pallas_call | solution.py:49
  88.0 2.0 %collective-permute-done.9 = bf16[64,256]{1,0:T(8,128)(2,1)S(1)} collective-permute-done((bf16[64,256]{1,0:T(8,128)(2,1)S(1)}, bf16[64,256]{1,0:T(8,128)(2,1)S(1)}, u32[]{:S(2)}, u32[]{:S(2)}) %collective-permute-start.9) | collective-permute-done | bytes 32800 | tf_op jit(solution)/shard_map/ppermute | solution.py:224
  90.0 7.8 %collective-permute-start.14 = (bf16[64,256]{1,0:T(8,128)(2,1)S(1)}, bf16[64,256]{1,0:T(8,128)(2,1)S(1)}, u32[]{:S(2)}, u32[]{:S(2)}) collective-permute-start(bf16[64,256]{1,0:T(8,128)(2,1)S(1)} %add_convert_fusion.3), channel_id=1, source_target_pairs={{0,3},{1,0},{2,1},{3,2},{4,7},{5,4},{6,5},{7,6},{8,11},{9,8},{10,9... | collective-permute-start | bytes 98312 | tf_op jit(solution)/shard_map/ppermute | solution.py:224
  99.4 3.8 %collective-permute-done.13 = bf16[64,256]{1,0:T(8,128)(2,1)S(1)} collective-permute-done((bf16[64,256]{1,0:T(8,128)(2,1)S(1)}, bf16[64,256]{1,0:T(8,128)(2,1)S(1)}, u32[]{:S(2)}, u32[]{:S(2)}) %collective-permute-start.13) | collective-permute-done | bytes 32800 | tf_op jit(solution)/shard_map/ppermute | solution.py:224
  103.2 18.1 %all-gather = bf16[1024,256]{1,0:T(8,128)(2,1)S(1)} all-gather(bf16[64,256]{1,0:T(8,128)(2,1)S(1)} %add_convert_fusion.2), channel_id=2, replica_groups=mesh['sub'=4,'z'=8,'core'=2,'col'=4] {'z','core'}, dimensions={0}, use_global_device_ids=true | all-gather | bytes 557056 | tf_op jit(solution)/shard_map/all_gather | solution.py:313
  121.4 4.9 %all-gather.3.cloned.1.call-done.refs_6_ = bf16[256,128,256]{2,1,0:T(8,128)(2,1)} async-done(((bf16[8,128,256]{2,1,0:T(8,128)(2,1)}), bf16[256,128,256]{2,1,0:T(8,128)(2,1)}) %all-gather.3.cloned.1.call-update) | async-done | bytes 16777232 | tf_op jit(solution)/shard_map/all_gather | solution.py:279
  126.2 15.9 %top_solve.1 = (bf16[64,256]{1,0:T(8,128)(2,1)}, bf16[3,4,64,256]{3,2,1,0:T(8,128)(2,1)S(1)}, bf16[3,4,64,256]{3,2,1,0:T(8,128)(2,1)S(1)}) custom-call(s32[2]{0:T(128)S(1)} %pad_add_fusion.refs_0_, s32[6]{0:T(128)S(1)} %stack.138.refs_1_, s32[64]{0:T(128)S(1)} %bitcast.74, bf16[16,64,256]{2,1,0:T(8,128)(2,1)S(1)} %copy-done.1, ...), custom_call_target="tpu_custom_call" | custom-call | tf_op jit(solution)/shard_map/top_solve/pallas_call | solution.py:197
  144.1 3.9 %collective-permute-start.18 = (bf16[3,4,64,256]{3,2,1,0:T(8,128)(2,1)S(1)}, bf16[3,4,64,256]{3,2,1,0:T(8,128)(2,1)S(1)}, u32[]{:S(2)}, u32[]{:S(2)}) collective-permute-start(bf16[3,4,64,256]{3,2,1,0:T(8,128)(2,1)S(1)} %add_convert_fusion), channel_id=1, source_target_pairs={{0,16},{4,52},{8,24},{12,60},{16,32},{20,4},{24,40},{28,12},{32,48... | collective-permute-start | bytes 1179656 | tf_op jit(solution)/shard_map/ppermute | solution.py:330
  148.9 4.1 %near_products.1 = (bf16[5,4,64,256]{3,2,1,0:T(8,128)(2,1)S(1)}, bf16[5,4,64,256]{3,2,1,0:T(8,128)(2,1)S(1)}) custom-call(s32[10]{0:T(128)S(1)} %stack.128.base_ref, s32[64]{0:T(128)S(1)} %bitcast.75, bf16[64,256]{1,0:T(8,128)(2,1)S(1)} %copy-done.2, bf16[64,256,256]{2,1,0:T(8,128)(2,1)} %bitcast.79), custom_call_target="tpu_custom_call" | custom-call | flops 335544320 | bytes 6553600 | tf_op jit(solution)/shard_map/near_products/pallas_call | solution.py:118
  153.6 3.3 %collective-permute-done.18 = bf16[3,4,64,256]{3,2,1,0:T(8,128)(2,1)S(1)} collective-permute-done((bf16[3,4,64,256]{3,2,1,0:T(8,128)(2,1)S(1)}, bf16[3,4,64,256]{3,2,1,0:T(8,128)(2,1)S(1)}, u32[]{:S(2)}, u32[]{:S(2)}) %collective-permute-start.18) | collective-permute-done | bytes 393248 | tf_op jit(solution)/shard_map/ppermute | solution.py:330
  157.3 2.3 %collective-permute-start.19 = (bf16[2,4,64,256]{3,2,1,0:T(8,128)(2,1)S(1)}, bf16[2,4,64,256]{3,2,1,0:T(8,128)(2,1)S(1)}, u32[]{:S(2)}, u32[]{:S(2)}) collective-permute-start(bf16[2,4,64,256]{3,2,1,0:T(8,128)(2,1)S(1)} %get-tuple-element.24), channel_id=1, source_target_pairs={{0,8},{4,60},{8,16},{12,4},{16,24},{20,12},{24,32},{28,20},{32,40}... | collective-permute-start | bytes 786440 | tf_op jit(solution)/shard_map/ppermute | solution.py:339
  159.6 1.9 %collective-permute-start.21 = (bf16[2,4,64,256]{3,2,1,0:T(8,128)(2,1)S(1)}, bf16[2,4,64,256]{3,2,1,0:T(8,128)(2,1)S(1)}, u32[]{:S(2)}, u32[]{:S(2)}) collective-permute-start(bf16[2,4,64,256]{3,2,1,0:T(8,128)(2,1)S(1)} %get-tuple-element.25), channel_id=1, source_target_pairs={{0,16},{4,52},{8,24},{12,60},{16,32},{20,4},{24,40},{28,12},{32,48... | collective-permute-start | bytes 786440 | tf_op jit(solution)/shard_map/ppermute | solution.py:339
  163.0 4.9 %collective-permute-done.21 = bf16[2,4,64,256]{3,2,1,0:T(8,128)(2,1)S(1)} collective-permute-done((bf16[2,4,64,256]{3,2,1,0:T(8,128)(2,1)S(1)}, bf16[2,4,64,256]{3,2,1,0:T(8,128)(2,1)S(1)}, u32[]{:S(2)}, u32[]{:S(2)}) %collective-permute-start.21) | collective-permute-done | bytes 262176 | tf_op jit(solution)/shard_map/ppermute | solution.py:339
  168.0 3.9 %collective-permute-start.22 = (bf16[4,64,256]{2,1,0:T(8,128)(2,1)S(1)}, bf16[4,64,256]{2,1,0:T(8,128)(2,1)S(1)}, u32[]{:S(2)}, u32[]{:S(2)}) collective-permute-start(bf16[4,64,256]{2,1,0:T(8,128)(2,1)S(1)} %fusion.6), channel_id=1, source_target_pairs={{0,4},{4,0},{1,5},{5,1},{2,6},{6,2},{3,7},{7,3},{8,12},{12,8},{9,1... | collective-permute-start | bytes 393224 | tf_op jit(solution)/shard_map/ppermute | solution.py:344
  172.9 2.0 %fusion = bf16[1,4,1,64,256]{4,3,2,1,0:T(8,128)(2,1)} fusion(bf16[1,4,1,256,256]{4,3,2,1,0:T(8,128)(2,1)} %param.8, pred[256,256]{1,0:T(8,128)(4,1)S(1)} %iota_compare_fusion, bf16[4,64,256]{2,1,0:T(8,128)(2,1)S(1)} %collective-permute-done.22, bf16[1,4,64,256]{3,2,1,0:T(8,128)(2,1)S(1)} %collective-permute-done.16, ...), kind=kOutput, calls=%fused_computation.3 | convolution fusion | flops 34537472 | bytes 1769473 | tf_op jit(solution)/shard_map/inb,ibd->ind/dot_general | solution.py:347
  (73 shorter events, 21.1 us)
Async XLA Ops:
  8.1 14.8 %collective-permute-start.1 = (bf16[128,256]{1,0:T(8,128)(2,1)S(1)}, bf16[128,256]{1,0:T(8,128)(2,1)S(1)}, u32[]{:S(2)}, u32[]{:S(2)}) collective-permute-start(bf16[128,256]{1,0:T(8,128)(2,1)S(1)} %dynamic-slice_bitcast_fusion), channel_id=1, source_target_pairs={{4,251},{8,247},{12,243},{16,239},{20,235},{21,234},{24,231},{25,2... | collective-permute-start | bytes 196616 | tf_op jit(solution)/shard_map/ppermute | solution.py:255
  24.6 22.2 %all-to-all-start = ((bf16[8,128,256]{2,1,0:T(8,128)(2,1)}), bf16[8,128,256]{2,1,0:T(8,128)(2,1)S(1)}, u32[]{:S(2)}, u32[]{:S(2)}) async-start(bf16[8,128,256]{2,1,0:T(8,128)(2,1)} %broadcast_in_dim.60), calls=%async_computation | async-start | bytes 1048576 | tf_op jit(solution)/shard_map/all_to_all | solution.py:262
  28.8 97.4 %all-gather.3.cloned.1.call-start = ((), (), s32[]{:S(2)}) async-start(), calls=%async_computation.1 | async-start | bytes 17301504 | tf_op jit(solution)/shard_map/all_gather | solution.py:279
  30.3 1.9 %collective-permute-start = (bf16[4,64,256]{2,1,0:T(8,128)(2,1)S(1)}, bf16[4,64,256]{2,1,0:T(8,128)(2,1)S(1)}, u32[]{:S(2)}, u32[]{:S(2)}) collective-permute-start(bf16[4,64,256]{2,1,0:T(8,128)(2,1)S(1)} %bitcast.80), channel_id=1, source_target_pairs={{0,4},{4,0},{1,5},{5,1},{2,6},{6,2},{3,7},{7,3},{8,12},{12,8},{9,1... | collective-permute-start | bytes 393224 | tf_op jit(solution)/shard_map/ppermute | solution.py:274
  47.6 6.5 %collective-permute-start.3 = (bf16[2,4,64,256]{3,2,1,0:T(8,128)(2,1)S(1)}, bf16[2,4,64,256]{3,2,1,0:T(8,128)(2,1)S(1)}, u32[]{:S(2)}, u32[]{:S(2)}) collective-permute-start(bf16[2,4,64,256]{3,2,1,0:T(8,128)(2,1)S(1)} %pad_maximum_fusion.1.refs_0_), channel_id=1, source_target_pairs={{0,16},{4,52},{8,24},{12,60},{16,32},{20,4},{24,40},{28,12},{32,48... | collective-permute-start | bytes 786440 | tf_op jit(solution)/shard_map/ppermute | solution.py:294
  47.7 8.4 %collective-permute-start.2 = (bf16[2,4,64,256]{3,2,1,0:T(8,128)(2,1)S(1)}, bf16[2,4,64,256]{3,2,1,0:T(8,128)(2,1)S(1)}, u32[]{:S(2)}, u32[]{:S(2)}) collective-permute-start(bf16[2,4,64,256]{3,2,1,0:T(8,128)(2,1)S(1)} %pad_maximum_fusion.1.refs_0_), channel_id=1, source_target_pairs={{0,8},{4,60},{8,16},{12,4},{16,24},{20,12},{24,32},{28,20},{32,40}... | collective-permute-start | bytes 786440 | tf_op jit(solution)/shard_map/ppermute | solution.py:293
  56.1 12.1 %collective-permute-start.6 = (bf16[3,4,64,256]{3,2,1,0:T(8,128)(2,1)S(1)}, bf16[3,4,64,256]{3,2,1,0:T(8,128)(2,1)S(1)}, u32[]{:S(2)}, u32[]{:S(2)}) collective-permute-start(bf16[3,4,64,256]{3,2,1,0:T(8,128)(2,1)S(1)} %pad_maximum_fusion), channel_id=1, source_target_pairs={{0,16},{4,52},{8,24},{12,60},{16,32},{20,4},{24,40},{28,12},{32,48... | collective-permute-start | bytes 1179656 | tf_op jit(solution)/shard_map/ppermute | solution.py:295
  56.5 19.2 %collective-permute-start.5 = (bf16[2,4,64,256]{3,2,1,0:T(8,128)(2,1)S(1)}, bf16[2,4,64,256]{3,2,1,0:T(8,128)(2,1)S(1)}, u32[]{:S(2)}, u32[]{:S(2)}) collective-permute-start(bf16[2,4,64,256]{3,2,1,0:T(8,128)(2,1)S(1)} %collective-permute-done.3.refs_2_), channel_id=1, source_target_pairs={{0,4},{4,0},{1,5},{5,1},{2,6},{6,2},{3,7},{7,3},{8,12},{12,8},{9,1... | collective-permute-start | bytes 786440 | tf_op jit(solution)/shard_map/ppermute | solution.py:297
  61.6 14.1 %collective-permute-start.4 = (bf16[2,4,64,256]{3,2,1,0:T(8,128)(2,1)S(1)}, bf16[2,4,64,256]{3,2,1,0:T(8,128)(2,1)S(1)}, u32[]{:S(2)}, u32[]{:S(2)}) collective-permute-start(bf16[2,4,64,256]{3,2,1,0:T(8,128)(2,1)S(1)} %collective-permute-done.2.refs_1_), channel_id=1, source_target_pairs={{0,4},{4,0},{1,5},{5,1},{2,6},{6,2},{3,7},{7,3},{8,12},{12,8},{9,1... | collective-permute-start | bytes 786440 | tf_op jit(solution)/shard_map/ppermute | solution.py:297
  68.3 12.0 %collective-permute-start.7 = (bf16[2,4,64,256]{3,2,1,0:T(8,128)(2,1)S(1)}, bf16[2,4,64,256]{3,2,1,0:T(8,128)(2,1)S(1)}, u32[]{:S(2)}, u32[]{:S(2)}) collective-permute-start(bf16[2,4,64,256]{3,2,1,0:T(8,128)(2,1)S(1)} %slice.68), channel_id=1, source_target_pairs={{0,4},{4,0},{1,5},{5,1},{2,6},{6,2},{3,7},{7,3},{8,12},{12,8},{9,1... | collective-permute-start | bytes 786440 | tf_op jit(solution)/shard_map/ppermute | solution.py:300
  75.3 5.0 %collective-permute-start.8 = (bf16[1,4,64,256]{3,2,1,0:T(8,128)(2,1)S(1)}, bf16[1,4,64,256]{3,2,1,0:T(8,128)(2,1)S(1)}, u32[]{:S(2)}, u32[]{:S(2)}) collective-permute-start(bf16[1,4,64,256]{3,2,1,0:T(8,128)(2,1)S(1)} %slice.69), channel_id=1, source_target_pairs={{0,4},{4,0},{1,5},{5,1},{2,6},{6,2},{3,7},{7,3},{8,12},{12,8},{9,1... | collective-permute-start | bytes 393224 | tf_op jit(solution)/shard_map/ppermute | solution.py:300
  83.8 2.8 %collective-permute-start.11 = (bf16[64,256]{1,0:T(8,128)(2,1)S(1)}, bf16[64,256]{1,0:T(8,128)(2,1)S(1)}, u32[]{:S(2)}, u32[]{:S(2)}) collective-permute-start(bf16[64,256]{1,0:T(8,128)(2,1)S(1)} %add_convert_fusion.4), channel_id=1, source_target_pairs={{0,192},{64,0},{128,64},{192,128},{1,193},{65,1},{129,65},{193,129... | collective-permute-start | bytes 98312 | tf_op jit(solution)/shard_map/ppermute | solution.py:224
  84.0 4.0 %collective-permute-start.10 = (bf16[64,256]{1,0:T(8,128)(2,1)S(1)}, bf16[64,256]{1,0:T(8,128)(2,1)S(1)}, u32[]{:S(2)}, u32[]{:S(2)}) collective-permute-start(bf16[64,256]{1,0:T(8,128)(2,1)S(1)} %add_convert_fusion.4), channel_id=1, source_target_pairs={{0,64},{64,128},{128,192},{192,0},{1,65},{65,129},{129,193},{193,1... | collective-permute-start | bytes 98312 | tf_op jit(solution)/shard_map/ppermute | solution.py:224
  85.3 4.7 %collective-permute-start.9 = (bf16[64,256]{1,0:T(8,128)(2,1)S(1)}, bf16[64,256]{1,0:T(8,128)(2,1)S(1)}, u32[]{:S(2)}, u32[]{:S(2)}) collective-permute-start(bf16[64,256]{1,0:T(8,128)(2,1)S(1)} %add_convert_fusion.4), channel_id=1, source_target_pairs={{0,128},{64,192},{128,0},{192,64},{1,129},{65,193},{129,1},{193,65... | collective-permute-start | bytes 98312 | tf_op jit(solution)/shard_map/ppermute | solution.py:224
  90.0 9.4 %collective-permute-start.14 = (bf16[64,256]{1,0:T(8,128)(2,1)S(1)}, bf16[64,256]{1,0:T(8,128)(2,1)S(1)}, u32[]{:S(2)}, u32[]{:S(2)}) collective-permute-start(bf16[64,256]{1,0:T(8,128)(2,1)S(1)} %add_convert_fusion.3), channel_id=1, source_target_pairs={{0,3},{1,0},{2,1},{3,2},{4,7},{5,4},{6,5},{7,6},{8,11},{9,8},{10,9... | collective-permute-start | bytes 98312 | tf_op jit(solution)/shard_map/ppermute | solution.py:224
  97.9 5.3 %collective-permute-start.13 = (bf16[64,256]{1,0:T(8,128)(2,1)S(1)}, bf16[64,256]{1,0:T(8,128)(2,1)S(1)}, u32[]{:S(2)}, u32[]{:S(2)}) collective-permute-start(bf16[64,256]{1,0:T(8,128)(2,1)S(1)} %add_convert_fusion.3), channel_id=1, source_target_pairs={{0,1},{1,2},{2,3},{3,0},{4,5},{5,6},{6,7},{7,4},{8,9},{9,10},{10,1... | collective-permute-start | bytes 98312 | tf_op jit(solution)/shard_map/ppermute | solution.py:224
  97.9 5.3 %collective-permute-start.12 = (bf16[64,256]{1,0:T(8,128)(2,1)S(1)}, bf16[64,256]{1,0:T(8,128)(2,1)S(1)}, u32[]{:S(2)}, u32[]{:S(2)}) collective-permute-start(bf16[64,256]{1,0:T(8,128)(2,1)S(1)} %add_convert_fusion.3), channel_id=1, source_target_pairs={{0,2},{1,3},{2,0},{3,1},{4,6},{5,7},{6,4},{7,5},{8,10},{9,11},{10,... | collective-permute-start | bytes 98312 | tf_op jit(solution)/shard_map/ppermute | solution.py:224
  144.1 12.9 %collective-permute-start.18 = (bf16[3,4,64,256]{3,2,1,0:T(8,128)(2,1)S(1)}, bf16[3,4,64,256]{3,2,1,0:T(8,128)(2,1)S(1)}, u32[]{:S(2)}, u32[]{:S(2)}) collective-permute-start(bf16[3,4,64,256]{3,2,1,0:T(8,128)(2,1)S(1)} %add_convert_fusion), channel_id=1, source_target_pairs={{0,16},{4,52},{8,24},{12,60},{16,32},{20,4},{24,40},{28,12},{32,48... | collective-permute-start | bytes 1179656 | tf_op jit(solution)/shard_map/ppermute | solution.py:330
  153.0 4.0 %collective-permute-start.17 = (bf16[2,4,64,256]{3,2,1,0:T(8,128)(2,1)S(1)}, bf16[2,4,64,256]{3,2,1,0:T(8,128)(2,1)S(1)}, u32[]{:S(2)}, u32[]{:S(2)}) collective-permute-start(bf16[2,4,64,256]{3,2,1,0:T(8,128)(2,1)S(1)} %get-tuple-element.26), channel_id=1, source_target_pairs={{0,4},{4,0},{1,5},{5,1},{2,6},{6,2},{3,7},{7,3},{8,12},{12,8},{9,1... | collective-permute-start | bytes 786440 | tf_op jit(solution)/shard_map/ppermute | solution.py:333
  153.1 3.9 %collective-permute-start.20 = (bf16[2,4,64,256]{3,2,1,0:T(8,128)(2,1)S(1)}, bf16[2,4,64,256]{3,2,1,0:T(8,128)(2,1)S(1)}, u32[]{:S(2)}, u32[]{:S(2)}) collective-permute-start(bf16[2,4,64,256]{3,2,1,0:T(8,128)(2,1)S(1)} %get-tuple-element.27), channel_id=1, source_target_pairs={{0,4},{4,0},{1,5},{5,1},{2,6},{6,2},{3,7},{7,3},{8,12},{12,8},{9,1... | collective-permute-start | bytes 786440 | tf_op jit(solution)/shard_map/ppermute | solution.py:333
  157.3 5.6 %collective-permute-start.19 = (bf16[2,4,64,256]{3,2,1,0:T(8,128)(2,1)S(1)}, bf16[2,4,64,256]{3,2,1,0:T(8,128)(2,1)S(1)}, u32[]{:S(2)}, u32[]{:S(2)}) collective-permute-start(bf16[2,4,64,256]{3,2,1,0:T(8,128)(2,1)S(1)} %get-tuple-element.24), channel_id=1, source_target_pairs={{0,8},{4,60},{8,16},{12,4},{16,24},{20,12},{24,32},{28,20},{32,40}... | collective-permute-start | bytes 786440 | tf_op jit(solution)/shard_map/ppermute | solution.py:339
  159.6 8.3 %collective-permute-start.21 = (bf16[2,4,64,256]{3,2,1,0:T(8,128)(2,1)S(1)}, bf16[2,4,64,256]{3,2,1,0:T(8,128)(2,1)S(1)}, u32[]{:S(2)}, u32[]{:S(2)}) collective-permute-start(bf16[2,4,64,256]{3,2,1,0:T(8,128)(2,1)S(1)} %get-tuple-element.25), channel_id=1, source_target_pairs={{0,16},{4,52},{8,24},{12,60},{16,32},{20,4},{24,40},{28,12},{32,48... | collective-permute-start | bytes 786440 | tf_op jit(solution)/shard_map/ppermute | solution.py:339
  161.5 10.4 %collective-permute-start.16 = (bf16[1,4,64,256]{3,2,1,0:T(8,128)(2,1)S(1)}, bf16[1,4,64,256]{3,2,1,0:T(8,128)(2,1)S(1)}, u32[]{:S(2)}, u32[]{:S(2)}) collective-permute-start(bf16[1,4,64,256]{3,2,1,0:T(8,128)(2,1)S(1)} %slice.58), channel_id=1, source_target_pairs={{0,4},{4,0},{1,5},{5,1},{2,6},{6,2},{3,7},{7,3},{8,12},{12,8},{9,1... | collective-permute-start | bytes 393224 | tf_op jit(solution)/shard_map/ppermute | solution.py:333
  168.0 4.9 %collective-permute-start.22 = (bf16[4,64,256]{2,1,0:T(8,128)(2,1)S(1)}, bf16[4,64,256]{2,1,0:T(8,128)(2,1)S(1)}, u32[]{:S(2)}, u32[]{:S(2)}) collective-permute-start(bf16[4,64,256]{2,1,0:T(8,128)(2,1)S(1)} %fusion.6), channel_id=1, source_target_pairs={{0,4},{4,0},{1,5},{5,1},{2,6},{6,2},{3,7},{7,3},{8,12},{12,8},{9,1... | collective-permute-start | bytes 393224 | tf_op jit(solution)/shard_map/ppermute | solution.py:344
  (7 other events, 119.9 us)
Sparse Core Ops, SparseCore 0:
  47.7 78.4 all-gather.2

commit v7 on v6

--- a/solution.py
+++ b/solution.py
@@ -68,6 +68,26 @@
         base, pattern, *parts,
         pltpu.with_memory_space_constraint(coupled, pltpu.HBM),
     )
+
+
+def unit_kernel(held_ref, own_ref, moved_ref, out_ref):
+    for held, source in ((1, own_ref), (0, moved_ref)):
+        @pl.when(held_ref[0] == held)
+        def _():
+            for z in range(out_ref.shape[0]):
+                out_ref[z] = source[...]
+
+
+def spread_unit(held, own, moved, zs):
+    whole = pl.BlockSpec(memory_space=pltpu.VMEM)
+    return pl.pallas_call(
+        unit_kernel,
+        out_shape=jax.ShapeDtypeStruct((zs,) + own.shape, BF),
+        in_specs=[pl.BlockSpec(memory_space=pltpu.SMEM), whole, whole],
+        out_specs=whole,
+        compiler_params=pltpu.CompilerParams(vmem_limit_bytes=4 << 20),
+        name="spread_unit",
+    )(held.astype(jnp.int32).reshape(1), own, moved)
 
 
 def first_block(a):
@@ -253,12 +273,7 @@
             if r > subs * c + s:
                 pairs.append((i, subs * rows * cols - 1 - i))
         moved = lax.ppermute(block[half:], ("sub", "z", "core", "col"), pairs)
-        eight = (zs,) + moved.shape
-        unit = jnp.where(
-            row > column,
-            jnp.broadcast_to(block[None, :half], eight),
-            jnp.broadcast_to(moved[None], eight),
-        )
+        unit = spread_unit(row > column, block[:half], moved, zs)
         ring = lax.all_to_all(unit, "z", 0, 0, tiled=True)
 
         def units(a, b):
@@ -275,7 +290,6 @@
         shared, ring = lax.optimization_barrier(
             (jnp.stack([leaf_forward, swapped]), ring)
         )
-        ring = pltpu.with_memory_space_constraint(ring, pltpu.HBM)
         factor = lax.all_gather(ring, ("sub", "col", "core"), axis=0, tiled=True)
         chip = lax.axis_index("z")
         turn = 1 - 2 * core
@@ -341,8 +355,9 @@
         ).astype(F32)
         first = core == 0
         rest = jnp.where(first, arrived[1], arrived[0]).astype(BF)
-        rest = lax.ppermute(rest, "core", SWAP).astype(F32)
-        back_sums = near[2][0] + jnp.where(first, arrived[0], arrived[1]) + rest
+        kept = near[2][0] + jnp.where(first, arrived[0], arrived[1])
+        kept, rest = lax.optimization_barrier((kept, rest))
+        back_sums = kept + lax.ppermute(rest, "core", SWAP).astype(F32)
         leaf_residue = (leaf_forward.astype(F32) - back_sums).astype(BF)
         leaf_result = jnp.einsum(
             "inb,ibd->ind", leaf_residue, own_inverse, preferred_element_type=F32

time: 182 us -> 179 us (0.984)
  starting transfers between devices: 56.2 us -> 52.8 us
  waiting for transfers between devices: 56.2 us -> 58.6 us
    ppermute x1, waiting for transfers between devices: 1 us -> 4.63 us  [local(): lax.ppermute(one, ROW, hop(zs, 1)).astype(F32)]
    ppermute x1, starting transfers between devices: 3.91 us -> 0.48 us  [local(): back_sums = kept + lax.ppermute(rest, 'core', SWAP).astype(F32)]
    ppermute x1, starting transfers between devices: 2.33 us -> 0.01 us  [local(): lax.ppermute(one, ROW, hop(zs, 1)).astype(F32)]
    ppermute x1, starting transfers between devices: 1.85 us -> 4.09 us  [local(): lax.ppermute(two, ROW, hop(zs, 2)).astype(F32)]
where the time goes in v7:
time: 179 us
  waiting for transfers between devices  58.6 us (33%)
  starting transfers between devices  52.8 us (29%)
  Pallas kernels  28.8 us (16%)
  blocking collectives  18.1 us (10%)
  between operations  14.5 us (8%)
  local copies, waits for them, and re-layouts  2.94 us (2%)
  matrix products  2.21 us (1%)
    all_gather x1, blocking collectives, local(): updates = lax.all_gather(update, ROW, axis=0)  18.1 us
    pallas_call x1, Pallas kernels, top_solve(): pl.pallas_call(lambda *refs: top_kernel(units, *refs), out_shape=(jax.Sha...  15.9 us
    all_to_all x1, waiting for transfers between devices, local(): ring = lax.all_to_all(unit, 'z', 0, 0, tiled=True)  14.6 us
    ppermute x1, starting transfers between devices, local(): moved = lax.ppermute(block[half:], ('sub', 'z', 'core', 'col'), pairs)  13.5 us
    ppermute x4, starting transfers between devices, local(): lax.ppermute(part, 'core', SWAP)  12.3 us
    ppermute x6, starting transfers between devices, sum_over(): lax.ppermute(value, axis, [(i, (i + k) % size) for i in range(size)])  11.2 us
    pallas_call x2, Pallas kernels, update_products(): pl.pallas_call(update_kernel, out_shape=jax.ShapeDtypeStruct((nrhs, size)...  7.95 us
    ppermute x6, waiting for transfers between devices, sum_over(): lax.ppermute(value, axis, [(i, (i + k) % size) for i in range(size)])  7.91 us
  transfers between devices with their start and end apart: 25, of which 17 were waited for; matrix products, arithmetic and copies ran while one was open for 1% of the time, Pallas kernels for 7%

profile of v7, /device:TPU:1, one launch (start us, length us, event | category | flops | bytes accessed | tf_op | source)
XLA Modules:
  0.0 178.9 jit_solution(5743669689126127701)
XLA Ops:
  8.1 13.5 %collective-permute-start.1 = (bf16[128,256]{1,0:T(8,128)(2,1)S(1)}, bf16[128,256]{1,0:T(8,128)(2,1)S(1)}, u32[]{:S(2)}, u32[]{:S(2)}) collective-permute-start(bf16[128,256]{1,0:T(8,128)(2,1)S(1)} %get-tuple-element.32), channel_id=1, source_target_pairs={{4,251},{8,247},{12,243},{16,239},{20,235},{21,234},{24,231},{25,2... | collective-permute-start | bytes 196616 | tf_op jit(solution)/shard_map/ppermute | solution.py:275
  23.8 4.3 %all-to-all-start = ((bf16[8,128,256]{2,1,0:T(8,128)(2,1)}), bf16[8,128,256]{2,1,0:T(8,128)(2,1)S(1)}, u32[]{:S(2)}, u32[]{:S(2)}) async-start(bf16[8,128,256]{2,1,0:T(8,128)(2,1)} %spread_unit.1), calls=%async_computation | async-start | bytes 1048576 | tf_op jit(solution)/shard_map/all_to_all | solution.py:277
  31.4 14.6 %all-to-all-done = bf16[8,128,256]{2,1,0:T(8,128)(2,1)S(1)} async-done(((bf16[8,128,256]{2,1,0:T(8,128)(2,1)}), bf16[8,128,256]{2,1,0:T(8,128)(2,1)S(1)}, u32[]{:S(2)}, u32[]{:S(2)}) %all-to-all-start) | async-done | bytes 524320 | tf_op jit(solution)/shard_map/all_to_all | solution.py:277
  47.0 6.4 %collective-permute-done.3.refs_2_ = bf16[2,4,64,256]{3,2,1,0:T(8,128)(2,1)S(1)} collective-permute-done((bf16[2,4,64,256]{3,2,1,0:T(8,128)(2,1)S(1)}, bf16[2,4,64,256]{3,2,1,0:T(8,128)(2,1)S(1)}, u32[]{:S(2)}, u32[]{:S(2)}) %collective-permute-start.3) | collective-permute-done | bytes 262176 | tf_op jit(solution)/shard_map/ppermute | solution.py:308
  53.4 1.9 %collective-permute-done.2.refs_1_ = bf16[2,4,64,256]{3,2,1,0:T(8,128)(2,1)S(1)} collective-permute-done((bf16[2,4,64,256]{3,2,1,0:T(8,128)(2,1)S(1)}, bf16[2,4,64,256]{3,2,1,0:T(8,128)(2,1)S(1)}, u32[]{:S(2)}, u32[]{:S(2)}) %collective-permute-start.2) | collective-permute-done | bytes 262176 | tf_op jit(solution)/shard_map/ppermute | solution.py:307
  55.7 5.1 %collective-permute-start.4 = (bf16[2,4,64,256]{3,2,1,0:T(8,128)(2,1)S(1)}, bf16[2,4,64,256]{3,2,1,0:T(8,128)(2,1)S(1)}, u32[]{:S(2)}, u32[]{:S(2)}) collective-permute-start(bf16[2,4,64,256]{3,2,1,0:T(8,128)(2,1)S(1)} %collective-permute-done.2.refs_1_), channel_id=1, source_target_pairs={{0,4},{4,0},{1,5},{5,1},{2,6},{6,2},{3,7},{7,3},{8,12},{12,8},{9,1... | collective-permute-start | bytes 786440 | tf_op jit(solution)/shard_map/ppermute | solution.py:311
  60.9 6.6 %collective-permute-done.6.refs_0_ = bf16[3,4,64,256]{3,2,1,0:T(8,128)(2,1)S(1)} collective-permute-done((bf16[3,4,64,256]{3,2,1,0:T(8,128)(2,1)S(1)}, bf16[3,4,64,256]{3,2,1,0:T(8,128)(2,1)S(1)}, u32[]{:S(2)}, u32[]{:S(2)}) %collective-permute-start.6) | collective-permute-done | bytes 393248 | tf_op jit(solution)/shard_map/ppermute | solution.py:309
  67.5 7.0 %collective-permute-start.7 = (bf16[2,4,64,256]{3,2,1,0:T(8,128)(2,1)S(1)}, bf16[2,4,64,256]{3,2,1,0:T(8,128)(2,1)S(1)}, u32[]{:S(2)}, u32[]{:S(2)}) collective-permute-start(bf16[2,4,64,256]{3,2,1,0:T(8,128)(2,1)S(1)} %slice.71), channel_id=1, source_target_pairs={{0,4},{4,0},{1,5},{5,1},{2,6},{6,2},{3,7},{7,3},{8,12},{12,8},{9,1... | collective-permute-start | bytes 786440 | tf_op jit(solution)/shard_map/ppermute | solution.py:314
  74.9 4.5 %update_products.2 = f32[64,256]{1,0:T(8,128)S(1)} custom-call(s32[10]{0:T(128)S(1)} %stack.147.base_ref, s32[64]{0:T(128)S(1)} %bitcast.66, bf16[2,4,64,256]{3,2,1,0:T(8,128)(2,1)S(1)} %pad_maximum_fusion.1.refs_0_, bf16[2,4,64,256]{3,2,1,0:T(8,128)(2,1)S(1)} %collective-permute-done.2.refs_1_, bf16[2,4,64,256]{3,2,1,0:T(8,128)(2,1)S(1)} %collective-permute-done.3.refs_2_, ...), custom_call_target="tpu_custom_call" | custom-call | flops 335544320 | bytes 6553600 | tf_op jit(solution)/shard_map/update_products/pallas_call | solution.py:49
  79.5 3.4 %update_products.3 = f32[64,256]{1,0:T(8,128)S(1)} custom-call(s32[6]{0:T(128)S(1)} %stack.155.base_ref, s32[64]{0:T(128)S(1)} %bitcast.67, bf16[3,4,64,256]{3,2,1,0:T(8,128)(2,1)S(1)} %collective-permute-done.6.refs_0_, bf16[2,4,64,256]{3,2,1,0:T(8,128)(2,1)S(1)} %collective-permute-done.7.refs_1_, ...), custom_call_target="tpu_custom_call" | custom-call | flops 201326592 | bytes 3932160 | tf_op jit(solution)/shard_map/update_products/pallas_call | solution.py:49
  85.8 1.4 collective-permute-done.10
  87.2 2.0 %collective-permute-done.9 = bf16[64,256]{1,0:T(8,128)(2,1)S(1)} collective-permute-done((bf16[64,256]{1,0:T(8,128)(2,1)S(1)}, bf16[64,256]{1,0:T(8,128)(2,1)S(1)}, u32[]{:S(2)}, u32[]{:S(2)}) %collective-permute-start.9) | collective-permute-done | bytes 32800 | tf_op jit(solution)/shard_map/ppermute | solution.py:244
  89.2 7.8 %collective-permute-start.14 = (bf16[64,256]{1,0:T(8,128)(2,1)S(1)}, bf16[64,256]{1,0:T(8,128)(2,1)S(1)}, u32[]{:S(2)}, u32[]{:S(2)}) collective-permute-start(bf16[64,256]{1,0:T(8,128)(2,1)S(1)} %add_convert_fusion.3), channel_id=1, source_target_pairs={{0,3},{1,0},{2,1},{3,2},{4,7},{5,4},{6,5},{7,6},{8,11},{9,8},{10,9... | collective-permute-start | bytes 98312 | tf_op jit(solution)/shard_map/ppermute | solution.py:244
  98.6 3.8 %collective-permute-done.13 = bf16[64,256]{1,0:T(8,128)(2,1)S(1)} collective-permute-done((bf16[64,256]{1,0:T(8,128)(2,1)S(1)}, bf16[64,256]{1,0:T(8,128)(2,1)S(1)}, u32[]{:S(2)}, u32[]{:S(2)}) %collective-permute-start.13) | collective-permute-done | bytes 32800 | tf_op jit(solution)/shard_map/ppermute | solution.py:244
  102.4 18.1 %all-gather = bf16[1024,256]{1,0:T(8,128)(2,1)S(1)} all-gather(bf16[64,256]{1,0:T(8,128)(2,1)S(1)} %add_convert_fusion.2), channel_id=2, replica_groups=mesh['sub'=4,'z'=8,'core'=2,'col'=4] {'z','core'}, dimensions={0}, use_global_device_ids=true | all-gather | bytes 557056 | tf_op jit(solution)/shard_map/all_gather | solution.py:327
  120.6 4.9 %all-gather.3.cloned.1.call-done.refs_6_ = bf16[256,128,256]{2,1,0:T(8,128)(2,1)} async-done(((bf16[8,128,256]{2,1,0:T(8,128)(2,1)}), bf16[256,128,256]{2,1,0:T(8,128)(2,1)}) %all-gather.3.cloned.1.call-update) | async-done | bytes 16777232 | tf_op jit(solution)/shard_map/all_gather | solution.py:293
  125.4 15.9 %top_solve.1 = (bf16[64,256]{1,0:T(8,128)(2,1)}, bf16[3,4,64,256]{3,2,1,0:T(8,128)(2,1)S(1)}, bf16[3,4,64,256]{3,2,1,0:T(8,128)(2,1)S(1)}) custom-call(s32[2]{0:T(128)S(1)} %pad_add_fusion.refs_0_, s32[6]{0:T(128)S(1)} %stack.138.refs_1_, s32[64]{0:T(128)S(1)} %bitcast.68, bf16[16,64,256]{2,1,0:T(8,128)(2,1)S(1)} %copy-done.1, ...), custom_call_target="tpu_custom_call" | custom-call | tf_op jit(solution)/shard_map/top_solve/pallas_call | solution.py:217
  141.7 1.5 collective-permute-done.15
  143.3 3.9 %collective-permute-start.18 = (bf16[3,4,64,256]{3,2,1,0:T(8,128)(2,1)S(1)}, bf16[3,4,64,256]{3,2,1,0:T(8,128)(2,1)S(1)}, u32[]{:S(2)}, u32[]{:S(2)}) collective-permute-start(bf16[3,4,64,256]{3,2,1,0:T(8,128)(2,1)S(1)} %add_convert_fusion), channel_id=1, source_target_pairs={{0,16},{4,52},{8,24},{12,60},{16,32},{20,4},{24,40},{28,12},{32,48... | collective-permute-start | bytes 1179656 | tf_op jit(solution)/shard_map/ppermute | solution.py:344
  148.0 4.1 %near_products.1 = (bf16[5,4,64,256]{3,2,1,0:T(8,128)(2,1)S(1)}, bf16[5,4,64,256]{3,2,1,0:T(8,128)(2,1)S(1)}) custom-call(s32[10]{0:T(128)S(1)} %stack.128.base_ref, s32[64]{0:T(128)S(1)} %bitcast.69, bf16[64,256]{1,0:T(8,128)(2,1)S(1)} %copy-done.2, bf16[64,256,256]{2,1,0:T(8,128)(2,1)} %bitcast.73), custom_call_target="tpu_custom_call" | custom-call | flops 335544320 | bytes 6553600 | tf_op jit(solution)/shard_map/near_products/pallas_call | solution.py:138
  152.8 3.3 %collective-permute-done.18 = bf16[3,4,64,256]{3,2,1,0:T(8,128)(2,1)S(1)} collective-permute-done((bf16[3,4,64,256]{3,2,1,0:T(8,128)(2,1)S(1)}, bf16[3,4,64,256]{3,2,1,0:T(8,128)(2,1)S(1)}, u32[]{:S(2)}, u32[]{:S(2)}) %collective-permute-start.18) | collective-permute-done | bytes 393248 | tf_op jit(solution)/shard_map/ppermute | solution.py:344
  156.5 4.1 %collective-permute-start.21 = (bf16[2,4,64,256]{3,2,1,0:T(8,128)(2,1)S(1)}, bf16[2,4,64,256]{3,2,1,0:T(8,128)(2,1)S(1)}, u32[]{:S(2)}, u32[]{:S(2)}) collective-permute-start(bf16[2,4,64,256]{3,2,1,0:T(8,128)(2,1)S(1)} %get-tuple-element.29), channel_id=1, source_target_pairs={{0,16},{4,52},{8,24},{12,60},{16,32},{20,4},{24,40},{28,12},{32,48... | collective-permute-start | bytes 786440 | tf_op jit(solution)/shard_map/ppermute | solution.py:353
  161.2 3.7 %collective-permute-done.21 = bf16[2,4,64,256]{3,2,1,0:T(8,128)(2,1)S(1)} collective-permute-done((bf16[2,4,64,256]{3,2,1,0:T(8,128)(2,1)S(1)}, bf16[2,4,64,256]{3,2,1,0:T(8,128)(2,1)S(1)}, u32[]{:S(2)}, u32[]{:S(2)}) %collective-permute-start.21) | collective-permute-done | bytes 262176 | tf_op jit(solution)/shard_map/ppermute | solution.py:353
  164.9 4.6 %collective-permute-done.19 = bf16[2,4,64,256]{3,2,1,0:T(8,128)(2,1)S(1)} collective-permute-done((bf16[2,4,64,256]{3,2,1,0:T(8,128)(2,1)S(1)}, bf16[2,4,64,256]{3,2,1,0:T(8,128)(2,1)S(1)}, u32[]{:S(2)}, u32[]{:S(2)}) %collective-permute-start.19) | collective-permute-done | bytes 262176 | tf_op jit(solution)/shard_map/ppermute | solution.py:353
  (75 shorter events, 17.9 us)
Async XLA Ops:
  8.1 14.8 %collective-permute-start.1 = (bf16[128,256]{1,0:T(8,128)(2,1)S(1)}, bf16[128,256]{1,0:T(8,128)(2,1)S(1)}, u32[]{:S(2)}, u32[]{:S(2)}) collective-permute-start(bf16[128,256]{1,0:T(8,128)(2,1)S(1)} %get-tuple-element.32), channel_id=1, source_target_pairs={{4,251},{8,247},{12,243},{16,239},{20,235},{21,234},{24,231},{25,2... | collective-permute-start | bytes 196616 | tf_op jit(solution)/shard_map/ppermute | solution.py:275
  23.8 22.2 %all-to-all-start = ((bf16[8,128,256]{2,1,0:T(8,128)(2,1)}), bf16[8,128,256]{2,1,0:T(8,128)(2,1)S(1)}, u32[]{:S(2)}, u32[]{:S(2)}) async-start(bf16[8,128,256]{2,1,0:T(8,128)(2,1)} %spread_unit.1), calls=%async_computation | async-start | bytes 1048576 | tf_op jit(solution)/shard_map/all_to_all | solution.py:277
  28.0 97.4 %all-gather.3.cloned.1.call-start = ((), (), s32[]{:S(2)}) async-start(), calls=%async_computation.1 | async-start | bytes 17301504 | tf_op jit(solution)/shard_map/all_gather | solution.py:293
  29.5 1.9 %collective-permute-start = (bf16[4,64,256]{2,1,0:T(8,128)(2,1)S(1)}, bf16[4,64,256]{2,1,0:T(8,128)(2,1)S(1)}, u32[]{:S(2)}, u32[]{:S(2)}) collective-permute-start(bf16[4,64,256]{2,1,0:T(8,128)(2,1)S(1)} %bitcast.74), channel_id=1, source_target_pairs={{0,4},{4,0},{1,5},{5,1},{2,6},{6,2},{3,7},{7,3},{8,12},{12,8},{9,1... | collective-permute-start | bytes 393224 | tf_op jit(solution)/shard_map/ppermute | solution.py:289
  46.8 6.5 %collective-permute-start.3 = (bf16[2,4,64,256]{3,2,1,0:T(8,128)(2,1)S(1)}, bf16[2,4,64,256]{3,2,1,0:T(8,128)(2,1)S(1)}, u32[]{:S(2)}, u32[]{:S(2)}) collective-permute-start(bf16[2,4,64,256]{3,2,1,0:T(8,128)(2,1)S(1)} %pad_maximum_fusion.1.refs_0_), channel_id=1, source_target_pairs={{0,16},{4,52},{8,24},{12,60},{16,32},{20,4},{24,40},{28,12},{32,48... | collective-permute-start | bytes 786440 | tf_op jit(solution)/shard_map/ppermute | solution.py:308
  46.9 8.4 %collective-permute-start.2 = (bf16[2,4,64,256]{3,2,1,0:T(8,128)(2,1)S(1)}, bf16[2,4,64,256]{3,2,1,0:T(8,128)(2,1)S(1)}, u32[]{:S(2)}, u32[]{:S(2)}) collective-permute-start(bf16[2,4,64,256]{3,2,1,0:T(8,128)(2,1)S(1)} %pad_maximum_fusion.1.refs_0_), channel_id=1, source_target_pairs={{0,8},{4,60},{8,16},{12,4},{16,24},{20,12},{24,32},{28,20},{32,40}... | collective-permute-start | bytes 786440 | tf_op jit(solution)/shard_map/ppermute | solution.py:307
  55.3 12.1 %collective-permute-start.6 = (bf16[3,4,64,256]{3,2,1,0:T(8,128)(2,1)S(1)}, bf16[3,4,64,256]{3,2,1,0:T(8,128)(2,1)S(1)}, u32[]{:S(2)}, u32[]{:S(2)}) collective-permute-start(bf16[3,4,64,256]{3,2,1,0:T(8,128)(2,1)S(1)} %pad_maximum_fusion), channel_id=1, source_target_pairs={{0,16},{4,52},{8,24},{12,60},{16,32},{20,4},{24,40},{28,12},{32,48... | collective-permute-start | bytes 1179656 | tf_op jit(solution)/shard_map/ppermute | solution.py:309
  55.7 19.2 %collective-permute-start.4 = (bf16[2,4,64,256]{3,2,1,0:T(8,128)(2,1)S(1)}, bf16[2,4,64,256]{3,2,1,0:T(8,128)(2,1)S(1)}, u32[]{:S(2)}, u32[]{:S(2)}) collective-permute-start(bf16[2,4,64,256]{3,2,1,0:T(8,128)(2,1)S(1)} %collective-permute-done.2.refs_1_), channel_id=1, source_target_pairs={{0,4},{4,0},{1,5},{5,1},{2,6},{6,2},{3,7},{7,3},{8,12},{12,8},{9,1... | collective-permute-start | bytes 786440 | tf_op jit(solution)/shard_map/ppermute | solution.py:311
  60.8 14.1 %collective-permute-start.5 = (bf16[2,4,64,256]{3,2,1,0:T(8,128)(2,1)S(1)}, bf16[2,4,64,256]{3,2,1,0:T(8,128)(2,1)S(1)}, u32[]{:S(2)}, u32[]{:S(2)}) collective-permute-start(bf16[2,4,64,256]{3,2,1,0:T(8,128)(2,1)S(1)} %collective-permute-done.3.refs_2_), channel_id=1, source_target_pairs={{0,4},{4,0},{1,5},{5,1},{2,6},{6,2},{3,7},{7,3},{8,12},{12,8},{9,1... | collective-permute-start | bytes 786440 | tf_op jit(solution)/shard_map/ppermute | solution.py:311
  67.5 12.0 %collective-permute-start.7 = (bf16[2,4,64,256]{3,2,1,0:T(8,128)(2,1)S(1)}, bf16[2,4,64,256]{3,2,1,0:T(8,128)(2,1)S(1)}, u32[]{:S(2)}, u32[]{:S(2)}) collective-permute-start(bf16[2,4,64,256]{3,2,1,0:T(8,128)(2,1)S(1)} %slice.71), channel_id=1, source_target_pairs={{0,4},{4,0},{1,5},{5,1},{2,6},{6,2},{3,7},{7,3},{8,12},{12,8},{9,1... | collective-permute-start | bytes 786440 | tf_op jit(solution)/shard_map/ppermute | solution.py:314
  74.5 5.0 %collective-permute-start.8 = (bf16[1,4,64,256]{3,2,1,0:T(8,128)(2,1)S(1)}, bf16[1,4,64,256]{3,2,1,0:T(8,128)(2,1)S(1)}, u32[]{:S(2)}, u32[]{:S(2)}) collective-permute-start(bf16[1,4,64,256]{3,2,1,0:T(8,128)(2,1)S(1)} %slice.72), channel_id=1, source_target_pairs={{0,4},{4,0},{1,5},{5,1},{2,6},{6,2},{3,7},{7,3},{8,12},{12,8},{9,1... | collective-permute-start | bytes 393224 | tf_op jit(solution)/shard_map/ppermute | solution.py:314
  82.9 2.8 %collective-permute-start.11 = (bf16[64,256]{1,0:T(8,128)(2,1)S(1)}, bf16[64,256]{1,0:T(8,128)(2,1)S(1)}, u32[]{:S(2)}, u32[]{:S(2)}) collective-permute-start(bf16[64,256]{1,0:T(8,128)(2,1)S(1)} %add_convert_fusion.4), channel_id=1, source_target_pairs={{0,192},{64,0},{128,64},{192,128},{1,193},{65,1},{129,65},{193,129... | collective-permute-start | bytes 98312 | tf_op jit(solution)/shard_map/ppermute | solution.py:244
  83.2 4.0 %collective-permute-start.10 = (bf16[64,256]{1,0:T(8,128)(2,1)S(1)}, bf16[64,256]{1,0:T(8,128)(2,1)S(1)}, u32[]{:S(2)}, u32[]{:S(2)}) collective-permute-start(bf16[64,256]{1,0:T(8,128)(2,1)S(1)} %add_convert_fusion.4), channel_id=1, source_target_pairs={{0,64},{64,128},{128,192},{192,0},{1,65},{65,129},{129,193},{193,1... | collective-permute-start | bytes 98312 | tf_op jit(solution)/shard_map/ppermute | solution.py:244
  84.5 4.7 %collective-permute-start.9 = (bf16[64,256]{1,0:T(8,128)(2,1)S(1)}, bf16[64,256]{1,0:T(8,128)(2,1)S(1)}, u32[]{:S(2)}, u32[]{:S(2)}) collective-permute-start(bf16[64,256]{1,0:T(8,128)(2,1)S(1)} %add_convert_fusion.4), channel_id=1, source_target_pairs={{0,128},{64,192},{128,0},{192,64},{1,129},{65,193},{129,1},{193,65... | collective-permute-start | bytes 98312 | tf_op jit(solution)/shard_map/ppermute | solution.py:244
  89.2 9.4 %collective-permute-start.14 = (bf16[64,256]{1,0:T(8,128)(2,1)S(1)}, bf16[64,256]{1,0:T(8,128)(2,1)S(1)}, u32[]{:S(2)}, u32[]{:S(2)}) collective-permute-start(bf16[64,256]{1,0:T(8,128)(2,1)S(1)} %add_convert_fusion.3), channel_id=1, source_target_pairs={{0,3},{1,0},{2,1},{3,2},{4,7},{5,4},{6,5},{7,6},{8,11},{9,8},{10,9... | collective-permute-start | bytes 98312 | tf_op jit(solution)/shard_map/ppermute | solution.py:244
  97.1 5.3 %collective-permute-start.13 = (bf16[64,256]{1,0:T(8,128)(2,1)S(1)}, bf16[64,256]{1,0:T(8,128)(2,1)S(1)}, u32[]{:S(2)}, u32[]{:S(2)}) collective-permute-start(bf16[64,256]{1,0:T(8,128)(2,1)S(1)} %add_convert_fusion.3), channel_id=1, source_target_pairs={{0,1},{1,2},{2,3},{3,0},{4,5},{5,6},{6,7},{7,4},{8,9},{9,10},{10,1... | collective-permute-start | bytes 98312 | tf_op jit(solution)/shard_map/ppermute | solution.py:244
  97.1 5.3 %collective-permute-start.12 = (bf16[64,256]{1,0:T(8,128)(2,1)S(1)}, bf16[64,256]{1,0:T(8,128)(2,1)S(1)}, u32[]{:S(2)}, u32[]{:S(2)}) collective-permute-start(bf16[64,256]{1,0:T(8,128)(2,1)S(1)} %add_convert_fusion.3), channel_id=1, source_target_pairs={{0,2},{1,3},{2,0},{3,1},{4,6},{5,7},{6,4},{7,5},{8,10},{9,11},{10,... | collective-permute-start | bytes 98312 | tf_op jit(solution)/shard_map/ppermute | solution.py:244
  141.3 1.8 %collective-permute-start.15 = (bf16[3,4,64,256]{3,2,1,0:T(8,128)(2,1)S(1)}, bf16[3,4,64,256]{3,2,1,0:T(8,128)(2,1)S(1)}, u32[]{:S(2)}, u32[]{:S(2)}) collective-permute-start(bf16[3,4,64,256]{3,2,1,0:T(8,128)(2,1)S(1)} %get-tuple-element.17), channel_id=1, source_target_pairs={{0,4},{4,0},{1,5},{5,1},{2,6},{6,2},{3,7},{7,3},{8,12},{12,8},{9,1... | collective-permute-start | bytes 1179656 | tf_op jit(solution)/shard_map/ppermute | solution.py:341
  143.3 12.9 %collective-permute-start.18 = (bf16[3,4,64,256]{3,2,1,0:T(8,128)(2,1)S(1)}, bf16[3,4,64,256]{3,2,1,0:T(8,128)(2,1)S(1)}, u32[]{:S(2)}, u32[]{:S(2)}) collective-permute-start(bf16[3,4,64,256]{3,2,1,0:T(8,128)(2,1)S(1)} %add_convert_fusion), channel_id=1, source_target_pairs={{0,16},{4,52},{8,24},{12,60},{16,32},{20,4},{24,40},{28,12},{32,48... | collective-permute-start | bytes 1179656 | tf_op jit(solution)/shard_map/ppermute | solution.py:344
  152.2 4.0 %collective-permute-start.17 = (bf16[2,4,64,256]{3,2,1,0:T(8,128)(2,1)S(1)}, bf16[2,4,64,256]{3,2,1,0:T(8,128)(2,1)S(1)}, u32[]{:S(2)}, u32[]{:S(2)}) collective-permute-start(bf16[2,4,64,256]{3,2,1,0:T(8,128)(2,1)S(1)} %get-tuple-element.30), channel_id=1, source_target_pairs={{0,4},{4,0},{1,5},{5,1},{2,6},{6,2},{3,7},{7,3},{8,12},{12,8},{9,1... | collective-permute-start | bytes 786440 | tf_op jit(solution)/shard_map/ppermute | solution.py:347
  152.3 3.9 %collective-permute-start.20 = (bf16[2,4,64,256]{3,2,1,0:T(8,128)(2,1)S(1)}, bf16[2,4,64,256]{3,2,1,0:T(8,128)(2,1)S(1)}, u32[]{:S(2)}, u32[]{:S(2)}) collective-permute-start(bf16[2,4,64,256]{3,2,1,0:T(8,128)(2,1)S(1)} %get-tuple-element.31), channel_id=1, source_target_pairs={{0,4},{4,0},{1,5},{5,1},{2,6},{6,2},{3,7},{7,3},{8,12},{12,8},{9,1... | collective-permute-start | bytes 786440 | tf_op jit(solution)/shard_map/ppermute | solution.py:347
  156.5 8.4 %collective-permute-start.21 = (bf16[2,4,64,256]{3,2,1,0:T(8,128)(2,1)S(1)}, bf16[2,4,64,256]{3,2,1,0:T(8,128)(2,1)S(1)}, u32[]{:S(2)}, u32[]{:S(2)}) collective-permute-start(bf16[2,4,64,256]{3,2,1,0:T(8,128)(2,1)S(1)} %get-tuple-element.29), channel_id=1, source_target_pairs={{0,16},{4,52},{8,24},{12,60},{16,32},{20,4},{24,40},{28,12},{32,48... | collective-permute-start | bytes 786440 | tf_op jit(solution)/shard_map/ppermute | solution.py:353
  160.6 8.9 %collective-permute-start.19 = (bf16[2,4,64,256]{3,2,1,0:T(8,128)(2,1)S(1)}, bf16[2,4,64,256]{3,2,1,0:T(8,128)(2,1)S(1)}, u32[]{:S(2)}, u32[]{:S(2)}) collective-permute-start(bf16[2,4,64,256]{3,2,1,0:T(8,128)(2,1)S(1)} %get-tuple-element.28), channel_id=1, source_target_pairs={{0,8},{4,60},{8,16},{12,4},{16,24},{20,12},{24,32},{28,20},{32,40}... | collective-permute-start | bytes 786440 | tf_op jit(solution)/shard_map/ppermute | solution.py:353
  160.6 9.0 %collective-permute-start.16 = (bf16[1,4,64,256]{3,2,1,0:T(8,128)(2,1)S(1)}, bf16[1,4,64,256]{3,2,1,0:T(8,128)(2,1)S(1)}, u32[]{:S(2)}, u32[]{:S(2)}) collective-permute-start(bf16[1,4,64,256]{3,2,1,0:T(8,128)(2,1)S(1)} %slice.61), channel_id=1, source_target_pairs={{0,4},{4,0},{1,5},{5,1},{2,6},{6,2},{3,7},{7,3},{8,12},{12,8},{9,1... | collective-permute-start | bytes 393224 | tf_op jit(solution)/shard_map/ppermute | solution.py:347
  (8 other events, 133.7 us)
Sparse Core Ops, SparseCore 0:
  46.9 78.4 all-gather.2
